TPU v7x, 32 devices: a whole 2x2x4 slice. The times are simulated.
32 devices in a mesh: fsdp: 4 (over y, x), ctx: 2 (over core), tp: 4 (over z).
Axes of the slice: x: 2, y: 2, z: 4, core: 2. Of those that a mesh axis runs over, the one named last changes fastest.
Arguments:
- residual: bfloat16 [8192, 2048], P(('fsdp', 'ctx'), 'tp'), may hold values from -6 to 6
- out_grad: bfloat16 [8192, 2048], P(('fsdp', 'ctx'), 'tp'), may hold values from -6 to 6
- path_depth: int32 [8192], P(('fsdp', 'ctx')), may hold values from 0 to 895, as said below
- seg_lengths: int32 [4, 13], P('fsdp'), may hold values from 64 to 512, as said below
- parents: int32 [4, 13], P('fsdp'), may hold values from 0 to 4, as said below
- attn_norm_gain: bfloat16 [2048], P('tp'), may hold values from 0.099609375 to 1.8984375
- attn_norm_bias: bfloat16 [2048], P('tp'), may hold values from -1.5 to 1.5
- ffn_norm_gain: bfloat16 [2048], P('tp'), may hold values from 0.099609375 to 1.8984375
- ffn_norm_bias: bfloat16 [2048], P('tp'), may hold values from -1.5 to 1.5
- qkv_weight: bfloat16 [2048, 6144], P(('fsdp', 'ctx'), 'tp'), may hold values from -0.125 to 0.125
- qkv_bias: bfloat16 [6144], P('tp'), may hold values from -2.5 to 2.5
- dense_weight: bfloat16 [2048, 2048], P('tp', ('fsdp', 'ctx')), may hold values from -2 to 2
- dense_bias: bfloat16 [2048], P('tp'), may hold values from -2.5 to 2.5
- up_weight: bfloat16 [2048, 8192], P(('fsdp', 'ctx'), 'tp'), may hold values from -0.125 to 0.125
- up_bias: bfloat16 [8192], P('tp'), may hold values from -2.5 to 2.5
- down_weight: bfloat16 [8192, 2048], P('tp', ('fsdp', 'ctx')), may hold values from -0.0625 to 0.0625
- down_bias: bfloat16 [2048], P('tp'), may hold values from -2.5 to 2.5
Outputs:
- output: bfloat16 [8192, 2048], P(('fsdp', 'ctx'), 'tp')
- input_grad: bfloat16 [8192, 2048], P(('fsdp', 'ctx'), 'tp')
- grad_attn_norm_gain: float32 [2048], P('tp')
- grad_attn_norm_bias: float32 [2048], P('tp')
- grad_ffn_norm_gain: float32 [2048], P('tp')
- grad_ffn_norm_bias: float32 [2048], P('tp')
- grad_qkv_weight: float32 [2048, 6144], P(('fsdp', 'ctx'), 'tp')
- grad_qkv_bias: float32 [6144], P('tp')
- grad_dense_weight: float32 [2048, 2048], P('tp', ('fsdp', 'ctx'))
- grad_dense_bias: float32 [2048], P('tp')
- grad_up_weight: float32 [2048, 8192], P(('fsdp', 'ctx'), 'tp')
- grad_up_bias: float32 [8192], P('tp')
- grad_down_weight: float32 [8192, 2048], P('tp', ('fsdp', 'ctx'))
- grad_down_bias: float32 [2048], P('tp')
Inputs may be any that keep to these rules, and one draw needn't show every extreme that they name: `seg_lengths`: row t lists tree t's segments in order: the trunk of 512 tokens, 4 branches, then 8 leaves; each row sums to 2048. `parents`: entry s of row t is the segment that segment s hangs from: 0 for the trunk itself and for each branch, a branch for each leaf; each branch holds exactly two leaves. `path_depth`: A token's place within its segment plus the lengths of the segment's proper ancestors in its tree.
All inputs are finite; a program needn't handle non-finite values.
Results may differ from a plain program's by a relative error of at most 0.012.
Values may be sent and summed in bfloat16 or wider, within the bound.
No kernel may reach another device: no remote copies, remote signals or barrier semaphores. Data moves between devices by JAX's collectives and lax.ppermute only.
A program may use at most 256 MiB of HBM per device.

v0:
```python
from functools import partial
import math

import jax
import jax.numpy as jnp
from jax import lax
from jax.sharding import PartitionSpec as P

HEAD_DIM = 256
ROTARY = 64
SEGS = 13


norm_epsilon = 1e-05
masked_score = -1e30
block_limit = 512


def from_behind(x, axis, by):
    peers = lax.axis_size(axis)
    pairs = [(i, i + by) for i in range(peers) if 0 <= i + by < peers]
    return lax.ppermute(x, axis, pairs)


def rotary(vectors, places):
    half_rot = ROTARY // 2
    frequency = jnp.power(10000.0, -2.0 * jnp.arange(half_rot).astype(jnp.float32) / ROTARY)
    angles = places.astype(jnp.float32)[:, None] * frequency[None, :]
    cosine = jnp.cos(angles)[:, None, :]
    sine_part = jnp.sin(angles)[:, None, :]
    first_half = vectors[..., :half_rot]
    second_half = vectors[..., half_rot:ROTARY]
    return jnp.concatenate(
        [
            first_half * cosine - second_half * sine_part,
            second_half * cosine + first_half * sine_part,
            vectors[..., ROTARY:],
        ],
        axis=-1,
    )


def tree_tables(lengths, parent):
    starts = jnp.cumsum(lengths) - lengths
    labels = jnp.arange(SEGS)
    grand_parent = jnp.sum(
        jnp.where(parent[:, None] == labels[None, :], parent[None, :], 0), axis=1
    )
    ancestor = (
        (labels[None, :] == labels[:, None])
        | (labels[None, :] == parent[:, None])
        | (labels[None, :] == grand_parent[:, None])
    )
    return (starts, ancestor.astype(jnp.float32))


def segment_onehot(places, starts):
    membership = jnp.sum((places[:, None] >= starts[None, :]).astype(jnp.int32), axis=1) - 1
    return (membership[:, None] == jnp.arange(SEGS)[None, :]).astype(jnp.float32)


def visible(hot_query, place_query, hot_key, place_key, ancestor):
    reachable = jnp.dot(jnp.dot(hot_query, ancestor), hot_key.T)
    return (reachable > 0.5) & (place_key[None, :] <= place_query[:, None])


def on_device(
    residual,
    out_grad,
    path_depth,
    seg_lengths,
    parents,
    attn_norm_gain,
    attn_norm_bias,
    ffn_norm_gain,
    ffn_norm_bias,
    qkv_weight,
    qkv_bias,
    dense_weight,
    dense_bias,
    up_weight,
    up_bias,
    down_weight,
    down_bias,
):
    row_count = residual.shape[0]
    local_width = residual.shape[1]
    head_count = qkv_weight.shape[1] // (3 * HEAD_DIM)
    score_scale = 1.0 / math.sqrt(HEAD_DIM)
    ctx_index = lax.axis_index("ctx")
    tp_index = lax.axis_index("tp")
    norm_stack = jnp.stack([attn_norm_gain, attn_norm_bias, ffn_norm_gain, ffn_norm_bias])
    full_rows, norm_terms = (
        lax.all_gather(residual, "tp", axis=1, tiled=True),
        lax.all_gather(norm_stack, "tp", axis=1, tiled=True),
    )
    norm_terms = norm_terms.astype(jnp.float32)
    qkv_full, up_full = (
        lax.all_gather(qkv_weight, ("fsdp", "ctx"), axis=0, tiled=True),
        lax.all_gather(up_weight, ("fsdp", "ctx"), axis=0, tiled=True),
    )
    dense_full, down_full = (
        lax.all_gather(dense_weight, ("fsdp", "ctx"), axis=1, tiled=True),
        lax.all_gather(down_weight, ("fsdp", "ctx"), axis=1, tiled=True),
    )
    rows_wide = full_rows.astype(jnp.float32)
    centred = rows_wide - jnp.mean(rows_wide, axis=1, keepdims=True)
    inverse_scale = lax.rsqrt(jnp.mean(centred * centred, axis=1, keepdims=True) + norm_epsilon)
    normed = centred * inverse_scale
    attn_in = (normed * norm_terms[0] + norm_terms[1]).astype(jnp.bfloat16)
    ffn_in = (normed * norm_terms[2] + norm_terms[3]).astype(jnp.bfloat16)
    joined = (
        jnp.dot(attn_in, qkv_full, preferred_element_type=jnp.float32)
        + qkv_bias.astype(jnp.float32)
    ).reshape(row_count, head_count, 3, HEAD_DIM)
    queries_pre = joined[:, :, 0]
    query_rows = rotary(queries_pre, path_depth).astype(jnp.bfloat16)
    key_rows = rotary(joined[:, :, 1], path_depth).astype(jnp.bfloat16)
    value_rows = joined[:, :, 2].astype(jnp.bfloat16)
    far_keys, far_values = from_behind((key_rows, value_rows), "ctx", 1)
    starts, ancestor = tree_tables(seg_lengths[0], parents[0])
    places = ctx_index * row_count + jnp.arange(row_count, dtype=jnp.int32)
    key_places = jnp.concatenate([places - row_count, places])
    hot_query = segment_onehot(places, starts)
    hot_key = segment_onehot(key_places, starts)
    all_keys = jnp.concatenate([far_keys, key_rows], axis=0)
    all_values = jnp.concatenate([far_values, value_rows], axis=0)
    block_starts = list(range(0, row_count, block_limit))

    def block_scores(block_start, block_size, key_set):
        key_span = row_count + block_start + block_size
        query_block = query_rows[block_start : block_start + block_size]
        scores = (
            jnp.einsum(
                "nhe,lhe->hnl", query_block, key_set[:key_span], preferred_element_type=jnp.float32
            )
            * score_scale
        )
        reachable = visible(
            hot_query[block_start : block_start + block_size],
            places[block_start : block_start + block_size],
            hot_key[:key_span],
            key_places[:key_span],
            ancestor,
        )
        return jnp.where(reachable[None], scores, masked_score)

    out_blocks = []
    log_totals = []
    for block_start in block_starts:
        block_size = min(block_limit, row_count - block_start)
        key_span = row_count + block_start + block_size
        scores = block_scores(block_start, block_size, all_keys)
        row_top = jnp.max(scores, axis=-1, keepdims=True)
        exp_scores = jnp.exp(scores - row_top)
        exp_total = jnp.sum(exp_scores, axis=-1, keepdims=True)
        attn_probs = exp_scores / exp_total
        out_blocks.append(
            jnp.einsum(
                "hnl,lhe->nhe",
                attn_probs.astype(jnp.bfloat16),
                all_values[:key_span],
                preferred_element_type=jnp.float32,
            )
        )
        log_totals.append(row_top + jnp.log(exp_total))
    attended = (
        jnp.concatenate(out_blocks, axis=0)
        .reshape(row_count, head_count * HEAD_DIM)
        .astype(jnp.bfloat16)
    )
    hidden_pre = jnp.dot(ffn_in, up_full, preferred_element_type=jnp.float32) + up_bias.astype(
        jnp.float32
    )
    hidden_wide, gelu_back = jax.vjp(partial(jax.nn.gelu, approximate=False), hidden_pre)
    hidden = hidden_wide.astype(jnp.bfloat16)
    partial_out = jnp.dot(attended, dense_full, preferred_element_type=jnp.float32) + jnp.dot(
        hidden, down_full, preferred_element_type=jnp.float32
    )
    shared_out = lax.psum_scatter(partial_out, "tp", scatter_dimension=1, tiled=True)
    output = (
        residual.astype(jnp.float32)
        + shared_out
        + dense_bias.astype(jnp.float32)
        + down_bias.astype(jnp.float32)
    ).astype(jnp.bfloat16)
    cotangent = lax.all_gather(out_grad, "tp", axis=1, tiled=True)
    grad_out_bias = jnp.sum(out_grad.astype(jnp.float32), axis=0)
    grad_dense_w = jnp.einsum("rf,rd->fd", attended, cotangent, preferred_element_type=jnp.float32)
    grad_down_w = jnp.einsum("rf,rd->fd", hidden, cotangent, preferred_element_type=jnp.float32)
    grad_attended = jnp.einsum(
        "rd,fd->rf", cotangent, dense_full, preferred_element_type=jnp.float32
    ).astype(jnp.bfloat16)
    grad_hidden = jnp.einsum("rd,fd->rf", cotangent, down_full, preferred_element_type=jnp.float32)
    grad_pre = gelu_back(grad_hidden)[0].astype(jnp.bfloat16)
    grad_up_w = jnp.einsum("rd,rf->df", ffn_in, grad_pre, preferred_element_type=jnp.float32)
    grad_up_b = jnp.sum(grad_pre.astype(jnp.float32), axis=0)
    grad_ffn_in = jnp.einsum("rf,df->rd", grad_pre, up_full, preferred_element_type=jnp.float32)
    key_set = all_keys
    grad_att_heads = grad_attended.reshape(row_count, head_count, HEAD_DIM)
    grad_query_parts = []
    grad_key_all = jnp.zeros((2 * row_count, head_count, HEAD_DIM), jnp.float32)
    grad_value_all = jnp.zeros((2 * row_count, head_count, HEAD_DIM), jnp.float32)
    for block_number, block_start in enumerate(block_starts):
        block_size = min(block_limit, row_count - block_start)
        key_span = row_count + block_start + block_size
        scores = block_scores(block_start, block_size, key_set)
        attn_probs = jnp.exp(scores - log_totals[block_number])
        grad_block = grad_att_heads[block_start : block_start + block_size]
        grad_value_all = grad_value_all.at[:key_span].add(
            jnp.einsum(
                "hnl,nhe->lhe",
                attn_probs.astype(jnp.bfloat16),
                grad_block,
                preferred_element_type=jnp.float32,
            )
        )
        grad_dots = jnp.einsum(
            "nhe,lhe->hnl", grad_block, all_values[:key_span], preferred_element_type=jnp.float32
        )
        row_delta = jnp.sum(attn_probs * grad_dots, axis=-1, keepdims=True)
        grad_scores = (attn_probs * (grad_dots - row_delta)).astype(jnp.bfloat16)
        grad_query_parts.append(
            jnp.einsum(
                "hnl,lhe->nhe", grad_scores, key_set[:key_span], preferred_element_type=jnp.float32
            )
            * score_scale
        )
        grad_key_all = grad_key_all.at[:key_span].add(
            jnp.einsum(
                "hnl,nhe->lhe",
                grad_scores,
                query_rows[block_start : block_start + block_size],
                preferred_element_type=jnp.float32,
            )
            * score_scale
        )
    arriving_keys, arriving_values = from_behind(
        (grad_key_all[:row_count], grad_value_all[:row_count]), "ctx", -1
    )
    grad_keys = grad_key_all[row_count:] + arriving_keys
    grad_values = grad_value_all[row_count:] + arriving_values
    grad_queries = jnp.concatenate(grad_query_parts, axis=0)
    rotated_unused, rotary_back = jax.vjp(lambda vectors: rotary(vectors, path_depth), queries_pre)
    grad_joined = (
        jnp.stack([rotary_back(grad_queries)[0], rotary_back(grad_keys)[0], grad_values], axis=2)
        .astype(jnp.bfloat16)
        .reshape(row_count, head_count * 3 * HEAD_DIM)
    )
    grad_qkv_w = jnp.einsum("rd,rf->df", attn_in, grad_joined, preferred_element_type=jnp.float32)
    grad_qkv_b = jnp.sum(grad_joined.astype(jnp.float32), axis=0)
    grad_attn_in = jnp.einsum(
        "rf,df->rd", grad_joined, qkv_full, preferred_element_type=jnp.float32
    )
    total_attn, total_ffn = lax.psum((grad_attn_in, grad_ffn_in), "tp")

    def norm_back(total_grad, gain_row):
        scaled = total_grad * gain_row
        mean_plain = jnp.mean(scaled, axis=1, keepdims=True)
        mean_normed = jnp.mean(scaled * normed, axis=1, keepdims=True)
        back_rows = inverse_scale * (scaled - mean_plain - normed * mean_normed)
        gain_grad = jnp.sum(total_grad * normed, axis=0)
        shift_grad = jnp.sum(total_grad, axis=0)
        return (
            lax.dynamic_slice_in_dim(back_rows, tp_index * local_width, local_width, 1),
            lax.dynamic_slice_in_dim(gain_grad, tp_index * local_width, local_width, 0),
            lax.dynamic_slice_in_dim(shift_grad, tp_index * local_width, local_width, 0),
        )

    back_attn, attn_gain_grad, attn_shift_grad = norm_back(total_attn, norm_terms[0])
    back_ffn, ffn_gain_grad, ffn_shift_grad = norm_back(total_ffn, norm_terms[2])
    norm_grads = jnp.stack([attn_gain_grad, attn_shift_grad, ffn_gain_grad, ffn_shift_grad])
    back_total = back_attn + back_ffn
    input_grad = (out_grad.astype(jnp.float32) + back_total).astype(jnp.bfloat16)
    qkv_bias_grad, up_bias_grad, out_bias_grad, norm_totals = lax.psum(
        (grad_qkv_b, grad_up_b, grad_out_bias, norm_grads), ("fsdp", "ctx")
    )
    qkv_weight_grad, up_weight_grad = (
        lax.psum_scatter(
            grad_qkv_w.astype(jnp.bfloat16), ("fsdp", "ctx"), scatter_dimension=0, tiled=True
        ).astype(jnp.float32),
        lax.psum_scatter(
            grad_up_w.astype(jnp.bfloat16), ("fsdp", "ctx"), scatter_dimension=0, tiled=True
        ).astype(jnp.float32),
    )
    dense_weight_grad, down_weight_grad = (
        lax.psum_scatter(
            grad_dense_w.astype(jnp.bfloat16), ("fsdp", "ctx"), scatter_dimension=1, tiled=True
        ).astype(jnp.float32),
        lax.psum_scatter(
            grad_down_w.astype(jnp.bfloat16), ("fsdp", "ctx"), scatter_dimension=1, tiled=True
        ).astype(jnp.float32),
    )
    return (
        output,
        input_grad,
        norm_totals[0],
        norm_totals[1],
        norm_totals[2],
        norm_totals[3],
        qkv_weight_grad,
        qkv_bias_grad,
        dense_weight_grad,
        out_bias_grad,
        up_weight_grad,
        up_bias_grad,
        down_weight_grad,
        out_bias_grad,
    )


def solution(mesh):
    placed = (
        P(("fsdp", "ctx"), "tp"),
        P(("fsdp", "ctx"), "tp"),
        P(("fsdp", "ctx")),
        P("fsdp", None),
        P("fsdp", None),
        P("tp"),
        P("tp"),
        P("tp"),
        P("tp"),
        P(("fsdp", "ctx"), "tp"),
        P("tp"),
        P("tp", ("fsdp", "ctx")),
        P("tp"),
        P(("fsdp", "ctx"), "tp"),
        P("tp"),
        P("tp", ("fsdp", "ctx")),
        P("tp"),
    )
    return jax.shard_map(
        on_device,
        mesh=mesh,
        in_specs=placed,
        out_specs=(
            P(("fsdp", "ctx"), "tp"),
            P(("fsdp", "ctx"), "tp"),
            P("tp"),
            P("tp"),
            P("tp"),
            P("tp"),
            P(("fsdp", "ctx"), "tp"),
            P("tp"),
            P("tp", ("fsdp", "ctx")),
            P("tp"),
            P(("fsdp", "ctx"), "tp"),
            P("tp"),
            P("tp", ("fsdp", "ctx")),
            P("tp"),
        ),
        check_vma=False,
    )
```

profile of v0, /device:TPU:0, one launch (start us, length us, event | category | flops | bytes accessed | tf_op | source)
XLA Modules:
  0.0 1347.8 jit_solution(2497140615921052916)
XLA Ops:
  19.3 15.1 %all_gather.22 = bf16[4,2048]{1,0:T(4,128)(2,1)S(1)} all-gather(bf16[4,512]{1,0:T(4,128)(2,1)S(1)} %pad_maximum_fusion.16), channel_id=1, replica_groups=mesh['fsdp'=4,'ctx'=2,'tp'=4] {'tp'}, dimensions={1}, use_global_device_ids=true | all-gather | bytes 20480 | tf_op jit(solution)/shard_map/all_gather | solution.py:95
  42.4 50.9 %all-gather.7.cloned.1.call-done = bf16[1024,2048]{1,0:T(8,128)(2,1)} async-done(((bf16[1024,512]{1,0:T(8,128)(2,1)}), bf16[1024,2048]{1,0:T(8,128)(2,1)}) %all-gather.7.cloned.1.call-update) | async-done | bytes 4194320 | tf_op jit(solution)/shard_map/all_gather | solution.py:94
  98.0 41.3 %all-gather.9.cloned.1.call-done = bf16[2048,1536]{1,0:T(8,128)(2,1)} async-done(((bf16[256,1536]{1,0:T(8,128)(2,1)}), bf16[2048,1536]{1,0:T(8,128)(2,1)}) %all-gather.9.cloned.1.call-update) | async-done | bytes 6291472 | tf_op jit(solution)/shard_map/all_gather | solution.py:99
  139.3 12.8 convolution_add_fusion
  152.1 6.6 copy.87
  177.9 73.7 %all-gather.17.cloned.1.call-done = bf16[1024,2048]{1,0:T(8,128)(2,1)} async-done(((bf16[1024,512]{1,0:T(8,128)(2,1)}), bf16[1024,2048]{1,0:T(8,128)(2,1)}) %all-gather.17.cloned.1.call-update) | async-done | bytes 4194320 | tf_op jit(solution)/shard_map/all_gather | solution.py:187
  251.6 5.2 convolution_convert_fusion.4
  292.7 5.3 bitcast_add_fusion.1
  331.8 13.6 %convolution_convert_fusion.2 = bf16[2048,1536]{1,0:T(8,128)(2,1)} fusion(bf16[1024,1536]{0,1:T(8,128)(2,1)} %bitcast.86, bf16[1024,2048]{1,0:T(8,128)(2,1)} %all-gather.7.cloned.1.call-done, f32[2048]{0:T(1024)S(1)} %bitcast.101, f32[2048]{0:T(1024)S(1)} %bitcast.89, f32[1024]{0:T(1024)S(1)} %add_rsqrt_fusion, f32[1024]{0:T(1024)S(1)} %broadcast_multiply_fusion.6), kind=kOutput, calls=%fused_computation.37 | convolution fusion | flops 6458179584 | bytes 13656064 | tf_op jit(solution)/shard_map/rd,rf->df/dot_general | solution.py:250
  346.1 14.8 %fusion.65 = f32[1024,2048]{1,0:T(8,128)} fusion(bf16[2048,2048]{1,0:T(8,128)(2,1)} %all-gather.13.cloned.1.call-done, bf16[1024,2048]{1,0:T(8,128)(2,1)} %all-gather.7.cloned.1.call-done, f32[2048]{0:T(1024)S(1)} %bitcast.98, f32[2048]{0:T(1024)S(1)} %bitcast.91, f32[1024]{0:T(1024)S(1)} %add_rsqrt_fusion, f32[1024]{0:T(1024)S(1)} %broadcast_multiply_fusion.6), kind=kOutput, calls=%fused_computation.166 | convolution fusion | flops 8602517504 | bytes 20996096 | tf_op jit(solution)/shard_map/dot_general | solution.py:172
  365.7 33.5 %convert_reduce_fusion.1 = (f32[2048]{0:T(1024)S(1)}, bf16[1024,2048]{1,0:T(8,128)(2,1)}, f32[1024,2048]{1,0:T(8,128)}) fusion(f32[1024,2048]{1,0:T(8,128)} %fusion.65, f32[2048]{0:T(1024)S(1)} %copy-done.36, bf16[1024,2048]{1,0:T(8,128)(2,1)} %all-gather.17.cloned.1.call-done, bf16[2048,2048]{1,0:T(8,128)(2,1)} %all-gather.15.cloned.1.call-done), kind=kOutput, calls=%fused_computation.7 | convolution fusion | flops 8747218944 | bytes 33570816 | tf_op jit(solution)/shard_map/rd,fd->rf/dot_general | solution.py:194
  399.3 8.2 multiply_convert_fusion.1
  409.5 13.6 %convolution_convert_fusion = bf16[2048,2048]{1,0:T(8,128)(2,1)} fusion(bf16[1024,2048]{1,0:T(8,128)(2,1)S(1)} %multiply_convert_fusion.1, bf16[1024,2048]{1,0:T(8,128)(2,1)} %all-gather.17.cloned.1.call-done), kind=kOutput, calls=%fused_computation.35 | convolution fusion | flops 8594128896 | bytes 16777216 | tf_op jit(solution)/shard_map/rf,rd->fd/dot_general | solution.py:190
  423.2 16.0 %convolution_convert_fusion.1 = bf16[2048,2048]{1,0:T(8,128)(2,1)} fusion(bf16[1024,2048]{1,0:T(8,128)(2,1)} %get-tuple-element.97, bf16[1024,2048]{1,0:T(8,128)(2,1)} %all-gather.7.cloned.1.call-done, f32[2048]{0:T(1024)S(1)} %bitcast.99, f32[2048]{0:T(1024)S(1)} %bitcast.92, f32[1024]{0:T(1024)S(1)} %add_rsqrt_fusion, f32[1024]{0:T(1024)S(1)} %broadcast_multiply_fusion.6), kind=kOutput, calls=%fused_computation.36 | convolution fusion | flops 8606711808 | bytes 16801792 | tf_op jit(solution)/shard_map/rd,rf->df/dot_general | solution.py:196
  441.1 11.5 fusion.77
  452.6 13.4 fusion.78
  466.1 12.8 fusion.76
  478.9 6.0 convolution_add_fusion.1
  490.1 60.5 %reduce-scatter.14.cloned.1.call-done = bf16[2048,256]{1,0:T(8,128)(2,1)} async-done(((bf16[2048,2048]{1,0:T(8,128)(2,1)}), bf16[2048,256]{1,0:T(8,128)(2,1)}) %reduce-scatter.14.cloned.1.call-update) | async-done | bytes 1048592 | tf_op jit(solution)/shard_map/reduce_scatter | solution.py:290
  553.3 72.3 %reduce-scatter.12.cloned.1.call-done = bf16[256,2048]{1,0:T(8,128)(2,1)} async-done(((bf16[2048,2048]{1,0:T(8,128)(2,1)}), bf16[256,2048]{1,0:T(8,128)(2,1)}) %reduce-scatter.12.cloned.1.call-update) | async-done | bytes 1048592 | tf_op jit(solution)/shard_map/reduce_scatter | solution.py:282
  628.4 563.1 %all-reduce.12.cloned.1.call-done = (f32[1024,2048]{1,0:T(8,128)}, f32[1024,2048]{1,0:T(8,128)}) async-done(((f32[1024,2048]{1,0:T(8,128)}, f32[1024,2048]{1,0:T(8,128)}), (f32[1024,2048]{1,0:T(8,128)}, f32[1024,2048]{1,0:T(8,128)})) %all-reduce.12.cloned.1.call-update) | async-done | bytes 16777232 | tf_op jit(solution)/shard_map/psum | solution.py:255
  1191.5 11.7 fusion.66
  1205.6 26.3 %all-reduce.8 = (f32[4,512]{1,0:T(4,128)S(1)}, f32[1536]{0:T(1024)}, f32[512]{0:T(512)S(1)}, f32[2048]{0:T(1024)}) all-reduce(f32[4,512]{1,0:T(4,128)S(1)} %pad_maximum_fusion.15, f32[1536]{0:T(1024)S(1)} %reduce_sum.200, f32[512]{0:T(512)S(1)} %get-tuple-element.121, ...), channel_id=1, replica_groups=mesh['fsdp'=4,'ctx'=2,'tp'=4] {'fsdp','ctx'}, use_global_device_ids=true, to_apply=%region_23.24 | all-reduce | flops 6144 | bytes 49152 | tf_op jit(solution)/shard_map/psum | solution.py:275
  1232.5 104.7 %reduce-scatter.6.cloned.1.call-done = f32[1024,512]{1,0:T(8,128)} async-done(((f32[1024,2048]{1,0:T(8,128)}), f32[1024,512]{1,0:T(8,128)}) %reduce-scatter.6.cloned.1.call-update) | async-done | bytes 2097168 | tf_op jit(solution)/shard_map/reduce_scatter | solution.py:180
  (228 shorter events, 139.4 us)
Async XLA Ops:
  7.2 30.3 %copy-start.46 = (s32[1,13]{1,0:T(1,128)S(1)}, s32[1,13]{1,0:T(1,128)}, u32[]{:S(2)}) copy-start(s32[1,13]{1,0:T(1,128)} %param.33) | copy-start | bytes 160
  7.2 86.1 %all-gather.7.cloned.1.call-start = ((), (), s32[]{:S(2)}) async-start(), calls=%async_computation.5 | async-start | bytes 5242880 | tf_op jit(solution)/shard_map/all_gather | solution.py:94
  7.9 131.4 %all-gather.9.cloned.1.call-start = ((), (), s32[]{:S(2)}) async-start(), calls=%async_computation.6 | async-start | bytes 7077888 | tf_op jit(solution)/shard_map/all_gather | solution.py:99
  8.7 169.3 %all-gather.11.cloned.1.call-start = ((), (), s32[]{:S(2)}) async-start(), calls=%async_computation.7 | async-start | bytes 2359296 | tf_op jit(solution)/shard_map/all_gather | solution.py:103
  9.4 242.2 %all-gather.17.cloned.1.call-start = ((), (), s32[]{:S(2)}) async-start(), calls=%async_computation.11 | async-start | bytes 5242880 | tf_op jit(solution)/shard_map/all_gather | solution.py:187
  10.0 335.5 %all-gather.13.cloned.1.call-start = ((), (), s32[]{:S(2)}) async-start(), calls=%async_computation.8 | async-start | bytes 9437184 | tf_op jit(solution)/shard_map/all_gather | solution.py:100
  10.6 355.2 %all-gather.15.cloned.1.call-start = ((), (), s32[]{:S(2)}) async-start(), calls=%async_computation.9 | async-start | bytes 9437184 | tf_op jit(solution)/shard_map/all_gather | solution.py:104
  11.1 474.5 %reduce-scatter.10.cloned.1.call-start = ((), (), s32[]{:S(2)}) async-start(), calls=%async_computation.13 | async-start | bytes 2359296 | tf_op jit(solution)/shard_map/reduce_scatter | solution.py:287
  35.0 296.7 %copy-start.37 = (f32[1,2048]{1,0:T(1,128)}, f32[1,2048]{1,0:T(1,128)S(1)}, u32[]{:S(2)}) copy-start(f32[1,2048]{1,0:T(1,128)S(1)} %get-tuple-element.129) | copy-start | bytes 24580
  37.5 132.0 %copy-start.12 = (f32[1024,32]{1,0:T(8,128)}, f32[1024,32]{1,0:T(8,128)S(1)}, u32[]{:S(2)}) copy-start(f32[1024,32]{1,0:T(8,128)S(1)} %get-tuple-element.137) | copy-start | bytes 393220
  37.5 132.0 %copy-start.14 = (f32[1024,32]{1,0:T(8,128)}, f32[1024,32]{1,0:T(8,128)S(1)}, u32[]{:S(2)}) copy-start(f32[1024,32]{1,0:T(8,128)S(1)} %get-tuple-element.138) | copy-start | bytes 393220
  174.7 87.8 %collective-permute-start.1 = (bf16[1024,2,256]{2,0,1:T(8,128)(2,1)}, bf16[1024,2,256]{2,0,1:T(8,128)(2,1)}, u32[]{:S(2)}, u32[]{:S(2)}) collective-permute-start(bf16[1024,2,256]{2,0,1:T(8,128)(2,1)} %pad_maximum_fusion.11), channel_id=1, source_target_pairs={{0,4},{1,5},{2,6},{3,7},{8,12},{9,13},{10,14},{11,15},{16,20},{17,... | collective-permute-start | bytes 3145736 | tf_op jit(solution)/shard_map/ppermute | solution.py:22
  259.8 20.5 %collective-permute-start = (bf16[1024,2,256]{0,2,1:T(8,128)(2,1)S(1)}, bf16[1024,2,256]{0,2,1:T(8,128)(2,1)S(1)}, u32[]{:S(2)}, u32[]{:S(2)}) collective-permute-start(bf16[1024,2,256]{0,2,1:T(8,128)(2,1)S(1)} %fusion.42), channel_id=1, source_target_pairs={{0,4},{1,5},{2,6},{3,7},{8,12},{9,13},{10,14},{11,15},{16,20},{17,... | collective-permute-start | bytes 3145736 | tf_op jit(solution)/shard_map/ppermute | solution.py:22
  262.6 21.1 %copy-start.22 = (bf16[1024,2,256]{2,0,1:T(8,128)(2,1)}, bf16[1024,2,256]{2,0,1:T(8,128)(2,1)S(1)}, u32[]{:S(2)}) copy-start(bf16[1024,2,256]{2,0,1:T(8,128)(2,1)S(1)} %pad_maximum_fusion.10) | copy-start | bytes 3145732
  278.7 46.7 %collective-permute-start.3 = (f32[1024,2,256]{2,0,1:T(8,128)}, f32[1024,2,256]{2,0,1:T(8,128)}, u32[]{:S(2)}, u32[]{:S(2)}) collective-permute-start(f32[1024,2,256]{2,0,1:T(8,128)} %slice.263), channel_id=1, source_target_pairs={{4,0},{5,1},{6,2},{7,3},{12,8},{13,9},{14,10},{15,11},{20,16},{21,... | collective-permute-start | bytes 6291464 | tf_op jit(solution)/shard_map/ppermute | solution.py:22
  301.4 17.6 %collective-permute-start.2 = (f32[1024,2,256]{2,0,1:T(8,128)}, f32[1024,2,256]{2,0,1:T(8,128)}, u32[]{:S(2)}, u32[]{:S(2)}) collective-permute-start(f32[1024,2,256]{2,0,1:T(8,128)} %slice.261), channel_id=1, source_target_pairs={{4,0},{5,1},{6,2},{7,3},{12,8},{13,9},{14,10},{15,11},{20,16},{21,... | collective-permute-start | bytes 6291464 | tf_op jit(solution)/shard_map/ppermute | solution.py:22
  311.8 175.7 %reduce-scatter.8.cloned.1.call-start = ((), (), s32[]{:S(2)}) async-start(), calls=%async_computation.12 | async-start | bytes 7077888 | tf_op jit(solution)/shard_map/reduce_scatter | solution.py:279
  345.4 205.2 %reduce-scatter.14.cloned.1.call-start = ((), (), s32[]{:S(2)}) async-start(), calls=%async_computation.15 | async-start | bytes 9437184 | tf_op jit(solution)/shard_map/reduce_scatter | solution.py:290
  423.2 202.4 %reduce-scatter.12.cloned.1.call-start = ((), (), s32[]{:S(2)}) async-start(), calls=%async_computation.14 | async-start | bytes 9437184 | tf_op jit(solution)/shard_map/reduce_scatter | solution.py:282
  439.2 752.3 %all-reduce.12.cloned.1.call-start = ((), (), s32[]{:S(2)}) async-start(), calls=%async_computation.16 | async-start | bytes 33554432 | tf_op jit(solution)/shard_map/psum | solution.py:255
  466.0 871.2 %reduce-scatter.6.cloned.1.call-start = ((), (), s32[]{:S(2)}) async-start(), calls=%async_computation.10 | async-start | bytes 10485760 | tf_op jit(solution)/shard_map/reduce_scatter | solution.py:180
  484.9 706.6 %copy-start.38 = (f32[1,2048]{1,0:T(1,128)S(1)}, f32[1,2048]{1,0:T(1,128)}, u32[]{:S(2)}) copy-start(f32[1,2048]{1,0:T(1,128)} %copy-done.37) | copy-start | bytes 24580
  1203.2 134.0 %copy-start.18 = (bf16[1024,512]{1,0:T(8,128)(2,1)S(1)}, bf16[1024,512]{1,0:T(8,128)(2,1)}, u32[]{:S(2)}) copy-start(bf16[1024,512]{1,0:T(8,128)(2,1)} %param.29) | copy-start | bytes 3145732
  1231.9 108.9 %copy-start.42 = (f32[512]{0:T(512)}, f32[512]{0:T(512)S(1)}, u32[]{:S(2)}) copy-start(f32[512]{0:T(512)S(1)} %get-tuple-element.178) | copy-start | bytes 6148
  (42 other events, 191.9 us)
Sparse Core Ops, SparseCore 0:
  9.6 83.6 all-gather.6
  95.1 44.1 all-gather.8
  141.2 28.1 all-gather.10
  170.8 80.7 all-gather.16
  253.4 52.9 all-gather.12
  308.1 57.6 all-gather.14
  369.0 41.2 reduce-scatter.9
  414.0 61.7 reduce-scatter.7
  479.3 71.2 reduce-scatter.13
  554.3 71.2 reduce-scatter.11
  628.2 563.2 all-reduce.11
  1193.7 143.4 reduce-scatter.5
where the time goes:
time: 1350 us
  waiting for transfers between devices  975 us (72%)
  matrix products  196 us (15%)
  other arithmetic  68.2 us (5%)
  local copies, waits for them, and re-layouts  43.1 us (3%)
  blocking collectives  41.4 us (3%)
  between operations  15.3 us (1%)
    psum x1, waiting for transfers between devices, on_device(): total_attn, total_ffn = lax.psum((grad_attn_in, grad_ffn_in), 'tp')  563 us
    reduce_scatter x1, waiting for transfers between devices, on_device(): lax.psum_scatter(partial_out, 'tp', scatter_dimension=1, tiled=True)  105 us
    all_gather x1, waiting for transfers between devices, on_device(): cotangent = lax.all_gather(out_grad, 'tp', axis=1, tiled=True)  73.7 us
    reduce_scatter x1, waiting for transfers between devices, on_device(): lax.psum_scatter(grad_up_w.astype(jnp.bfloat16), ('fsdp', 'ctx'), scatter...  72.3 us
    reduce_scatter x1, waiting for transfers between devices, on_device(): lax.psum_scatter(grad_down_w.astype(jnp.bfloat16), ('fsdp', 'ctx'), scatt...  60.5 us
    all_gather x1, waiting for transfers between devices, on_device(): lax.all_gather(residual, 'tp', axis=1, tiled=True)  50.9 us
    all_gather x1, waiting for transfers between devices, on_device(): lax.all_gather(qkv_weight, ('fsdp', 'ctx'), axis=0, tiled=True)  41.3 us
    dot_general x1, matrix products, on_device(): jnp.einsum('rd,fd->rf', cotangent, down_full, preferred_element_type=jnp....  33.5 us
  transfers between devices with their start and end apart: 16, of which 8 were waited for; matrix products, arithmetic and copies ran while one was open for 22% of the time, Pallas kernels for 0%

commit v1 on v0

--- a/solution.py
+++ b/solution.py
@@ -4,6 +4,8 @@
 import jax
 import jax.numpy as jnp
 from jax import lax
+from jax.experimental import pallas as pl
+from jax.experimental.pallas import tpu as pltpu
 from jax.sharding import PartitionSpec as P
 
 HEAD_DIM = 256
@@ -309,6 +311,426 @@
     )
 
 
+low = jnp.bfloat16
+wide = jnp.float32
+tile = 256
+
+
+def trade(x, axis, bit):
+    peers = lax.axis_size(axis)
+    return lax.ppermute(x, axis, [(i, i ^ bit) for i in range(peers)])
+
+
+def gather_line(x, axis):
+    near = trade(x, axis, 1)
+    far = trade(x, axis, 2)
+    return (x, near, far, trade(far, axis, 1))
+
+
+def lay_out(pieces, place, dim):
+    width = pieces[0].shape[dim]
+    shape = list(pieces[0].shape)
+    shape[dim] = width * len(pieces)
+    whole = jnp.zeros(shape, pieces[0].dtype)
+    for step, piece in enumerate(pieces):
+        whole = lax.dynamic_update_slice_in_dim(whole, piece, (place ^ step) * width, dim)
+    return whole
+
+
+def block_of(x, index, dim, blocks):
+    width = x.shape[dim] // blocks
+    return lax.dynamic_slice_in_dim(x, index * width, width, dim)
+
+
+def scatter_line(total, axis, dim):
+    place = lax.axis_index(axis)
+    far_side = trade(block_of(total, place ^ 3, dim, 4).astype(low), axis, 1)
+    near = trade(block_of(total, place ^ 1, dim, 4).astype(low), axis, 1)
+    passed = block_of(total, place ^ 2, dim, 4).astype(wide) + far_side.astype(wide)
+    far = trade(passed.astype(low), axis, 2)
+    own = block_of(total, place, dim, 4).astype(wide)
+    return own + near.astype(wide) + far.astype(wide)
+
+
+def half_of(x, index, dim):
+    return block_of(x, index, dim, 2)
+
+
+def join_cores(mine, theirs, core, dim):
+    first = jnp.where(core == 0, mine, theirs)
+    second = jnp.where(core == 0, theirs, mine)
+    return jnp.concatenate([first, second], axis=dim)
+
+
+def turn(rows, cosine, sine, sign):
+    half_rot = ROTARY // 2
+    lane = lax.broadcasted_iota(jnp.int32, cosine.shape, 1)
+    front = rows[:, :128]
+    ahead = pltpu.roll(front, 128 - half_rot, 1)
+    behind = pltpu.roll(front, half_rot, 1)
+    other = jnp.where(lane < half_rot, -ahead, behind)
+    turned = front * cosine + other * (sine * sign)
+    return jnp.concatenate([turned, rows[:, 128:]], axis=1)
+
+
+def contract(a, b, dims):
+    return lax.dot_general(a, b, ((dims[:1], dims[1:]), ((), ())), preferred_element_type=wide)
+
+
+def scores_of(keys, query, info, trunk_end, first_row, scale):
+    scores = contract(keys, query, (1, 1)) * scale
+    span = scores.shape[0]
+    key_place = lax.broadcasted_iota(jnp.int32, scores.shape, 0)
+    query_place = first_row + lax.broadcasted_iota(jnp.int32, scores.shape, 1)
+    seen = (
+        (key_place < trunk_end)
+        | ((key_place >= info[0:1]) & (key_place < info[1:2]))
+        | (key_place >= info[2:3])
+    ) & (key_place <= query_place)
+    return jnp.where(seen, scores, masked_score)
+
+
+def attend_kernel(scalars, joined, cosine, sine, info, packed, attended, log_total, scale):
+    rows = joined.shape[0]
+    blocks = rows // tile
+    shift = scalars[0] * (blocks // 2)
+    for block in range(blocks):
+        here = pl.ds(block * tile, tile)
+        there = pl.ds(pl.multiple_of(lax.rem(block + shift, blocks) * tile, tile), tile)
+        for part in range(3):
+            vectors = joined[here, part * HEAD_DIM : (part + 1) * HEAD_DIM]
+            if part < 2:
+                vectors = turn(vectors, cosine[here, :], sine[here, :], 1.0)
+            packed[part, there, :] = vectors.astype(low)
+    for block in range(blocks):
+        span = (block + 1) * tile
+        query = packed[0, block * tile : span, :]
+        about = info[:, block * tile : span]
+        scores = scores_of(packed[1, :span, :], query, about, scalars[1], block * tile, scale)
+        top = jnp.max(scores, axis=0, keepdims=True)
+        powers = jnp.exp(scores - top)
+        total = jnp.sum(powers, axis=0, keepdims=True)
+        probs = (powers * (1.0 / total)).astype(low)
+        there = pl.ds(pl.multiple_of(lax.rem(block + shift, blocks) * tile, tile), tile)
+        attended[there, :] = contract(probs, packed[2, :span, :], (0, 0)).astype(low)
+        log_total[0:1, block * tile : span] = top + jnp.log(total)
+
+
+def attend_back_kernel(
+    scalars, packed, grads, log_total, cosine, sine, info, joined_grad, bias_grad, key_grad,
+    value_grad, scale
+):
+    rows = grads.shape[0]
+    blocks = rows // tile
+    shift = scalars[0] * (blocks // 2)
+    bias_total = jnp.zeros((1, 3 * HEAD_DIM), wide)
+    for block in reversed(range(blocks)):
+        span = (block + 1) * tile
+        before = block * tile
+        query = packed[0, before:span, :]
+        about = info[:, before:span]
+        there = pl.ds(pl.multiple_of(lax.rem(block + shift, blocks) * tile, tile), tile)
+        grad = grads[there, :]
+        scores = scores_of(packed[1, :span, :], query, about, scalars[1], before, scale)
+        probs = jnp.exp(scores - log_total[0:1, before:span])
+        value_part = contract(probs.astype(low), grad, (1, 0))
+        dots = contract(packed[2, :span, :], grad, (1, 1))
+        delta = jnp.sum(probs * dots, axis=0, keepdims=True)
+        score_grad = (probs * (dots - delta)).astype(low)
+        query_grad = contract(score_grad, packed[1, :span, :], (0, 0)) * scale
+        key_part = contract(score_grad, query, (1, 0)) * scale
+        if block == blocks - 1:
+            key_grad[...] = key_part
+            value_grad[...] = value_part
+        else:
+            key_grad[:span, :] += key_part
+            value_grad[:span, :] += value_part
+        parts = (
+            turn(query_grad, cosine[there, :], sine[there, :], -1.0),
+            turn(key_grad[before:span, :], cosine[there, :], sine[there, :], -1.0),
+            value_grad[before:span, :],
+        )
+        together = jnp.concatenate(parts, axis=1).astype(low)
+        joined_grad[there, :] = together
+        bias_total += jnp.sum(together.astype(wide), axis=0, keepdims=True)
+    bias_grad[...] = jnp.broadcast_to(bias_total, bias_grad.shape)
+
+
+def whole(shape):
+    return pl.BlockSpec(shape, lambda head, scalars: (0,) * len(shape))
+
+
+def attend(scalars, joined, cosine, sine, info):
+    rows, columns = joined.shape
+    heads = columns // (3 * HEAD_DIM)
+    pairs = rows * (rows + tile) // 2
+    return pl.pallas_call(
+        partial(attend_kernel, scale=1.0 / math.sqrt(HEAD_DIM)),
+        grid_spec=pltpu.PrefetchScalarGridSpec(
+            num_scalar_prefetch=1,
+            grid=(heads,),
+            in_specs=[
+                pl.BlockSpec((rows, 3 * HEAD_DIM), lambda head, scalars: (0, head)),
+                whole((rows, 128)),
+                whole((rows, 128)),
+                whole((8, rows)),
+            ],
+            out_specs=[
+                pl.BlockSpec((3, rows, HEAD_DIM), lambda head, scalars: (0, 0, head)),
+                pl.BlockSpec((rows, HEAD_DIM), lambda head, scalars: (0, head)),
+                pl.BlockSpec((8, rows), lambda head, scalars: (head, 0)),
+            ],
+        ),
+        out_shape=[
+            jax.ShapeDtypeStruct((3, rows, heads * HEAD_DIM), low),
+            jax.ShapeDtypeStruct((rows, heads * HEAD_DIM), low),
+            jax.ShapeDtypeStruct((heads * 8, rows), wide),
+        ],
+        compiler_params=pltpu.CompilerParams(vmem_limit_bytes=56 * 1024 * 1024),
+        cost_estimate=pl.CostEstimate(
+            flops=heads * pairs * HEAD_DIM * 4,
+            bytes_accessed=rows * columns * 8,
+            transcendentals=heads * pairs,
+        ),
+        name="attend",
+    )(scalars, joined, cosine, sine, info)
+
+
+def attend_back(scalars, packed, grads, log_total, cosine, sine, info):
+    rows, width = grads.shape
+    heads = width // HEAD_DIM
+    pairs = rows * (rows + tile) // 2
+    return pl.pallas_call(
+        partial(attend_back_kernel, scale=1.0 / math.sqrt(HEAD_DIM)),
+        grid_spec=pltpu.PrefetchScalarGridSpec(
+            num_scalar_prefetch=1,
+            grid=(heads,),
+            in_specs=[
+                pl.BlockSpec((3, rows, HEAD_DIM), lambda head, scalars: (0, 0, head)),
+                pl.BlockSpec((rows, HEAD_DIM), lambda head, scalars: (0, head)),
+                pl.BlockSpec((8, rows), lambda head, scalars: (head, 0)),
+                whole((rows, 128)),
+                whole((rows, 128)),
+                whole((8, rows)),
+            ],
+            out_specs=[
+                pl.BlockSpec((rows, 3 * HEAD_DIM), lambda head, scalars: (0, head)),
+                pl.BlockSpec((8, 3 * HEAD_DIM), lambda head, scalars: (0, head)),
+            ],
+            scratch_shapes=[
+                pltpu.VMEM((rows, HEAD_DIM), wide),
+                pltpu.VMEM((rows, HEAD_DIM), wide),
+            ],
+        ),
+        out_shape=[
+            jax.ShapeDtypeStruct((rows, 3 * width), low),
+            jax.ShapeDtypeStruct((8, 3 * width), wide),
+        ],
+        compiler_params=pltpu.CompilerParams(vmem_limit_bytes=56 * 1024 * 1024),
+        cost_estimate=pl.CostEstimate(
+            flops=heads * pairs * HEAD_DIM * 10,
+            bytes_accessed=rows * width * 16,
+            transcendentals=heads * pairs,
+        ),
+        name="attend_back",
+    )(scalars, packed, grads, log_total, cosine, sine, info)
+
+
+def tree_info(lengths, parent, rows):
+    labels = jnp.arange(SEGS)
+    ends = jnp.sum(jnp.where(labels[None, :] <= labels[:, None], lengths[None, :], 0), axis=1)
+    starts = ends - lengths
+    hot_parent = parent[:, None] == labels[None, :]
+    parent_start = jnp.sum(jnp.where(hot_parent, starts[None, :], 0), axis=1)
+    parent_end = jnp.sum(jnp.where(hot_parent, ends[None, :], 0), axis=1)
+    places = jnp.arange(rows, dtype=jnp.int32)
+    inside = (places[None, :] >= starts[:, None]) & (places[None, :] < ends[:, None])
+    pick = lambda table: jnp.sum(jnp.where(inside, table[:, None], 0), axis=0)
+    spans = [pick(parent_start), pick(parent_end), pick(starts)]
+    return jnp.stack(spans + [places] * 5).astype(jnp.int32), ends[0]
+
+
+def rotary_tables(depth):
+    half_rot = ROTARY // 2
+    lane = jnp.arange(128)
+    frequency = jnp.power(10000.0, -2.0 * (lane % half_rot).astype(wide) / ROTARY)
+    frequency = jnp.where(lane < ROTARY, frequency, 0.0)
+    angles = depth.astype(wide)[:, None] * frequency[None, :]
+    return jnp.cos(angles), jnp.sin(angles)
+
+
+def on_device_split(
+    residual,
+    out_grad,
+    path_depth,
+    seg_lengths,
+    parents,
+    attn_norm_gain,
+    attn_norm_bias,
+    ffn_norm_gain,
+    ffn_norm_bias,
+    qkv_weight,
+    qkv_bias,
+    dense_weight,
+    dense_bias,
+    up_weight,
+    up_bias,
+    down_weight,
+    down_bias,
+):
+    core = lax.axis_index("ctx")
+    line = lax.axis_index("tp")
+    held_rows, held_width = residual.shape
+    rows = 2 * held_rows
+    width = 4 * held_width
+
+    norm_rows = jnp.stack([attn_norm_gain, attn_norm_bias, ffn_norm_gain, ffn_norm_bias] * 4)
+    pieces = gather_line(jnp.concatenate([residual, norm_rows], axis=0), "tp")
+    twins = [trade(piece[:held_rows], "ctx", 1) for piece in pieces]
+    other_depth = trade(path_depth, "ctx", 1)
+
+    def share(weight, dim_split, dim_join):
+        mine = half_of(weight, core, dim_split)
+        theirs = trade(half_of(weight, 1 - core, dim_split), "ctx", 1)
+        return join_cores(mine, theirs, core, dim_join)
+
+    def gather_fsdp(weight, dim):
+        return lax.all_gather(weight, "fsdp", axis=dim, tiled=True)
+
+    up_full = gather_fsdp(share(up_weight, 1, 0), 0)
+    qkv_full = gather_fsdp(share(qkv_weight, 1, 0), 0)
+    down_full = gather_fsdp(share(down_weight, 0, 1), 1)
+    dense_full = gather_fsdp(share(dense_weight, 0, 1), 1)
+    qkv_shift = half_of(qkv_bias, core, 0).astype(wide)
+    up_shift = half_of(up_bias, core, 0).astype(wide)
+
+    info, trunk_end = tree_info(seg_lengths[0], parents[0], rows)
+    scalars = jnp.stack([core, trunk_end]).astype(jnp.int32)
+    cosine, sine = rotary_tables(jnp.concatenate([path_depth, other_depth]))
+
+    norm_terms = lay_out([piece[held_rows : held_rows + 8] for piece in pieces], line, 1).astype(wide)
+    rows_low = jnp.concatenate(
+        [lay_out([piece[:held_rows] for piece in pieces], line, 1), lay_out(twins, line, 1)], axis=0
+    )
+    rows_wide = rows_low.astype(wide)
+    mean = jnp.mean(rows_wide, axis=1, keepdims=True)
+    centred = rows_wide - mean
+    inverse_scale = lax.rsqrt(jnp.mean(centred * centred, axis=1, keepdims=True) + norm_epsilon)
+    normed = centred * inverse_scale
+    attn_in = (normed * norm_terms[0:1] + norm_terms[1:2]).astype(low)
+    ffn_in = (normed * norm_terms[2:3] + norm_terms[3:4]).astype(low)
+
+    joined = jnp.dot(attn_in, qkv_full, preferred_element_type=wide) + qkv_shift
+    packed, attended, log_total = attend(scalars, joined, cosine, sine, info)
+
+    hidden_pre = jnp.dot(ffn_in, up_full, preferred_element_type=wide) + up_shift
+    phi = 0.5 * (1.0 + lax.erf(hidden_pre * math.sqrt(0.5)))
+    hidden = (hidden_pre * phi).astype(low)
+
+    def branches(first, last):
+        return jnp.dot(attended[first:last], dense_full, preferred_element_type=wide) + jnp.dot(
+            hidden[first:last], down_full, preferred_element_type=wide
+        )
+
+    for_twin = trade(branches(held_rows, rows).astype(low), "ctx", 1)
+    chip_out = branches(0, held_rows) + for_twin.astype(wide)
+    shared_out = scatter_line(chip_out, "tp", 1)
+    output = (
+        residual.astype(wide) + shared_out + dense_bias.astype(wide) + down_bias.astype(wide)
+    ).astype(low)
+
+    grad_pieces = gather_line(out_grad, "tp")
+    grad_twins = [trade(piece, "ctx", 1) for piece in grad_pieces]
+    cotangent = jnp.concatenate(
+        [lay_out(grad_pieces, line, 1), lay_out(grad_twins, line, 1)], axis=0
+    )
+
+    def reduce_fsdp(grad, dim_split, dim_join):
+        mine = lax.psum_scatter(grad.astype(low), "fsdp", scatter_dimension=dim_join, tiled=True)
+        theirs = trade(half_of(mine, 1 - core, dim_join), "ctx", 1)
+        return join_cores(half_of(mine, core, dim_join), theirs, core, dim_split).astype(wide)
+
+    grad_hidden = contract(cotangent, down_full, (1, 1))
+    slope = phi + hidden_pre * (jnp.exp(-0.5 * hidden_pre * hidden_pre) * (1.0 / math.sqrt(2.0 * math.pi)))
+    grad_pre = (grad_hidden * slope).astype(low)
+    grad_up_bias = jnp.sum(grad_pre.astype(wide), axis=0)
+    down_weight_grad = reduce_fsdp(contract(hidden, cotangent, (0, 0)), 0, 1)
+    up_weight_grad = reduce_fsdp(contract(ffn_in, grad_pre, (0, 0)), 1, 0)
+    grad_ffn_in = contract(grad_pre, up_full, (1, 1))
+
+    dense_weight_grad = reduce_fsdp(contract(attended, cotangent, (0, 0)), 0, 1)
+    grad_attended = contract(cotangent, dense_full, (1, 1)).astype(low)
+    grad_joined, bias_rows = attend_back(
+        scalars, packed, grad_attended, log_total, cosine, sine, info
+    )
+    grad_qkv_bias = bias_rows[0]
+    grad_attn_in = contract(grad_joined, qkv_full, (1, 1))
+    qkv_weight_grad = reduce_fsdp(contract(attn_in, grad_joined, (0, 0)), 1, 0)
+
+    mixed = grad_attn_in * norm_terms[0:1] + grad_ffn_in * norm_terms[2:3]
+    row_sums = jnp.stack([jnp.sum(mixed, axis=1), jnp.sum(mixed * normed, axis=1)])
+    norm_sums = jnp.stack(
+        [
+            jnp.sum(grad_attn_in * normed, axis=0),
+            jnp.sum(grad_attn_in, axis=0),
+            jnp.sum(grad_ffn_in * normed, axis=0),
+            jnp.sum(grad_ffn_in, axis=0),
+        ]
+    )
+    mixed_twin = trade(mixed[held_rows:].astype(low), "ctx", 1)
+    shared_mixed = scatter_line(mixed[:held_rows] + mixed_twin.astype(wide), "tp", 1)
+
+    row_total = row_sums[:, :held_rows] + trade(row_sums[:, held_rows:], "ctx", 1)
+    for bit in (1, 2):
+        row_total = row_total + trade(row_total, "tp", bit)
+    row_means = row_total / width
+
+    held_grad_sum = jnp.sum(out_grad.astype(wide), axis=0)
+    columns = jnp.concatenate([norm_sums.reshape(-1), held_grad_sum, grad_qkv_bias, grad_up_bias])
+    for bit in (1, 2):
+        columns = columns + trade(columns, "fsdp", bit)
+    other_columns = trade(columns, "ctx", 1)
+    summed = 4 * width + held_width
+    together = columns[:summed] + other_columns[:summed]
+    out_bias_grad = together[4 * width :]
+    norm_total = together[: 4 * width].reshape(4, width)
+    for bit in (1, 2):
+        norm_total = norm_total + trade(norm_total, "tp", bit)
+    norm_total = block_of(norm_total, line, 1, 4)
+    parts = qkv_bias.shape[0] // 2
+    qkv_bias_grad = join_cores(
+        columns[summed : summed + parts], other_columns[summed : summed + parts], core, 0
+    )
+    up_bias_grad = join_cores(columns[summed + parts :], other_columns[summed + parts :], core, 0)
+
+    own_scale = inverse_scale[:held_rows]
+    own_normed = (residual.astype(wide) - mean[:held_rows]) * own_scale
+    back = own_scale * (
+        shared_mixed - row_means[0][:, None] - own_normed * row_means[1][:, None]
+    )
+    input_grad = (out_grad.astype(wide) + back).astype(low)
+    return (
+        output,
+        input_grad,
+        norm_total[0],
+        norm_total[1],
+        norm_total[2],
+        norm_total[3],
+        qkv_weight_grad,
+        qkv_bias_grad,
+        dense_weight_grad,
+        out_bias_grad,
+        up_weight_grad,
+        up_bias_grad,
+        down_weight_grad,
+        out_bias_grad,
+    )
+
+
+def splits_heads(mesh):
+    return mesh.shape["tp"] == 4 and mesh.shape["fsdp"] == 4 and mesh.shape["ctx"] == 2
+
+
 def solution(mesh):
     placed = (
         P(("fsdp", "ctx"), "tp"),
@@ -330,7 +752,7 @@
         P("tp"),
     )
     return jax.shard_map(
-        on_device,
+        on_device_split if splits_heads(mesh) else on_device,
         mesh=mesh,
         in_specs=placed,
         out_specs=(

time: 1350 us -> 577 us (0.43)
  waiting for transfers between devices: 975 us -> 225 us
  blocking collectives: 41.4 us -> 0 us
  Pallas kernels: 0 us -> 31.3 us
  matrix products: 196 us -> 169 us
  other arithmetic: 68.2 us -> 50.2 us
  starting transfers between devices: 8.65 us -> 25.1 us
  local copies, waits for them, and re-layouts: 43.1 us -> 56.8 us
    psum x1 -> x0, waiting for transfers between devices: 563 us -> none  [on_device(): total_attn, total_ffn = lax.psum((grad_attn_in, grad_ffn_in), 'tp')]
    reduce_scatter x5 -> x4, waiting for transfers between devices: 238 us -> 0.02 us  [reduce_fsdp(): lax.psum_scatter(grad.astype(low), 'fsdp', scatter_dimension=dim_join, ti...]
    ppermute x4 -> x39, waiting for transfers between devices: 0.01 us -> 225 us  [trade(): return lax.ppermute(x, axis, [(i, i ^ bit) for i in range(peers)])]
    all_gather x6 -> x4, waiting for transfers between devices: 171 us -> 0.06 us  [gather_fsdp(): return lax.all_gather(weight, 'fsdp', axis=dim, tiled=True)]
    pallas_call x0 -> x2, Pallas kernels: none -> 31.3 us  [the longest x1 17 us: attend_back(): pl.pallas_call(partial(attend_back_kernel, scale=1.0 / math.sqrt(HEAD_DIM...]
    dot_general x26 -> x14, matrix products: 196 us -> 169 us  [the longest x8 103 us: contract(): lax.dot_general(a, b, ((dims[:1], dims[1:]), ((), ())), preferred_element...]
    dynamic_update_slice x0 -> x20, local copies, waits for them, and re-layouts: none -> 26.6 us  [lay_out(): lax.dynamic_update_slice_in_dim(whole, piece, (place ^ step) * width, dim)]
    psum x1 -> x0, blocking collectives: 26.3 us -> none  [on_device(): lax.psum((grad_qkv_b, grad_up_b, grad_out_bias, norm_grads), ('fsdp', 'ct...]
  transfers between devices with their start and end apart: 16 -> 47, of which waited for: 8 -> 17; matrix products, arithmetic and copies ran while one was open for 22% -> 47% of each run, Pallas kernels for 0% -> 5%
where the time goes in v1:
time: 577 us; the launch traced here: 572 us
  waiting for transfers between devices  225 us (39%)
  matrix products  169 us (29%)
  local copies, waits for them, and re-layouts  56.8 us (10%)
  other arithmetic  50.2 us (9%)
  Pallas kernels  31.3 us (5%)
  starting transfers between devices  25.1 us (4%)
  between operations  15.1 us (3%)
    ppermute x39, waiting for transfers between devices, trade(): return lax.ppermute(x, axis, [(i, i ^ bit) for i in range(peers)])  225 us
    dot_general x8, matrix products, contract(): lax.dot_general(a, b, ((dims[:1], dims[1:]), ((), ())), preferred_element...  103 us
    dynamic_update_slice x20, local copies, waits for them, and re-layouts, lay_out(): lax.dynamic_update_slice_in_dim(whole, piece, (place ^ step) * width, dim)  26.6 us
    ppermute x39, starting transfers between devices, trade(): return lax.ppermute(x, axis, [(i, i ^ bit) for i in range(peers)])  24.1 us
    dot_general x2, matrix products, branches(): jnp.dot(hidden[first:last], down_full, preferred_element_type=wide)  22 us
    pallas_call x1, Pallas kernels, attend_back(): pl.pallas_call(partial(attend_back_kernel, scale=1.0 / math.sqrt(HEAD_DIM...  17 us
    dot_general x1, matrix products, on_device_split(): jnp.dot(ffn_in, up_full, preferred_element_type=wide) + up_shift  16.7 us
    dot_general x1, matrix products, on_device_split(): joined = jnp.dot(attn_in, qkv_full, preferred_element_type=wide) + qkv_shift  15.5 us
  transfers between devices with their start and end apart: 47, of which 17 were waited for; matrix products, arithmetic and copies ran while one was open for 47% of the time, Pallas kernels for 5%

profile of v1, /device:TPU:0, one launch (start us, length us, event | category | flops | bytes accessed | tf_op | source)
XLA Modules:
  0.0 572.4 jit_solution(14421910767447487619)
XLA Ops:
  46.3 24.5 %collective-permute-done.16 = bf16[1024,512]{1,0:T(8,128)(2,1)} collective-permute-done((bf16[1024,512]{1,0:T(8,128)(2,1)S(1)}, bf16[1024,512]{1,0:T(8,128)(2,1)}, u32[]{:S(2)}, u32[]{:S(2)}) %collective-permute-start.16) | collective-permute-done | bytes 1048608 | tf_op jit(solution)/shard_map/ppermute | solution.py:321
  84.1 31.9 %collective-permute-done = bf16[1040,512]{1,0:T(8,128)(2,1)} collective-permute-done((bf16[1040,512]{1,0:T(8,128)(2,1)S(1)}, bf16[1040,512]{1,0:T(8,128)(2,1)}, u32[]{:S(2)}, u32[]{:S(2)}) %collective-permute-start) | collective-permute-done | bytes 1064992 | tf_op jit(solution)/shard_map/ppermute | solution.py:321
  129.6 12.7 %collective-permute-done.18 = bf16[1024,512]{1,0:T(8,128)(2,1)S(1)} collective-permute-done((bf16[1024,512]{1,0:T(8,128)(2,1)}, bf16[1024,512]{1,0:T(8,128)(2,1)S(1)}, u32[]{:S(2)}, u32[]{:S(2)}) %collective-permute-start.18) | collective-permute-done | bytes 1048608 | tf_op jit(solution)/shard_map/ppermute | solution.py:321
  147.7 16.8 %collective-permute-done.2 = bf16[1040,512]{1,0:T(8,128)(2,1)S(1)} collective-permute-done((bf16[1040,512]{1,0:T(8,128)(2,1)}, bf16[1040,512]{1,0:T(8,128)(2,1)S(1)}, u32[]{:S(2)}, u32[]{:S(2)}) %collective-permute-start.2) | collective-permute-done | bytes 1064992 | tf_op jit(solution)/shard_map/ppermute | solution.py:321
  166.9 7.1 %convolution_convert_fusion.4.grads = bf16[2048,256]{1,0:T(8,128)(2,1)} fusion(bf16[256,2048]{1,0:T(8,128)(2,1)} %all-gather.7.cloned.1.call-done, bf16[1024,2048]{1,0:T(8,128)(2,1)} %constant_dynamic-update-slice_fusion, bf16[1024,2048]{1,0:T(8,128)(2,1)} %constant_dynamic-update-slice_fusion.4), kind=kOutput, calls=%fused_computation.43 | convolution fusion | flops 2164785152 | bytes 10485760 | tf_op jit(solution)/shard_map/dot_general | solution.py:377
  180.0 5.9 %fusion.14 = f32[2048]{0:T(1024)S(1)} fusion(f32[2048]{0:T(1024)S(1)} %broadcast_multiply_fusion, bf16[1024,2048]{1,0:T(8,128)(2,1)} %constant_dynamic-update-slice_fusion.12, bf16[1024,2048]{1,0:T(8,128)(2,1)} %get-tuple-element.56), kind=kLoop, calls=%fused_computation.16 | loop fusion | flops 29358080 | bytes 8404992 | tf_op jit(solution)/shard_map/reduce_sum | solution.py:618
  186.0 15.5 %broadcast_add_fusion.joined = f32[2048,768]{1,0:T(8,128)} fusion(f32[768]{0:T(1024)S(1)} %dynamic-slice_convert_fusion.5, bf16[2048,768]{1,0:T(8,128)(2,1)} %all-gather.5.cloned.1.call-done, f32[2048]{0:T(1024)S(1)} %bitcast.74, f32[2048]{0:T(1024)S(1)} %bitcast.71, f32[2048]{0:T(1024)S(1)} %add_rsqrt_fusion, f32[2048]{0:T(1024)S(1)} %broadcast_multiply_fusion, ...), kind=kOutput, calls=%fused_computation.37 | convolution fusion | flops 6481772544 | bytes 17861632 | tf_op jit(solution)/shard_map/dot_general | solution.py:623
  201.4 14.3 %attend.1 = (bf16[3,2048,256]{2,1,0:T(8,128)(2,1)}, bf16[2048,256]{1,0:T(8,128)(2,1)}, f32[8,2048]{1,0:T(8,128)}) custom-call(s32[2]{0:T(128)} %pad_add_fusion.scalars, f32[2048,768]{1,0:T(8,128)} %broadcast_add_fusion.joined, f32[2048,128]{1,0:T(8,128)} %get-tuple-element.78.cosine, f32[2048,128]{1,0:T(8,128)} %get-tuple-element.77.sine, s32[8,2048]{1,0:T(8,128)} %stack.84.info), custom_call_target="tpu_custom_call" | custom-call | flops 2415919104 | bytes 12582912 | tf_op jit(solution)/shard_map/attend/pallas_call | solution.py:467
  215.8 7.1 %convolution_convert_fusion.3 = bf16[256,2048]{1,0:T(8,128)(2,1)} fusion(bf16[2048,256]{1,0:T(8,128)(2,1)} %get-tuple-element.19, bf16[1024,2048]{1,0:T(8,128)(2,1)} %constant_dynamic-update-slice_fusion, bf16[1024,2048]{1,0:T(8,128)(2,1)} %constant_dynamic-update-slice_fusion.4), kind=kOutput, calls=%fused_computation.42 | convolution fusion | flops 2164785152 | bytes 10485760 | tf_op jit(solution)/shard_map/dot_general | solution.py:377
  223.4 17.0 %attend_back.1 = (bf16[2048,768]{1,0:T(8,128)(2,1)}, f32[8,768]{1,0:T(8,128)}) custom-call(s32[2]{0:T(128)} %pad_add_fusion.scalars, bf16[3,2048,256]{2,1,0:T(8,128)(2,1)} %get-tuple-element.20.packed, bf16[2048,256]{1,0:T(8,128)(2,1)} %convolution_convert_fusion.4.grads, f32[8,2048]{1,0:T(8,128)} %get-tuple-element.21.log_total, ...), custom_call_target="tpu_custom_call" | custom-call | flops 6039797760 | bytes 8388608 | tf_op jit(solution)/shard_map/attend_back/pallas_call | solution.py:503
  240.3 12.5 %convolution_convert_fusion.2 = bf16[2048,768]{1,0:T(8,128)(2,1)} fusion(bf16[2048,768]{1,0:T(8,128)(2,1)} %get-tuple-element.22, f32[2048]{0:T(1024)S(1)} %bitcast.75, f32[2048]{0:T(1024)S(1)} %bitcast.72, f32[2048]{0:T(1024)S(1)} %add_rsqrt_fusion, f32[2048]{0:T(1024)S(1)} %broadcast_multiply_fusion, ...), kind=kOutput, calls=%fused_computation.36 | convolution fusion | flops 6481772544 | bytes 14712832 | tf_op jit(solution)/shard_map/dot_general | solution.py:377
  252.9 16.7 %multiply_convert_fusion = (bf16[2048,1024]{1,0:T(8,128)(2,1)S(1)}, f32[2048,1024]{1,0:T(8,128)}) fusion(f32[1024]{0:T(1024)S(1)} %dynamic-slice_convert_fusion.4, bf16[2048,1024]{1,0:T(8,128)(2,1)} %all-gather.9.cloned.1.call-done, f32[2048]{0:T(1024)S(1)} %bitcast.69, f32[2048]{0:T(1024)S(1)} %bitcast.66, f32[2048]{0:T(1024)S(1)} %add_rsqrt_fusion, ...), kind=kOutput, calls=%fused_computation.32 | convolution fusion | flops 8640266240 | bytes 25202688 | tf_op jit(solution)/shard_map/dot_general | solution.py:626
  271.6 13.0 %convolution_convert_fusion = bf16[1024,2048]{1,0:T(8,128)(2,1)} fusion(bf16[2048,1024]{1,0:T(8,128)(2,1)S(1)} %get-tuple-element.85, bf16[1024,2048]{1,0:T(8,128)(2,1)} %constant_dynamic-update-slice_fusion, bf16[1024,2048]{1,0:T(8,128)(2,1)} %constant_dynamic-update-slice_fusion.4), kind=kOutput, calls=%fused_computation.34 | convolution fusion | flops 8608808960 | bytes 16777216 | tf_op jit(solution)/shard_map/dot_general | solution.py:377
  284.7 17.3 %convert_reduce_fusion.1 = (f32[1024]{0:T(1024)S(1)}, bf16[2048,1024]{1,0:T(8,128)(2,1)S(1)}) fusion(f32[2048,1024]{1,0:T(8,128)} %get-tuple-element.86, f32[1024]{0:T(1024)S(1)} %dynamic-slice_convert_fusion.4, bf16[1024,2048]{1,0:T(8,128)(2,1)} %all-gather.11.cloned.1.call-done, bf16[1024,2048]{1,0:T(8,128)(2,1)} %constant_dynamic-update-slice_fusion, ...), kind=kOutput, calls=%fused_computation.29 | convolution fusion | flops 8633973760 | bytes 25174016 | tf_op jit(solution)/shard_map/dot_general | solution.py:377
  304.1 11.8 %fusion.53 = f32[2048,2048]{1,0:T(8,128)} fusion(bf16[2048,1024]{1,0:T(8,128)(2,1)S(1)} %get-tuple-element.88, bf16[2048,1024]{1,0:T(8,128)(2,1)S(1)} %copy-done.25), kind=kOutput, calls=%fused_computation.169 | convolution fusion | flops 8589934592 | bytes 25165824 | tf_op jit(solution)/shard_map/dot_general | solution.py:377
  315.9 20.1 %fusion.49 = (f32[2048]{0:T(1024)S(1)}, f32[2048]{0:T(1024)S(1)}, f32[2048]{0:T(1024)S(1)}, f32[2048]{0:T(1024)S(1)}, f32[2048]{0:T(1024)S(1)}, /*index=5*/f32[2048]{0:T(1024)S(1)}, f32[2048,2048]{1,0:T(8,128)S(1)}) fusion(f32[2048]{0:T(1024)S(1)} %add_rsqrt_fusion, f32[2048]{0:T(1024)S(1)} %broadcast_multiply_fusion, ...), kind=kOutput, calls=%fused_computation.165 | convolution fusion | flops 6517936128 | bytes 48316416 | tf_op jit(solution)/shard_map/dot_general | solution.py:377
  339.7 11.4 %fusion.29 = f32[1024,2048]{1,0:T(8,128)S(1)} fusion(bf16[1024,2048]{1,0:T(8,128)(2,1)} %all-gather.11.cloned.1.call-done, bf16[2048,1024]{1,0:T(8,128)(2,1)} %copy-done.27), kind=kOutput, calls=%fused_computation.52 | convolution fusion | flops 4294967296 | bytes 14680064 | tf_op jit(solution)/shard_map/dot_general | solution.py:631
  354.3 14.5 %convolution_convert_fusion.1 = bf16[2048,1024]{1,0:T(8,128)(2,1)} fusion(bf16[2048,1024]{1,0:T(8,128)(2,1)S(1)} %copy-done.29, f32[2048]{0:T(1024)S(1)} %bitcast.70, f32[2048]{0:T(1024)S(1)} %bitcast.68, f32[2048]{0:T(1024)S(1)} %add_rsqrt_fusion, f32[2048]{0:T(1024)S(1)} %broadcast_multiply_fusion, ...), kind=kOutput, calls=%fused_computation.35 | convolution fusion | flops 8629780480 | bytes 16809984 | tf_op jit(solution)/shard_map/dot_general | solution.py:377
  368.8 10.6 %fusion.31 = f32[1024,2048]{1,0:T(8,128)} fusion(bf16[1024,2048]{1,0:T(8,128)(2,1)} %all-gather.11.cloned.1.call-done, bf16[2048,1024]{1,0:T(8,128)(2,1)} %copy-done.27), kind=kOutput, calls=%fused_computation.54 | convolution fusion | flops 4294967296 | bytes 14680064 | tf_op jit(solution)/shard_map/dot_general | solution.py:631
  379.4 6.1 %slice_add_fusion = f32[1024,2048]{1,0:T(8,128)S(1)} fusion(f32[2048,2048]{1,0:T(8,128)} %copy-done.4, bf16[1024,2048]{1,0:T(8,128)(2,1)} %collective-permute-done.23), kind=kLoop, calls=%fused_computation.26 | loop fusion | flops 4194304 | bytes 20971520 | tf_op jit(solution)/shard_map/add | solution.py:681
  387.1 8.1 %convert_add_fusion = f32[1024,2048]{1,0:T(8,128)S(1)} fusion(bf16[1024,2048]{1,0:T(8,128)(2,1)} %collective-permute-done.12, f32[1024,2048]{1,0:T(8,128)} %fusion.31, bf16[256,2048]{1,0:T(8,128)(2,1)S(1)} %copy-done.5, bf16[2048,256]{1,0:T(8,128)(2,1)S(1)} %copy-done.8), kind=kOutput, calls=%fused_computation.30 | convolution fusion | flops 1080033280 | bytes 22544384 | tf_op jit(solution)/shard_map/dot_general | solution.py:631
  401.2 11.9 %collective-permute-done.25 = bf16[1024,512]{1,0:T(8,128)(2,1)S(1)} collective-permute-done((bf16[1024,512]{1,0:T(8,128)(2,1)S(1)}, bf16[1024,512]{1,0:T(8,128)(2,1)S(1)}, u32[]{:S(2)}, u32[]{:S(2)}) %collective-permute-start.25) | collective-permute-done | bytes 1048608 | tf_op jit(solution)/shard_map/ppermute | solution.py:321
  416.0 42.0 %collective-permute-done.14 = bf16[1024,512]{1,0:T(8,128)(2,1)S(1)} collective-permute-done((bf16[1024,512]{1,0:T(8,128)(2,1)S(1)}, bf16[1024,512]{1,0:T(8,128)(2,1)S(1)}, u32[]{:S(2)}, u32[]{:S(2)}) %collective-permute-start.14) | collective-permute-done | bytes 1048608 | tf_op jit(solution)/shard_map/ppermute | solution.py:321
  462.4 67.8 %collective-permute-done.29 = f32[2,1024]{1,0:T(2,128)S(1)} collective-permute-done((f32[2,1024]{1,0:T(2,128)S(1)}, f32[2,1024]{1,0:T(2,128)S(1)}, u32[]{:S(2)}, u32[]{:S(2)}) %collective-permute-start.29) | collective-permute-done | bytes 8224 | tf_op jit(solution)/shard_map/ppermute | solution.py:321
  (263 shorter events, 140.8 us)
Async XLA Ops:
  7.2 159.7 %all-gather.7.cloned.1.call-start = ((), (), s32[]{:S(2)}) async-start(), calls=%async_computation.5 | async-start | bytes 1310720 | tf_op jit(solution)/shard_map/all_gather | solution.py:598
  11.4 174.5 %all-gather.5.cloned.1.call-start = ((), (), s32[]{:S(2)}) async-start(), calls=%async_computation.4 | async-start | bytes 3932160 | tf_op jit(solution)/shard_map/all_gather | solution.py:598
  16.5 236.4 %all-gather.9.cloned.1.call-start = ((), (), s32[]{:S(2)}) async-start(), calls=%async_computation.6 | async-start | bytes 5242880 | tf_op jit(solution)/shard_map/all_gather | solution.py:598
  22.0 262.7 %all-gather.11.cloned.1.call-start = ((), (), s32[]{:S(2)}) async-start(), calls=%async_computation.7 | async-start | bytes 5242880 | tf_op jit(solution)/shard_map/all_gather | solution.py:598
  22.1 48.8 %collective-permute-start.16 = (bf16[1024,512]{1,0:T(8,128)(2,1)S(1)}, bf16[1024,512]{1,0:T(8,128)(2,1)}, u32[]{:S(2)}, u32[]{:S(2)}) collective-permute-start(bf16[1024,512]{1,0:T(8,128)(2,1)S(1)} %copy-done.6), channel_id=1, source_target_pairs={{0,1},{1,0},{2,3},{3,2},{4,5},{5,4},{6,7},{7,6},{8,9},{9,8},{10,11... | collective-permute-start | bytes 3145736 | tf_op jit(solution)/shard_map/ppermute | solution.py:321
  25.1 47.1 %collective-permute-start.19 = (bf16[1024,512]{1,0:T(8,128)(2,1)S(1)}, bf16[1024,512]{1,0:T(8,128)(2,1)}, u32[]{:S(2)}, u32[]{:S(2)}) collective-permute-start(bf16[1024,512]{1,0:T(8,128)(2,1)S(1)} %copy-done.6), channel_id=1, source_target_pairs={{0,4},{4,0},{1,5},{5,1},{2,6},{6,2},{3,7},{7,3},{8,12},{12,8},{9,1... | collective-permute-start | bytes 3145736 | tf_op jit(solution)/shard_map/ppermute | solution.py:321
  25.1 49.6 %collective-permute-start.17 = (bf16[1024,512]{1,0:T(8,128)(2,1)S(1)}, bf16[1024,512]{1,0:T(8,128)(2,1)}, u32[]{:S(2)}, u32[]{:S(2)}) collective-permute-start(bf16[1024,512]{1,0:T(8,128)(2,1)S(1)} %copy-done.6), channel_id=1, source_target_pairs={{0,2},{1,3},{2,0},{3,1},{4,6},{5,7},{6,4},{7,5},{8,10},{9,11},{10,... | collective-permute-start | bytes 3145736 | tf_op jit(solution)/shard_map/ppermute | solution.py:321
  38.8 77.2 %collective-permute-start = (bf16[1040,512]{1,0:T(8,128)(2,1)S(1)}, bf16[1040,512]{1,0:T(8,128)(2,1)}, u32[]{:S(2)}, u32[]{:S(2)}) collective-permute-start(bf16[1040,512]{1,0:T(8,128)(2,1)S(1)} %concatenate.51), channel_id=1, source_target_pairs={{0,1},{1,0},{2,3},{3,2},{4,5},{5,4},{6,7},{7,6},{8,9},{9,8},{10,11... | collective-permute-start | bytes 3194888 | tf_op jit(solution)/shard_map/ppermute | solution.py:321
  44.7 75.2 %collective-permute-start.1 = (bf16[1040,512]{1,0:T(8,128)(2,1)S(1)}, bf16[1040,512]{1,0:T(8,128)(2,1)}, u32[]{:S(2)}, u32[]{:S(2)}) collective-permute-start(bf16[1040,512]{1,0:T(8,128)(2,1)S(1)} %concatenate.51), channel_id=1, source_target_pairs={{0,2},{1,3},{2,0},{3,1},{4,6},{5,7},{6,4},{7,5},{8,10},{9,11},{10,... | collective-permute-start | bytes 3194888 | tf_op jit(solution)/shard_map/ppermute | solution.py:321
  70.8 51.5 %collective-permute-start.3 = (bf16[1024,512]{1,0:T(8,128)(2,1)S(1)}, bf16[1024,512]{1,0:T(8,128)(2,1)}, u32[]{:S(2)}, u32[]{:S(2)}) collective-permute-start(bf16[1024,512]{1,0:T(8,128)(2,1)S(1)} %copy-done.2), channel_id=1, source_target_pairs={{0,4},{4,0},{1,5},{5,1},{2,6},{6,2},{3,7},{7,3},{8,12},{12,8},{9,1... | collective-permute-start | bytes 3145736 | tf_op jit(solution)/shard_map/ppermute | solution.py:321
  71.9 458.3 %reduce-scatter.7.cloned.1.call-start = ((), (), s32[]{:S(2)}) async-start(), calls=%async_computation.9 | async-start | bytes 1310720 | tf_op jit(solution)/shard_map/reduce_scatter | solution.py:649
  72.1 55.6 %collective-permute-start.20 = (bf16[1024,512]{1,0:T(8,128)(2,1)}, bf16[1024,512]{1,0:T(8,128)(2,1)S(1)}, u32[]{:S(2)}, u32[]{:S(2)}) collective-permute-start(bf16[1024,512]{1,0:T(8,128)(2,1)} %collective-permute-done.16), channel_id=1, source_target_pairs={{0,4},{4,0},{1,5},{5,1},{2,6},{6,2},{3,7},{7,3},{8,12},{12,8},{9,1... | collective-permute-start | bytes 3145736 | tf_op jit(solution)/shard_map/ppermute | solution.py:321
  74.6 68.8 %collective-permute-start.21 = (bf16[1024,512]{1,0:T(8,128)(2,1)}, bf16[1024,512]{1,0:T(8,128)(2,1)S(1)}, u32[]{:S(2)}, u32[]{:S(2)}) collective-permute-start(bf16[1024,512]{1,0:T(8,128)(2,1)} %collective-permute-done.17), channel_id=1, source_target_pairs={{0,4},{4,0},{1,5},{5,1},{2,6},{6,2},{3,7},{7,3},{8,12},{12,8},{9,1... | collective-permute-start | bytes 3145736 | tf_op jit(solution)/shard_map/ppermute | solution.py:321
  222.9 318.1 %reduce-scatter.5.cloned.1.call-start = ((), (), s32[]{:S(2)}) async-start(), calls=%async_computation.8 | async-start | bytes 3932160 | tf_op jit(solution)/shard_map/reduce_scatter | solution.py:649
  252.8 301.9 %reduce-scatter.11.cloned.1.call-start = ((), (), s32[]{:S(2)}) async-start(), calls=%async_computation.11 | async-start | bytes 5242880 | tf_op jit(solution)/shard_map/reduce_scatter | solution.py:649
  284.6 274.3 %reduce-scatter.9.cloned.1.call-start = ((), (), s32[]{:S(2)}) async-start(), calls=%async_computation.10 | async-start | bytes 5242880 | tf_op jit(solution)/shard_map/reduce_scatter | solution.py:649
  339.0 40.4 %collective-permute-start.23 = (bf16[1024,2048]{1,0:T(8,128)(2,1)}, bf16[1024,2048]{1,0:T(8,128)(2,1)}, u32[]{:S(2)}, u32[]{:S(2)}) collective-permute-start(bf16[1024,2048]{1,0:T(8,128)(2,1)} %slice.221), channel_id=1, source_target_pairs={{0,4},{4,0},{1,5},{5,1},{2,6},{6,2},{3,7},{7,3},{8,12},{12,8},{9,1... | collective-permute-start | bytes 12582920 | tf_op jit(solution)/shard_map/ppermute | solution.py:321
  395.6 62.4 %collective-permute-start.14 = (bf16[1024,512]{1,0:T(8,128)(2,1)S(1)}, bf16[1024,512]{1,0:T(8,128)(2,1)S(1)}, u32[]{:S(2)}, u32[]{:S(2)}) collective-permute-start(bf16[1024,512]{1,0:T(8,128)(2,1)S(1)} %get-tuple-element.43), channel_id=1, source_target_pairs={{0,1},{1,0},{2,3},{3,2},{4,5},{5,4},{6,7},{7,6},{8,9},{9,8},{10,11... | collective-permute-start | bytes 3145736 | tf_op jit(solution)/shard_map/ppermute | solution.py:321
  397.6 62.9 %collective-permute-start.28 = (f32[2,1024]{1,0:T(2,128)S(1)}, f32[2,1024]{1,0:T(2,128)S(1)}, u32[]{:S(2)}, u32[]{:S(2)}) collective-permute-start(f32[2,1024]{1,0:T(2,128)S(1)} %fusion.38), channel_id=1, source_target_pairs={{0,1},{1,0},{2,3},{3,2},{4,5},{5,4},{6,7},{7,6},{8,9},{9,8},{10,11... | collective-permute-start | bytes 24584 | tf_op jit(solution)/shard_map/ppermute | solution.py:321
  399.1 135.3 %collective-permute-start.24 = (bf16[1024,512]{1,0:T(8,128)(2,1)}, bf16[1024,512]{1,0:T(8,128)(2,1)}, u32[]{:S(2)}, u32[]{:S(2)}) collective-permute-start(bf16[1024,512]{1,0:T(8,128)(2,1)} %get-tuple-element.40), channel_id=1, source_target_pairs={{0,1},{1,0},{2,3},{3,2},{4,5},{5,4},{6,7},{7,6},{8,9},{9,8},{10,11... | collective-permute-start | bytes 3145736 | tf_op jit(solution)/shard_map/ppermute | solution.py:321
  399.7 134.7 %collective-permute-start.13 = (bf16[1024,512]{1,0:T(8,128)(2,1)S(1)}, bf16[1024,512]{1,0:T(8,128)(2,1)}, u32[]{:S(2)}, u32[]{:S(2)}) collective-permute-start(bf16[1024,512]{1,0:T(8,128)(2,1)S(1)} %get-tuple-element.42), channel_id=1, source_target_pairs={{0,1},{1,0},{2,3},{3,2},{4,5},{5,4},{6,7},{7,6},{8,9},{9,8},{10,11... | collective-permute-start | bytes 3145736 | tf_op jit(solution)/shard_map/ppermute | solution.py:321
  414.4 120.0 %collective-permute-start.26 = (bf16[1024,512]{1,0:T(8,128)(2,1)}, bf16[1024,512]{1,0:T(8,128)(2,1)}, u32[]{:S(2)}, u32[]{:S(2)}) collective-permute-start(bf16[1024,512]{1,0:T(8,128)(2,1)} %add_convert_fusion.1), channel_id=1, source_target_pairs={{0,2},{1,3},{2,0},{3,1},{4,6},{5,7},{6,4},{7,5},{8,10},{9,11},{10,... | collective-permute-start | bytes 3145736 | tf_op jit(solution)/shard_map/ppermute | solution.py:321
  459.4 75.0 %collective-permute-start.15 = (bf16[1024,512]{1,0:T(8,128)(2,1)}, bf16[1024,512]{1,0:T(8,128)(2,1)}, u32[]{:S(2)}, u32[]{:S(2)}) collective-permute-start(bf16[1024,512]{1,0:T(8,128)(2,1)} %add_convert_fusion.2), channel_id=1, source_target_pairs={{0,2},{1,3},{2,0},{3,1},{4,6},{5,7},{6,4},{7,5},{8,10},{9,11},{10,... | collective-permute-start | bytes 3145736 | tf_op jit(solution)/shard_map/ppermute | solution.py:321
  460.5 69.7 %collective-permute-start.29 = (f32[2,1024]{1,0:T(2,128)S(1)}, f32[2,1024]{1,0:T(2,128)S(1)}, u32[]{:S(2)}, u32[]{:S(2)}) collective-permute-start(f32[2,1024]{1,0:T(2,128)S(1)} %fusion.70), channel_id=1, source_target_pairs={{0,2},{1,3},{2,0},{3,1},{4,6},{5,7},{6,4},{7,5},{8,10},{9,11},{10,... | collective-permute-start | bytes 24584 | tf_op jit(solution)/shard_map/ppermute | solution.py:321
  (55 other events, 1549.1 us)
Sparse Core Ops, SparseCore 0:
  11.6 29.1 all-gather.6
  43.1 43.9 all-gather.4
  89.6 52.6 all-gather.8
  144.6 52.5 all-gather.10
  223.0 28.4 reduce-scatter.6
  254.7 43.9 reduce-scatter.4
  301.9 52.6 reduce-scatter.10
  368.9 53.4 reduce-scatter.8

commit v2 on v0

--- a/solution.py
+++ b/solution.py
@@ -4,6 +4,8 @@
 import jax
 import jax.numpy as jnp
 from jax import lax
+from jax.experimental import pallas as pl
+from jax.experimental.pallas import tpu as pltpu
 from jax.sharding import PartitionSpec as P
 
 HEAD_DIM = 256
@@ -309,6 +311,842 @@
     )
 
 
+low = jnp.bfloat16
+wide = jnp.float32
+tile = 256
+megabyte = 1024 * 1024
+pace = 16
+
+
+def trade(x, axis, bit):
+    peers = lax.axis_size(axis)
+    return lax.ppermute(x, axis, [(i, i ^ bit) for i in range(peers)])
+
+
+def after(x, *earlier):
+    return lax.optimization_barrier((x, *earlier))[0]
+
+
+def meet(*values):
+    return lax.optimization_barrier(values)
+
+
+def block_of(x, index, dim, blocks):
+    width = x.shape[dim] // blocks
+    return lax.dynamic_slice_in_dim(x, index * width, width, dim)
+
+
+def lay_out(pieces, place, dim):
+    width = pieces[0].shape[dim]
+    shape = list(pieces[0].shape)
+    shape[dim] = width * 4
+    whole = jnp.zeros(shape, pieces[0].dtype)
+    for step, piece in enumerate(pieces):
+        whole = lax.dynamic_update_slice_in_dim(whole, piece, (place ^ step) * width, dim)
+    return whole
+
+
+def plane_corner(near, far, axis):
+    half = near.shape[0] // 2
+    corner = [trade(far[:half], axis, 1), trade(near[half:], axis, 2)]
+    return jnp.concatenate(corner, axis=0)
+
+
+def scatter_plane(total, axis, dim):
+    place = lax.axis_index(axis)
+    own, near, far, corner = (block_of(total, place ^ k, dim, 4) for k in range(4))
+    half = own.shape[0] // 2
+    upper = trade(corner[:half].astype(low), axis, 1)
+    lower = trade(corner[half:].astype(low), axis, 2)
+    add = lambda a, b: (a.astype(wide) + b.astype(wide)).astype(low)
+    far = jnp.concatenate([add(far[:half], upper), far[half:].astype(low)], axis=0)
+    near = jnp.concatenate([near[:half].astype(low), add(near[half:], lower)], axis=0)
+    far_in = trade(far, axis, 2)
+    near_in = trade(near, axis, 1)
+    return (own.astype(wide) + near_in.astype(wide) + far_in.astype(wide)).astype(low), (far, near)
+
+
+def half_of(x, index, dim):
+    return block_of(x, index, dim, 2)
+
+
+def join_cores(mine, theirs, core, dim):
+    first = jnp.where(core == 0, mine, theirs)
+    second = jnp.where(core == 0, theirs, mine)
+    return jnp.concatenate([first, second], axis=dim)
+
+
+def contract(a, b, dims):
+    return lax.dot_general(a, b, ((dims[:1], dims[1:]), ((), ())), preferred_element_type=wide)
+
+
+def place_of(index, size):
+    return pl.ds(pl.multiple_of(index * size, size), size)
+
+
+def fold_rows(x):
+    return jnp.sum(x.reshape(x.shape[0] // 8, 8, x.shape[1]), axis=0)
+
+
+def fixed(shape):
+    return pl.BlockSpec(
+        shape, lambda step, scalars: (0,) * len(shape), pipeline_mode=pl.Buffered(1)
+    )
+
+
+def kept(shape):
+    return pl.BlockSpec(shape, lambda step, scalars: (0,) * len(shape))
+
+
+def by_row(width):
+    return pl.BlockSpec((tile, width), lambda step, scalars: (step, 0))
+
+
+def by_column(rows, width, first=0):
+    return pl.BlockSpec((rows, width), lambda step, scalars: (0, jnp.maximum(step - first, 0)))
+
+
+def call(kernel, name, steps, in_specs, out_specs, out_shape, operands, flops, moved, scratch=(), exps=0):
+    return pl.pallas_call(
+        kernel,
+        grid_spec=pltpu.PrefetchScalarGridSpec(
+            num_scalar_prefetch=1,
+            grid=(steps,),
+            in_specs=in_specs,
+            out_specs=out_specs,
+            scratch_shapes=list(scratch),
+        ),
+        out_shape=out_shape,
+        compiler_params=pltpu.CompilerParams(vmem_limit_bytes=56 * megabyte),
+        cost_estimate=pl.CostEstimate(
+            flops=flops * pace, bytes_accessed=moved * pace, transcendentals=exps * pace
+        ),
+        name=name,
+    )(*operands)
+
+
+def shaped(*shape, kind=low):
+    return jax.ShapeDtypeStruct(shape, kind)
+
+
+def own_first(piece, core):
+    return piece[:, place_of(core, tile)], piece[:, place_of(1 - core, tile)]
+
+
+def norm_kernel(scalars, *refs):
+    pieces, terms = refs[:4], refs[4:8]
+    attn_out, ffn_out, stats_out, terms_out = refs[8:]
+    width = 8 * tile
+    parts = [piece[...].astype(wide) for piece in pieces]
+    total = sum(jnp.sum(part, axis=1, keepdims=True) for part in parts)
+    mean = total * (1.0 / width)
+    spread = sum(jnp.sum((part - mean) * (part - mean), axis=1, keepdims=True) for part in parts)
+    inverse = lax.rsqrt(spread * (1.0 / width) + norm_epsilon)
+    for k in range(4):
+        block = scalars[2] ^ k
+        for half in range(2):
+            side = scalars[0] if half == 0 else 1 - scalars[0]
+            source = place_of(side, tile)
+            columns = place_of(4 * half + block, tile)
+            normed = (pieces[k][:, source].astype(wide) - mean) * inverse
+            term = terms[k][:, source].astype(wide)
+            attn_out[:, columns] = (normed * term[0:1] + term[1:2]).astype(low)
+            ffn_out[:, columns] = (normed * term[2:3] + term[3:4]).astype(low)
+    lane = lax.broadcasted_iota(jnp.int32, stats_out.shape, 1)
+    stats_out[...] = jnp.where(lane < 64, mean, inverse)
+
+    @pl.when(pl.program_id(0) == 0)
+    def _():
+        for k in range(4):
+            for half in range(2):
+                side = scalars[0] if half == 0 else 1 - scalars[0]
+                columns = place_of(4 * half + (scalars[2] ^ k), tile)
+                terms_out[:, columns] = terms[k][0:8, place_of(side, tile)].astype(wide)
+
+
+def norm(scalars, pieces, terms):
+    rows, width = pieces[0].shape
+    term = fixed(terms[0].shape)
+    return call(
+        norm_kernel,
+        "norm",
+        rows // tile,
+        [by_row(width)] * 4 + [term] * 4,
+        [by_row(4 * width), by_row(4 * width), by_row(128), kept((8, 4 * width))],
+        [
+            shaped(rows, 4 * width),
+            shaped(rows, 4 * width),
+            shaped(rows, 128, kind=wide),
+            shaped(8, 4 * width, kind=wide),
+        ],
+        (scalars, *pieces, *terms),
+        rows * width * 40,
+        rows * width * 24,
+    )
+
+
+def assemble_kernel(scalars, own, near, far, upper, lower, first_out, second_out):
+    step = pl.program_id(0)
+    split = first_out.shape[1]
+    middle = upper.shape[0]
+
+    def write(piece, rows):
+        first_out[rows, :] = piece[:, :split]
+        second_out[rows, :] = piece[:, split:]
+
+    for k, piece in enumerate((own, near, far)):
+        pl.when(step == k)(partial(write, piece, slice(None)))
+
+    @pl.when(step == 3)
+    def _():
+        write(upper, slice(0, middle))
+        write(lower, slice(middle, 2 * middle))
+
+
+def assemble(scalars, pieces, halves, split):
+    rows, columns = pieces[0].shape
+    place = lambda step, scalars: (scalars[3] ^ step, 0)
+    return call(
+        assemble_kernel,
+        "assemble",
+        4,
+        [fixed((rows, columns))] * 3 + [fixed((rows // 2, columns))] * 2,
+        [pl.BlockSpec((rows, split), place), pl.BlockSpec((rows, columns - split), place)],
+        [shaped(4 * rows, split), shaped(4 * rows, columns - split)],
+        (scalars, *pieces, *halves),
+        rows * columns,
+        rows * columns * 16,
+    )
+
+
+def double(rows_in, own, other):
+    half = rows_in.shape[1] // 2
+    return contract(rows_in[:, :half], own, (1, 0)) + contract(rows_in[:, half:], other, (1, 0))
+
+
+def heads_kernel(scalars, rows_in, own, other, shift_row, cosine, sine, mine, theirs):
+    step = pl.program_id(0)
+    joined = double(rows_in, own[...], other[...]) + shift_row[0:1, :]
+    part = lax.rem(step, 3)
+
+    def write(vectors):
+        @pl.when(step < 3)
+        def _():
+            theirs[0] = vectors.astype(low)
+
+        @pl.when(step >= 3)
+        def _():
+            mine[0] = vectors.astype(low)
+
+    @pl.when(part < 2)
+    def _():
+        write(turn(joined, cosine[...], sine[...], 1.0))
+
+    @pl.when(part == 2)
+    def _():
+        write(joined)
+
+
+def heads(scalars, attn_in, weights, shift_row, cosine, sine):
+    rows, width = attn_in.shape
+
+    def column(step, scalars):
+        return jnp.where(step < 3, 1 - scalars[0], scalars[0]) * 3 + lax.rem(step, 3)
+
+    weight = pl.BlockSpec((width // 2, HEAD_DIM), lambda step, scalars: (0, column(step, scalars)))
+    shift = pl.BlockSpec((1, HEAD_DIM), lambda step, scalars: (0, column(step, scalars)))
+    last = lambda step, scalars: (jnp.maximum(step - 3, 0), 0, 0)
+    early = lambda step, scalars: (jnp.minimum(step, 2), 0, 0)
+    return call(
+        heads_kernel,
+        "heads",
+        6,
+        [fixed(attn_in.shape), weight, weight, shift, fixed((rows, 128)), fixed((rows, 128))],
+        [pl.BlockSpec((1, rows, HEAD_DIM), last), pl.BlockSpec((1, rows, HEAD_DIM), early)],
+        [shaped(3, rows, HEAD_DIM)] * 2,
+        (scalars, attn_in, *weights, shift_row, cosine, sine),
+        12 * rows * width * HEAD_DIM,
+        2 * (rows * width + 6 * width * HEAD_DIM + 6 * rows * HEAD_DIM),
+    )
+
+
+def expand_kernel(scalars, rows_in, own, other, shift_row, hidden, slope):
+    pre = double(rows_in, own[...], other[...]) + shift_row[0:1, :]
+    phi = 0.5 + 0.5 * lax.erf(pre * math.sqrt(0.5))
+    density = jnp.exp(pre * pre * -0.5) * (1.0 / math.sqrt(2.0 * math.pi))
+    hidden[...] = (pre * phi).astype(low)
+    slope[...] = (phi + pre * density).astype(low)
+
+
+def expand(scalars, ffn_in, weights, shift_row):
+    rows, width = ffn_in.shape
+    columns = weights[0].shape[1]
+    return call(
+        expand_kernel,
+        "expand",
+        columns // tile,
+        [fixed(ffn_in.shape)] + [by_column(width // 2, tile)] * 2 + [by_column(1, tile)],
+        [by_column(rows, tile)] * 2,
+        [shaped(rows, columns), shaped(rows, columns)],
+        (scalars, ffn_in, *weights, shift_row),
+        2 * rows * width * columns,
+        2 * (rows * width + width * columns + 2 * rows * columns),
+        exps=2 * rows * columns,
+    )
+
+
+def project_kernel(scalars, mine, theirs, hidden, dense_own, dense_other, down_own, down_other, out):
+    for half, dense, down in ((0, dense_own, down_own), (1, dense_other, down_other)):
+        total = contract(hidden[...], down[...], (1, 0))
+        total += contract(mine[...], dense[place_of(scalars[0], HEAD_DIM), :], (1, 0))
+        total += contract(theirs[...], dense[place_of(1 - scalars[0], HEAD_DIM), :], (1, 0))
+        out[:, half * tile : (half + 1) * tile] = total.astype(out.dtype)
+
+
+def project(scalars, mine, theirs, hidden, dense, down):
+    rows = hidden.shape[0]
+    depth = dense[0].shape[0] + down[0].shape[0]
+    weight = lambda x: by_column(x.shape[0], tile)
+    return call(
+        project_kernel,
+        "project",
+        4,
+        [fixed(mine.shape), fixed(mine.shape), fixed(hidden.shape)]
+        + [weight(x) for x in (*dense, *down)],
+        [by_column(rows, 2 * tile)],
+        [shaped(rows, 8 * tile)],
+        (scalars, mine, theirs, hidden, *dense, *down),
+        16 * rows * tile * depth,
+        2 * (rows * 8 * tile + depth * 8 * tile + rows * depth),
+    )[0]
+
+
+def hidden_back_kernel(scalars, *refs):
+    pieces, (slope, dense_own, dense_other, down_own, down_other) = refs[:4], refs[4:9]
+    cotangent, pre_grad, mine, theirs, bias_grad = refs[9:]
+    step = pl.program_id(0)
+    half = cotangent.shape[1] // 2
+
+    @pl.when(step == 0)
+    def _():
+        for k in range(4):
+            block = scalars[2] ^ k
+            own, other = own_first(pieces[k], scalars[0])
+            cotangent[:, place_of(block, tile)] = own
+            cotangent[:, place_of(4 + block, tile)] = other
+
+    def back(own, other):
+        return contract(cotangent[:, :half], own[...], (1, 1)) + contract(
+            cotangent[:, half:], other[...], (1, 1)
+        )
+
+    @pl.when(step == 0)
+    def _():
+        theirs[...] = back(dense_own, dense_other).astype(low)
+
+    @pl.when(step == 1)
+    def _():
+        mine[...] = back(dense_own, dense_other).astype(low)
+
+    @pl.when(step >= 2)
+    def _():
+        grad = (back(down_own, down_other) * slope[...].astype(wide)).astype(low)
+        pre_grad[...] = grad
+        bias_grad[...] = fold_rows(grad.astype(wide))
+
+
+def hidden_back(scalars, pieces, slope, dense, down):
+    rows, width = pieces[0].shape
+    hidden = down[0].shape[0]
+    heads_weight = pl.BlockSpec(
+        (HEAD_DIM, 2 * width),
+        lambda step, scalars: (jnp.where(step == 0, 1 - scalars[0], scalars[0]), 0),
+    )
+    weight = pl.BlockSpec(
+        (tile, 2 * width), lambda step, scalars: (jnp.maximum(step - 2, 0), 0)
+    )
+    return call(
+        hidden_back_kernel,
+        "hidden_back",
+        2 + hidden // tile,
+        [fixed((rows, width))] * 4
+        + [by_column(rows, tile, 2), heads_weight, heads_weight, weight, weight],
+        [
+            kept((rows, 4 * width)),
+            by_column(rows, tile, 2),
+            kept((rows, HEAD_DIM)),
+            kept((rows, HEAD_DIM)),
+            by_column(8, tile, 2),
+        ],
+        [
+            shaped(rows, 4 * width),
+            shaped(rows, hidden),
+            shaped(rows, HEAD_DIM),
+            shaped(rows, HEAD_DIM),
+            shaped(8, hidden, kind=wide),
+        ],
+        (scalars, *pieces, slope, *dense, *down),
+        8 * rows * width * (2 * HEAD_DIM + hidden),
+        rows * width * 16 + 8 * width * hidden + rows * hidden * 4,
+    )
+
+
+def mix_kernel(
+    scalars, mine, theirs, pre_grad, qkv_own, qkv_other, up_own, up_other, terms_own, terms_other,
+    stats, first_piece, second_piece, first_out, second_out, sums_own, sums_other, row_sums
+):
+    mean = stats[:, 0:1]
+    inverse = stats[:, 64:65]
+    step = pl.program_id(0)
+
+    def run(piece, out):
+        plain = None
+        for half, qkv, up, terms, sums in (
+            (0, qkv_own, up_own, terms_own, sums_own),
+            (1, qkv_other, up_other, terms_other, sums_other),
+        ):
+            attn = contract(mine[...], qkv[:, place_of(scalars[0], 3 * HEAD_DIM)], (1, 1))
+            attn += contract(theirs[...], qkv[:, place_of(1 - scalars[0], 3 * HEAD_DIM)], (1, 1))
+            ffn = contract(pre_grad[...], up[...], (1, 1))
+            side = scalars[0] if half == 0 else 1 - scalars[0]
+            normed = (piece[:, place_of(side, tile)].astype(wide) - mean) * inverse
+            mixed = attn * terms[0:1, :] + ffn * terms[2:3, :]
+            sums[0:8, :] = fold_rows(attn * normed)
+            sums[8:16, :] = fold_rows(attn)
+            sums[16:24, :] = fold_rows(ffn * normed)
+            sums[24:32, :] = fold_rows(ffn)
+            out[:, half * tile : (half + 1) * tile] = mixed.astype(out.dtype)
+            weighed = mixed * normed
+            here = mixed[:, :128] + mixed[:, 128:], weighed[:, :128] + weighed[:, 128:]
+            plain = here if plain is None else (plain[0] + here[0], plain[1] + here[1])
+        lane = lax.broadcasted_iota(jnp.int32, row_sums.shape, 1)
+        together = jnp.where(
+            lane < 64,
+            jnp.sum(plain[0], axis=1, keepdims=True),
+            jnp.sum(plain[1], axis=1, keepdims=True),
+        )
+        return together
+
+    @pl.when(step == 0)
+    def _():
+        row_sums[...] = run(first_piece, first_out)
+
+    @pl.when(step == 1)
+    def _():
+        row_sums[...] += run(second_piece, second_out)
+
+
+def mix(scalars, mine, theirs, pre_grad, qkv, up, terms, stats, pieces, order, kinds):
+    rows = pre_grad.shape[0]
+    width = pieces[0].shape[1]
+    depth = qkv[0].shape[1] + up[0].shape[1]
+
+    def block(step, scalars):
+        return scalars[2] ^ jnp.where(step == 0, order[0], order[1])
+
+    weight = lambda x: pl.BlockSpec((tile, x.shape[1]), lambda step, scalars: (block(step, scalars), 0))
+    term = lambda first: pl.BlockSpec((8, tile), lambda step, scalars: (0, first + block(step, scalars)))
+    sums = pl.BlockSpec((32, tile), lambda step, scalars: (0, step))
+    return call(
+        mix_kernel,
+        "mix",
+        2,
+        [fixed(mine.shape), fixed(mine.shape), fixed(pre_grad.shape)]
+        + [weight(x) for x in (*qkv, *up)]
+        + [term(0), term(4), fixed((rows, 128))]
+        + [fixed((rows, width))] * 2,
+        [kept((rows, width))] * 2 + [sums, sums, kept((rows, 128))],
+        [shaped(rows, width, kind=kind) for kind in kinds]
+        + [shaped(32, 2 * tile, kind=wide)] * 2
+        + [shaped(rows, 128, kind=wide)],
+        (scalars, mine, theirs, pre_grad, *qkv, *up, terms, terms, stats, pieces[order[0]], pieces[order[1]]),
+        4 * rows * width * depth,
+        2 * (4 * rows * width + 2 * depth * width + rows * depth),
+    )
+
+
+def attend_kernel(scalars, mine, theirs, info, packed, own_out, twin_out, log_total, natural, scale):
+    rows = natural.shape[0]
+    blocks = rows // tile
+    own = place_of(scalars[0], rows // 2)
+    twin = place_of(1 - scalars[0], rows // 2)
+    for part in range(3):
+        packed[part, own, :] = mine[part]
+        packed[part, twin, :] = theirs[part]
+    for block in range(blocks):
+        span = (block + 1) * tile
+        query = packed[0, block * tile : span, :]
+        about = info[:, block * tile : span]
+        scores = scores_of(packed[1, :span, :], query, about, scalars[1], block * tile, scale)
+        top = jnp.max(scores, axis=0, keepdims=True)
+        powers = jnp.exp(scores - top)
+        total = jnp.sum(powers, axis=0, keepdims=True)
+        probs = (powers * (1.0 / total)).astype(low)
+        natural[block * tile : span, :] = contract(probs, packed[2, :span, :], (0, 0)).astype(low)
+        log_total[0:1, block * tile : span] = top + jnp.log(total)
+    own_out[...] = natural[own, :]
+    twin_out[...] = natural[twin, :]
+
+
+def attend(scalars, mine, theirs, info):
+    held = mine.shape[1]
+    rows = 2 * held
+    pairs = rows * (rows + tile) // 2
+    return call(
+        partial(attend_kernel, scale=1.0 / math.sqrt(HEAD_DIM)),
+        "attend",
+        1,
+        [fixed(mine.shape), fixed(mine.shape), fixed((8, rows))],
+        [kept((3, rows, HEAD_DIM)), kept((held, HEAD_DIM)), kept((held, HEAD_DIM)), kept((8, rows))],
+        [
+            shaped(3, rows, HEAD_DIM),
+            shaped(held, HEAD_DIM),
+            shaped(held, HEAD_DIM),
+            shaped(8, rows, kind=wide),
+        ],
+        (scalars, mine, theirs, info),
+        pairs * HEAD_DIM * 4,
+        rows * HEAD_DIM * 16,
+        scratch=[pltpu.VMEM((rows, HEAD_DIM), low)],
+        exps=pairs,
+    )
+
+
+def attend_back_kernel(
+    scalars, packed, own_grads, twin_grads, log_total, cosine, sine, info, own_out, twin_out,
+    bias_grad, grads, natural, key_grad, value_grad, scale
+):
+    rows = grads.shape[0]
+    blocks = rows // tile
+    shift = scalars[0] * (blocks // 2)
+    own = place_of(scalars[0], rows // 2)
+    twin = place_of(1 - scalars[0], rows // 2)
+    grads[own, :] = own_grads[...]
+    grads[twin, :] = twin_grads[...]
+    bias_total = jnp.zeros((8, 3 * HEAD_DIM), wide)
+    for block in reversed(range(blocks)):
+        span = (block + 1) * tile
+        before = block * tile
+        query = packed[0, before:span, :]
+        about = info[:, before:span]
+        there = place_of(lax.rem(block + shift, blocks), tile)
+        grad = grads[before:span, :]
+        scores = scores_of(packed[1, :span, :], query, about, scalars[1], before, scale)
+        probs = jnp.exp(scores - log_total[0:1, before:span])
+        value_part = contract(probs.astype(low), grad, (1, 0))
+        dots = contract(packed[2, :span, :], grad, (1, 1))
+        delta = jnp.sum(probs * dots, axis=0, keepdims=True)
+        score_grad = (probs * (dots - delta)).astype(low)
+        query_grad = contract(score_grad, packed[1, :span, :], (0, 0)) * scale
+        key_part = contract(score_grad, query, (1, 0)) * scale
+        if block == blocks - 1:
+            key_grad[...] = key_part
+            value_grad[...] = value_part
+        else:
+            key_grad[:span, :] += key_part
+            value_grad[:span, :] += value_part
+        parts = (
+            turn(query_grad, cosine[there, :], sine[there, :], -1.0),
+            turn(key_grad[before:span, :], cosine[there, :], sine[there, :], -1.0),
+            value_grad[before:span, :],
+        )
+        together = jnp.concatenate(parts, axis=1).astype(low)
+        natural[before:span, :] = together
+        bias_total += fold_rows(together.astype(wide))
+    bias_grad[...] = bias_total
+    own_out[...] = natural[own, :]
+    twin_out[...] = natural[twin, :]
+
+
+def attend_back(scalars, packed, own_grads, twin_grads, log_total, cosine, sine, info):
+    held = own_grads.shape[0]
+    rows = 2 * held
+    pairs = rows * (rows + tile) // 2
+    return call(
+        partial(attend_back_kernel, scale=1.0 / math.sqrt(HEAD_DIM)),
+        "attend_back",
+        1,
+        [
+            fixed((3, rows, HEAD_DIM)),
+            fixed((held, HEAD_DIM)),
+            fixed((held, HEAD_DIM)),
+            fixed((8, rows)),
+            fixed((rows, 128)),
+            fixed((rows, 128)),
+            fixed((8, rows)),
+        ],
+        [kept((held, 3 * HEAD_DIM)), kept((held, 3 * HEAD_DIM)), kept((8, 3 * HEAD_DIM))],
+        [
+            shaped(held, 3 * HEAD_DIM),
+            shaped(held, 3 * HEAD_DIM),
+            shaped(8, 3 * HEAD_DIM, kind=wide),
+        ],
+        (scalars, packed, own_grads, twin_grads, log_total, cosine, sine, info),
+        pairs * HEAD_DIM * 10,
+        rows * HEAD_DIM * 16,
+        scratch=[
+            pltpu.VMEM((rows, HEAD_DIM), low),
+            pltpu.VMEM((rows, 3 * HEAD_DIM), low),
+            pltpu.VMEM((rows, HEAD_DIM), wide),
+            pltpu.VMEM((rows, HEAD_DIM), wide),
+        ],
+        exps=pairs,
+    )
+
+
+def turn(rows, cosine, sine, sign):
+    half_rot = ROTARY // 2
+    lane = lax.broadcasted_iota(jnp.int32, cosine.shape, 1)
+    front = rows[:, :128]
+    ahead = pltpu.roll(front, 128 - half_rot, 1)
+    behind = pltpu.roll(front, half_rot, 1)
+    other = jnp.where(lane < half_rot, -ahead, behind)
+    turned = front * cosine + other * (sine * sign)
+    return jnp.concatenate([turned, rows[:, 128:]], axis=1)
+
+
+def scores_of(keys, query, info, trunk_end, first_row, scale):
+    scores = contract(keys, query, (1, 1)) * scale
+    key_place = lax.broadcasted_iota(jnp.int32, scores.shape, 0)
+    query_place = first_row + lax.broadcasted_iota(jnp.int32, scores.shape, 1)
+    seen = (
+        (key_place < trunk_end)
+        | ((key_place >= info[0:1]) & (key_place < info[1:2]))
+        | (key_place >= info[2:3])
+    ) & (key_place <= query_place)
+    return jnp.where(seen, scores, masked_score)
+
+
+def tree_info(lengths, parent, rows):
+    labels = jnp.arange(SEGS)
+    ends = jnp.sum(jnp.where(labels[None, :] <= labels[:, None], lengths[None, :], 0), axis=1)
+    starts = ends - lengths
+    hot_parent = parent[:, None] == labels[None, :]
+    parent_start = jnp.sum(jnp.where(hot_parent, starts[None, :], 0), axis=1)
+    parent_end = jnp.sum(jnp.where(hot_parent, ends[None, :], 0), axis=1)
+    places = jnp.arange(rows, dtype=jnp.int32)
+    inside = (places[None, :] >= starts[:, None]) & (places[None, :] < ends[:, None])
+    pick = lambda table: jnp.sum(jnp.where(inside, table[:, None], 0), axis=0)
+    spans = [pick(parent_start), pick(parent_end), pick(starts)]
+    return jnp.stack(spans + [places] * 5).astype(jnp.int32), ends[0]
+
+
+def rotary_tables(depth):
+    half_rot = ROTARY // 2
+    lane = jnp.arange(128)
+    frequency = jnp.power(10000.0, -2.0 * (lane % half_rot).astype(wide) / ROTARY)
+    frequency = jnp.where(lane < ROTARY, frequency, 0.0)
+    angles = depth.astype(wide)[:, None] * frequency[None, :]
+    return jnp.cos(angles), jnp.sin(angles)
+
+
+def on_device_split(
+    residual,
+    out_grad,
+    path_depth,
+    seg_lengths,
+    parents,
+    attn_norm_gain,
+    attn_norm_bias,
+    ffn_norm_gain,
+    ffn_norm_bias,
+    qkv_weight,
+    qkv_bias,
+    dense_weight,
+    dense_bias,
+    up_weight,
+    up_bias,
+    down_weight,
+    down_bias,
+):
+    core = lax.axis_index("ctx")
+    line = lax.axis_index("tp")
+    plane = lax.axis_index("fsdp")
+    rows, held_width = residual.shape
+    width = 4 * held_width
+    half = width // 2
+
+    inward = jnp.concatenate([qkv_weight, up_weight], axis=1)
+    split = qkv_weight.shape[1]
+    other_depth = trade(path_depth, "ctx", 1)
+    cosine, sine = rotary_tables(jnp.concatenate([path_depth, other_depth]))
+    info, trunk_end = tree_info(seg_lengths[0], parents[0], 2 * rows)
+    scalars = jnp.stack([core, trunk_end, line, plane]).astype(jnp.int32)
+    qkv_shift = qkv_bias.astype(wide)[None, :]
+    up_shift = up_bias.astype(wide)[None, :]
+    inward_near, inward_far, inward, cosine, sine, info = meet(
+        trade(inward, "fsdp", 1), trade(inward, "fsdp", 2), inward, cosine, sine, info
+    )
+    middle = inward.shape[0] // 2
+    upper_corner = trade(inward_far[:middle], "fsdp", 1)
+    lower_corner = trade(inward_near[middle:], "fsdp", 2)
+    near, far = meet(
+        trade(residual, "tp", 1), trade(residual, "tp", 2), inward_near, inward_far
+    )[:2]
+    corner = trade(far, "tp", 1)
+    norm_rows = jnp.stack([attn_norm_gain, attn_norm_bias, ffn_norm_gain, ffn_norm_bias] * 4)
+    first_rows = after(norm_rows, far)
+    terms = [trade(first_rows, "tp", bit) for bit in (1, 2, 3)]
+    upper_corner, lower_corner, corner, *terms = meet(upper_corner, lower_corner, corner, *terms)
+    qkv_own, up_own = assemble(
+        scalars, (inward, inward_near, inward_far), (upper_corner, lower_corner), split
+    )
+    terms = (norm_rows, *terms)
+    pieces = (residual, near, far, corner)
+
+    def both_cores(own, *gate):
+        return own, trade(after(own, *gate), "ctx", 1)
+
+    def offloaded(weight, dim):
+        return lax.all_gather(after(weight, near), "fsdp", axis=dim, tiled=True)
+
+    qkv = both_cores(qkv_own)
+    up = both_cores(up_own)
+    first_grad = after(out_grad, corner)
+    grad_near = trade(first_grad, "tp", 1)
+    grad_far = trade(first_grad, "tp", 2)
+
+    attn_in, ffn_in, stats, terms = norm(scalars, pieces, terms)
+    mine, theirs = heads(scalars, attn_in, qkv, qkv_shift, cosine, sine)
+    theirs = trade(theirs, "ctx", 1)
+    hidden, slope = expand(after(scalars, mine), ffn_in, up, up_shift)
+    grad_corner = trade(after(grad_far, slope), "tp", 1)
+    down = both_cores(offloaded(down_weight, 1), slope)
+    packed, attended, twin_attended, log_total = attend(
+        after(scalars, slope, grad_near, grad_far), mine, theirs, info
+    )
+    dense = both_cores(offloaded(dense_weight, 1), attended)
+    other_attended = trade(twin_attended, "ctx", 1)
+    chip_out = project(scalars, attended, other_attended, hidden, dense, down)
+    shared_out = lax.psum_scatter(chip_out, "tp", scatter_dimension=1, tiled=True)
+
+    grad_pieces = (out_grad, grad_near, grad_far, grad_corner)
+    cotangent, pre_grad, head_grad, other_grad, up_bias_rows = hidden_back(
+        after(scalars, chip_out), grad_pieces, slope, dense, down
+    )
+    other_grad = trade(other_grad, "ctx", 1)
+
+    def outer(left, right):
+        return contract(left, right, (0, 0))
+
+    def add_low(own, arrived):
+        return (own + arrived.astype(wide)).astype(low)
+
+    def to_owner(total, dim):
+        return lax.psum_scatter(total, "fsdp", scatter_dimension=dim, tiled=True)
+
+    both_attended = join_cores(attended, other_attended, core, 1)
+    down_other = outer(after(hidden, pre_grad), cotangent[:, half:]).astype(low)
+    down_arrived = trade(down_other, "ctx", 1)
+    dense_other = outer(after(both_attended, down_other), cotangent[:, half:]).astype(low)
+    dense_arrived = trade(dense_other, "ctx", 1)
+    joined_grad, twin_grad, qkv_bias_rows = attend_back(
+        after(scalars, dense_other), packed, head_grad, other_grad, log_total, cosine, sine, info
+    )
+    other_joined = trade(twin_grad, "ctx", 1)
+    down_total = add_low(
+        outer(after(hidden, joined_grad), cotangent[:, :half]), down_arrived
+    )
+    dense_total = add_low(
+        outer(after(both_attended, down_total), cotangent[:, :half]), dense_arrived
+    )
+    dense_grad = to_owner(dense_total, 1)
+    mix_in = (joined_grad, other_joined, pre_grad, qkv, up, terms, stats, pieces)
+    *leave, sums_a, sums_b, row_a = mix(
+        after(scalars, dense_total), *mix_in, (3, 1), (low, low)
+    )
+    mixed_side, mixed_near = trade(leave[0], "tp", 1), trade(leave[1], "tp", 1)
+    down_grad, down_hop = scatter_plane(down_total, "fsdp", 1)
+    *stay_mixed, sums_c, sums_d, row_b = mix(
+        after(scalars, leave[0], *down_hop), *mix_in, (2, 0), (wide, wide)
+    )
+    passed = (stay_mixed[0] + mixed_side.astype(wide)).astype(low)
+    far_mixed = trade(passed, "tp", 2)
+    both_joined = join_cores(joined_grad, other_joined, core, 1)
+    up_other = outer(
+        after(ffn_in, stay_mixed[0], passed, down_grad, shared_out)[:, half:], pre_grad
+    ).astype(low)
+    up_arrived = trade(up_other, "ctx", 1)
+
+    shared_out = shared_out.astype(wide)
+    shared_out = join_cores(shared_out[:, :tile], shared_out[:, tile:], core, 1)
+    output = (
+        residual.astype(wide) + shared_out + dense_bias.astype(wide) + down_bias.astype(wide)
+    ).astype(low)
+
+    row_sums = row_a + row_b
+    row_total = jnp.stack([row_sums[:, 0], row_sums[:, 64]])
+    fold = lambda x: jnp.sum(x.reshape(4, 8, 2, tile), axis=1)
+    gather_sums = lambda own, other: jnp.stack([fold(own), fold(other)], axis=2).reshape(4, 2, 2 * tile)
+    leaving, norm_sums = gather_sums(sums_a, sums_b), gather_sums(sums_c, sums_d)
+    hop_side = trade(jnp.concatenate([leaving.reshape(-1), row_total.reshape(-1)]), "tp", 1)
+    qkv_other = outer(after(attn_in, up_other, hop_side)[:, half:], both_joined).astype(low)
+    qkv_arrived = trade(qkv_other, "ctx", 1)
+    norm_sums = norm_sums + hop_side[: 8 * held_width].reshape(norm_sums.shape)
+    row_total = row_total + hop_side[8 * held_width :].reshape(row_total.shape)
+    hop_far = trade(jnp.concatenate([norm_sums[:, 0].reshape(-1), row_total.reshape(-1)]), "tp", 2)
+    up_total = add_low(
+        outer(after(ffn_in, qkv_other, hop_far)[:, :half], pre_grad), up_arrived
+    )
+    up_grad = to_owner(up_total, 0)
+    norm_total = norm_sums[:, 1] + hop_far[: 4 * held_width].reshape(4, held_width)
+    row_total = row_total + hop_far[4 * held_width :].reshape(row_total.shape)
+    row_means = row_total / width
+    norm_total = join_cores(norm_total[:, :tile], norm_total[:, tile:], core, 1)
+    held_grad_sum = jnp.sum(out_grad.astype(wide), axis=0)
+    columns = jnp.concatenate(
+        [
+            norm_total.reshape(-1),
+            held_grad_sum,
+            jnp.sum(up_bias_rows, axis=0),
+            jnp.sum(qkv_bias_rows, axis=0),
+        ]
+    )
+    columns = columns + trade(columns, "fsdp", 1)
+    qkv_total = add_low(
+        outer(after(attn_in, up_total, dense_grad)[:, :half], both_joined), qkv_arrived
+    )
+    columns = columns + trade(columns, "fsdp", 2)
+    other_columns = trade(columns, "ctx", 1)
+    cut = columns.shape[0] - qkv_bias.shape[0] // 2
+    qkv_bias_grad = join_cores(columns[cut:], other_columns[cut:], core, 0)
+    together = columns[:cut] + other_columns[:cut]
+    norm_grads = together[:width].reshape(4, held_width)
+    out_bias_grad = together[width : width + held_width]
+    up_bias_grad = together[width + held_width :]
+
+    qkv_grad, qkv_hop = scatter_plane(qkv_total, "fsdp", 0)
+
+    far_mixed = after(far_mixed, mixed_near, other_columns, *qkv_hop)
+    shared_mixed = stay_mixed[1] + mixed_near.astype(wide) + far_mixed.astype(wide)
+    shared_mixed = join_cores(shared_mixed[:, :tile], shared_mixed[:, tile:], core, 1)
+    mean = stats[:, 0:1]
+    inverse = stats[:, 64:65]
+    own_normed = (residual.astype(wide) - mean) * inverse
+    back = inverse * (shared_mixed - row_means[0][:, None] - own_normed * row_means[1][:, None])
+    input_grad = (out_grad.astype(wide) + back).astype(low)
+    return (
+        output,
+        input_grad,
+        norm_grads[0],
+        norm_grads[1],
+        norm_grads[2],
+        norm_grads[3],
+        qkv_grad.astype(wide),
+        qkv_bias_grad,
+        dense_grad.astype(wide),
+        out_bias_grad,
+        up_grad.astype(wide),
+        up_bias_grad,
+        down_grad.astype(wide),
+        out_bias_grad,
+    )
+
+
+def splits_heads(mesh):
+    return mesh.shape["tp"] == 4 and mesh.shape["fsdp"] == 4 and mesh.shape["ctx"] == 2
+
+
 def solution(mesh):
     placed = (
         P(("fsdp", "ctx"), "tp"),
@@ -330,7 +1168,7 @@
         P("tp"),
     )
     return jax.shard_map(
-        on_device,
+        on_device_split if splits_heads(mesh) else on_device,
         mesh=mesh,
         in_specs=placed,
         out_specs=(

time: 1350 us -> 464 us (0.34)
  waiting for transfers between devices: 975 us -> 149 us
  Pallas kernels: 0 us -> 152 us
  matrix products: 196 us -> 53 us
  blocking collectives: 41.4 us -> 0 us
  other arithmetic: 68.2 us -> 30.7 us
  starting transfers between devices: 8.65 us -> 34.9 us
  local copies, waits for them, and re-layouts: 43.1 us -> 22.4 us
    psum x1 -> x0, waiting for transfers between devices: 563 us -> none  [on_device(): total_attn, total_ffn = lax.psum((grad_attn_in, grad_ffn_in), 'tp')]
    reduce_scatter x5 -> x3, waiting for transfers between devices: 238 us -> 0.02 us  [the longest x2 0.02 us: to_owner(): return lax.psum_scatter(total, 'fsdp', scatter_dimension=dim, tiled=True)]
    all_gather x6 -> x2, waiting for transfers between devices: 171 us -> 0.01 us  [offloaded(): return lax.all_gather(after(weight, near), 'fsdp', axis=dim, tiled=True)]
    pallas_call x0 -> x10, Pallas kernels: none -> 152 us  [call(): pl.pallas_call(kernel, grid_spec=pltpu.PrefetchScalarGridSpec(num_scalar_...]
    ppermute x4 -> x42, waiting for transfers between devices: 0.01 us -> 149 us  [trade(): return lax.ppermute(x, axis, [(i, i ^ bit) for i in range(peers)])]
    dot_general x26 -> x8, matrix products: 196 us -> 53 us  [contract(): lax.dot_general(a, b, ((dims[:1], dims[1:]), ((), ())), preferred_element...]
    ppermute x4 -> x42, starting transfers between devices: 7.77 us -> 34.5 us  [trade(): return lax.ppermute(x, axis, [(i, i ^ bit) for i in range(peers)])]
    psum x1 -> x0, blocking collectives: 26.3 us -> none  [on_device(): lax.psum((grad_qkv_b, grad_up_b, grad_out_bias, norm_grads), ('fsdp', 'ct...]
  transfers between devices with their start and end apart: 16 -> 47, of which waited for: 8 -> 20; matrix products, arithmetic and copies ran while one was open for 22% -> 17% of each run, Pallas kernels for 0% -> 29%
where the time goes in v2:
time: 464 us; the launch traced here: 457 us
  Pallas kernels  152 us (33%)
  waiting for transfers between devices  149 us (32%)
  matrix products  53 us (11%)
  starting transfers between devices  34.9 us (8%)
  other arithmetic  30.7 us (7%)
  local copies, waits for them, and re-layouts  22.4 us (5%)
  between operations  14.8 us (3%)
    pallas_call x10, Pallas kernels, call(): pl.pallas_call(kernel, grid_spec=pltpu.PrefetchScalarGridSpec(num_scalar_...  152 us
    ppermute x42, waiting for transfers between devices, trade(): return lax.ppermute(x, axis, [(i, i ^ bit) for i in range(peers)])  149 us
    dot_general x8, matrix products, contract(): lax.dot_general(a, b, ((dims[:1], dims[1:]), ((), ())), preferred_element...  53 us
    ppermute x42, starting transfers between devices, trade(): return lax.ppermute(x, axis, [(i, i ^ bit) for i in range(peers)])  34.5 us
    unnamed x108, local copies, waits for them, and re-layouts  13.1 us
  transfers between devices with their start and end apart: 47, of which 20 were waited for; matrix products, arithmetic and copies ran while one was open for 17% of the time, Pallas kernels for 29%

profile of v2, /device:TPU:0, one launch (start us, length us, event | category | flops | bytes accessed | tf_op | source)
XLA Modules:
  0.0 456.5 jit_solution(13227983695569946690)
XLA Ops:
  20.4 5.5 %multiply_sine_fusion = (f32[2048,128]{1,0:T(8,128)}, f32[2048,128]{1,0:T(8,128)}) fusion(f32[128]{0:T(128)S(1)} %compare_select_fusion, f32[2048]{0:T(1024)S(1)} %add_convert_fusion.11), kind=kLoop, calls=%fused_computation.37 | loop fusion | flops 262144 | bytes 2105856 | tf_op jit(solution)/shard_map/sin | solution.py:940
  25.9 27.8 %collective-permute-done.2.near = bf16[256,3584]{1,0:T(8,128)(2,1)S(1)} collective-permute-done((bf16[256,3584]{1,0:T(8,128)(2,1)}, bf16[256,3584]{1,0:T(8,128)(2,1)S(1)}, u32[]{:S(2)}, u32[]{:S(2)}) %collective-permute-start.2) | collective-permute-done | bytes 1835040 | tf_op jit(solution)/shard_map/ppermute | solution.py:323
  55.2 6.5 %collective-permute-done.refs_1_.second_piece = bf16[1024,512]{1,0:T(8,128)(2,1)} collective-permute-done((bf16[1024,512]{1,0:T(8,128)(2,1)S(1)}, bf16[1024,512]{1,0:T(8,128)(2,1)}, u32[]{:S(2)}, u32[]{:S(2)}) %collective-permute-start) | collective-permute-done | bytes 1048608 | tf_op jit(solution)/shard_map/ppermute | solution.py:323
  72.4 15.8 %collective-permute-done.10.refs_7_ = bf16[16,512]{1,0:T(8,128)(2,1)S(1)} collective-permute-done((bf16[16,512]{1,0:T(8,128)(2,1)S(1)}, bf16[16,512]{1,0:T(8,128)(2,1)S(1)}, u32[]{:S(2)}, u32[]{:S(2)}) %collective-permute-start.10) | collective-permute-done | bytes 16416 | tf_op jit(solution)/shard_map/ppermute | solution.py:323
  92.9 6.9 %collective-permute-done.5.upper = bf16[128,3584]{1,0:T(8,128)(2,1)} collective-permute-done((bf16[128,3584]{1,0:T(8,128)(2,1)}, bf16[128,3584]{1,0:T(8,128)(2,1)}, u32[]{:S(2)}, u32[]{:S(2)}) %collective-permute-start.5) | collective-permute-done | bytes 917536 | tf_op jit(solution)/shard_map/ppermute | solution.py:323
  100.8 7.7 %assemble.1 = (bf16[1024,1536]{1,0:T(8,128)(2,1)}, bf16[1024,2048]{1,0:T(8,128)(2,1)}) custom-call(s32[4]{0:T(128)} %pad_add_fusion.scalars, bf16[256,3584]{1,0:T(8,128)(2,1)} %constant_dynamic-update-slice_fusion.own, bf16[256,3584]{1,0:T(8,128)(2,1)} %copy-done.4, bf16[256,3584]{1,0:T(8,128)(2,1)} %collective-permute-done.3.far, ...), custom_call_target="tpu_custom_call" | custom-call | flops 14680064 | bytes 234881024 | tf_op jit(solution)/shard_map/assemble/pallas_call | solution.py:410
  111.8 9.9 %norm.1 = (bf16[1024,2048]{1,0:T(8,128)(2,1)}, bf16[1024,2048]{1,0:T(8,128)(2,1)}, f32[1024,128]{1,0:T(8,128)}, f32[8,2048]{1,0:T(8,128)}) custom-call(s32[4]{0:T(128)} %pad_add_fusion.scalars, bf16[1024,512]{1,0:T(8,128)(2,1)} %second_piece.1, bf16[1024,512]{1,0:T(8,128)(2,1)} %collective-permute-done.refs_1_.second_piece, ...), custom_call_target="tpu_custom_call" | custom-call | flops 335544320 | bytes 201326592 | tf_op jit(solution)/shard_map/norm/pallas_call | solution.py:410
  121.7 14.2 %heads.1 = (bf16[3,1024,256]{2,1,0:T(8,128)(2,1)}, bf16[3,1024,256]{2,1,0:T(8,128)(2,1)}) custom-call(s32[4]{0:T(128)} %pad_add_fusion.scalars, bf16[1024,2048]{1,0:T(8,128)(2,1)} %get-tuple-element.148.rows_in, bf16[1024,1536]{1,0:T(8,128)(2,1)} %get-tuple-element.95.own.qkv_own, bf16[1024,1536]{1,0:T(8,128)(2,1)} %collective-permute-done.11.other.qkv_other, ...), custom_call_target="tpu_custom_call" | custom-call | flops 103079215104 | bytes 218103808 | tf_op jit(solution)/shard_map/heads/pallas_call | solution.py:410
  138.4 17.6 %expand.1 = (bf16[1024,2048]{1,0:T(8,128)(2,1)}, bf16[1024,2048]{1,0:T(8,128)(2,1)}) custom-call(s32[4]{0:T(128)} %pad_add_fusion.scalars, bf16[1024,2048]{1,0:T(8,128)(2,1)} %get-tuple-element.147.rows_in, bf16[1024,2048]{1,0:T(8,128)(2,1)} %get-tuple-element.101.own.up_own, bf16[1024,2048]{1,0:T(8,128)(2,1)} %copy-done.42, f32[1,2048]{1,0:T(1,128)} %bitcast.71), custom_call_target="tpu_custom_call" | custom-call | flops 137438953472 | bytes 335544320 | tf_op jit(solution)/shard_map/expand/pallas_call | solution.py:410
  160.4 11.8 %attend.1 = (bf16[3,2048,256]{2,1,0:T(8,128)(2,1)}, bf16[1024,256]{1,0:T(8,128)(2,1)}, bf16[1024,256]{1,0:T(8,128)(2,1)}, f32[8,2048]{1,0:T(8,128)}) custom-call(s32[4]{0:T(128)} %pad_add_fusion.scalars, bf16[3,1024,256]{2,1,0:T(8,128)(2,1)} %get-tuple-element.98.mine, bf16[3,1024,256]{2,1,0:T(8,128)(2,1)} %copy-done.43, s32[8,2048]{1,0:T(8,128)} %stack.84.info), custom_call_target="tpu_custom_call" | custom-call | flops 38654705664 | bytes 134217728 | tf_op jit(solution)/shard_map/attend/pallas_call | solution.py:410
  179.3 16.6 %project.1 = bf16[1024,2048]{1,0:T(8,128)(2,1)} custom-call(s32[4]{0:T(128)} %pad_add_fusion.scalars, bf16[1024,256]{1,0:T(8,128)(2,1)} %get-tuple-element.107.mine, bf16[1024,256]{1,0:T(8,128)(2,1)} %copy-done.18, bf16[1024,2048]{1,0:T(8,128)(2,1)} %get-tuple-element.127.hidden, bf16[512,1024]{1,0:T(8,128)(2,1)} %all-gather.3.cloned.1.call-done.dense_own.refs_5_, ...), custom_call_target="tpu_custom_call" | custom-call | flops 171798691840 | bytes 318767104 | tf_op jit(solution)/shard_map/project/pallas_call | solution.py:410
  198.6 21.6 %hidden_back.1 = (bf16[1024,2048]{1,0:T(8,128)(2,1)}, bf16[1024,2048]{1,0:T(8,128)(2,1)}, bf16[1024,256]{1,0:T(8,128)(2,1)}, bf16[1024,256]{1,0:T(8,128)(2,1)}, f32[8,2048]{1,0:T(8,128)}) custom-call(s32[4]{0:T(128)} %pad_add_fusion.scalars, bf16[1024,512]{1,0:T(8,128)(2,1)} %refs_0_.3, bf16[1024,512]{1,0:T(8,128)(2,1)} %collective-permute-done.13.refs_1_, ...), custom_call_target="tpu_custom_call" | custom-call | flops 171798691840 | bytes 402653184 | tf_op jit(solution)/shard_map/hidden_back/pallas_call | solution.py:410
  220.3 7.9 %convolution_convert_fusion.2 = bf16[2048,1024]{1,0:T(8,128)(2,1)} fusion(bf16[1024,2048]{1,0:T(8,128)(2,1)S(1)} %copy-done.50, bf16[1024,2048]{1,0:T(8,128)(2,1)} %get-tuple-element.119), kind=kOutput, calls=%fused_computation.5 | convolution fusion | flops 4297064448 | bytes 10485760 | tf_op jit(solution)/shard_map/dot_general | solution.py:380
  232.1 17.8 %attend_back.1 = (bf16[1024,768]{1,0:T(8,128)(2,1)}, bf16[1024,768]{1,0:T(8,128)(2,1)}, f32[8,768]{1,0:T(8,128)}) custom-call(s32[4]{0:T(128)} %pad_add_fusion.scalars, bf16[3,2048,256]{2,1,0:T(8,128)(2,1)} %get-tuple-element.122.packed, bf16[1024,256]{1,0:T(8,128)(2,1)} %get-tuple-element.123.own_grads, bf16[1024,256]{1,0:T(8,128)(2,1)} %copy-done.45, ...), custom_call_target="tpu_custom_call" | custom-call | flops 96636764160 | bytes 134217728 | tf_op jit(solution)/shard_map/attend_back/pallas_call | solution.py:410
  250.5 7.7 %add_convert_fusion.1 = bf16[2048,1024]{1,0:T(8,128)(2,1)S(1)} fusion(bf16[2048,1024]{1,0:T(8,128)(2,1)} %collective-permute-done.21, bf16[1024,2048]{1,0:T(8,128)(2,1)} %get-tuple-element.127.hidden, bf16[1024,2048]{1,0:T(8,128)(2,1)S(1)} %copy-done.48), kind=kOutput, calls=%fused_computation.1 | convolution fusion | flops 4301258752 | bytes 14680064 | tf_op jit(solution)/shard_map/dot_general | solution.py:380
  266.8 17.3 %mix.2 = (bf16[1024,512]{1,0:T(8,128)(2,1)}, bf16[1024,512]{1,0:T(8,128)(2,1)}, f32[32,512]{1,0:T(8,128)}, f32[32,512]{1,0:T(8,128)}, f32[1024,128]{1,0:T(8,128)}) custom-call(s32[4]{0:T(128)} %pad_add_fusion.scalars, bf16[1024,768]{1,0:T(8,128)(2,1)} %get-tuple-element.126.mine, bf16[1024,768]{1,0:T(8,128)(2,1)} %copy-done.9, ...), custom_call_target="tpu_custom_call" | custom-call | flops 120259084288 | bytes 301989888 | tf_op jit(solution)/shard_map/mix/pallas_call | solution.py:410
  288.3 17.6 %mix.3 = (f32[1024,512]{1,0:T(8,128)}, f32[1024,512]{1,0:T(8,128)}, f32[32,512]{1,0:T(8,128)}, f32[32,512]{1,0:T(8,128)}, f32[1024,128]{1,0:T(8,128)}) custom-call(s32[4]{0:T(128)} %pad_add_fusion.scalars, bf16[1024,768]{1,0:T(8,128)(2,1)} %get-tuple-element.126.mine, bf16[1024,768]{1,0:T(8,128)(2,1)} %copy-done.9, ...), custom_call_target="tpu_custom_call" | custom-call | flops 120259084288 | bytes 301989888 | tf_op jit(solution)/shard_map/mix/pallas_call | solution.py:410
  306.0 21.8 %collective-permute-done.27 = bf16[1024,512]{1,0:T(8,128)(2,1)} collective-permute-done((bf16[1024,512]{1,0:T(8,128)(2,1)}, bf16[1024,512]{1,0:T(8,128)(2,1)}, u32[]{:S(2)}, u32[]{:S(2)}) %collective-permute-start.27) | collective-permute-done | bytes 1048608 | tf_op jit(solution)/shard_map/ppermute | solution.py:323
  334.0 9.5 %convolution_convert_fusion.1 = bf16[1024,2048]{1,0:T(8,128)(2,1)} fusion(bf16[1024,2048]{1,0:T(8,128)(2,1)} %get-tuple-element.117.pre_grad, bf16[1024,2048]{1,0:T(8,128)(2,1)} %get-tuple-element.147.rows_in), kind=kOutput, calls=%fused_computation.4 | convolution fusion | flops 4297064448 | bytes 10485760 | tf_op jit(solution)/shard_map/dot_general | solution.py:380
  353.3 7.1 %convolution_convert_fusion = bf16[1024,1536]{1,0:T(8,128)(2,1)} fusion(bf16[1024,2048]{1,0:T(8,128)(2,1)} %get-tuple-element.148.rows_in, bf16[1024,768]{1,0:T(8,128)(2,1)S(1)} %get-tuple-element.174, bf16[1024,768]{1,0:T(8,128)(2,1)S(1)} %get-tuple-element.173), kind=kOutput, calls=%fused_computation.3 | convolution fusion | flops 3229089792 | bytes 8388608 | tf_op jit(solution)/shard_map/dot_general | solution.py:380
  360.4 8.0 %add_convert_fusion = bf16[1024,2048]{1,0:T(8,128)(2,1)} fusion(bf16[1024,2048]{1,0:T(8,128)(2,1)} %collective-permute-done.36, bf16[1024,2048]{1,0:T(8,128)(2,1)S(1)} %copy-done.49, bf16[1024,2048]{1,0:T(8,128)(2,1)S(1)} %copy-done.41), kind=kOutput, calls=%fused_computation | convolution fusion | flops 4301258752 | bytes 14680064 | tf_op jit(solution)/shard_map/dot_general | solution.py:380
  381.0 7.1 %add_convert_fusion.2 = bf16[1024,1536]{1,0:T(8,128)(2,1)S(1)} fusion(bf16[1024,1536]{1,0:T(8,128)(2,1)} %collective-permute-done.37, bf16[1024,2048]{1,0:T(8,128)(2,1)} %get-tuple-element.148.rows_in, bf16[1024,768]{1,0:T(8,128)(2,1)} %copy-done.7, bf16[1024,768]{1,0:T(8,128)(2,1)S(1)} %get-tuple-element.173), kind=kOutput, calls=%fused_computation.2 | convolution fusion | flops 3232235520 | bytes 11534336 | tf_op jit(solution)/shard_map/dot_general | solution.py:380
  393.3 15.1 %collective-permute-done.38 = bf16[128,1536]{1,0:T(8,128)(2,1)S(1)} collective-permute-done((bf16[128,1536]{1,0:T(8,128)(2,1)S(1)}, bf16[128,1536]{1,0:T(8,128)(2,1)S(1)}, u32[]{:S(2)}, u32[]{:S(2)}) %collective-permute-start.38) | collective-permute-done | bytes 393248 | tf_op jit(solution)/shard_map/ppermute | solution.py:323
  412.4 27.6 %collective-permute-done.28 = bf16[1024,512]{1,0:T(8,128)(2,1)S(1)} collective-permute-done((bf16[1024,512]{1,0:T(8,128)(2,1)S(1)}, bf16[1024,512]{1,0:T(8,128)(2,1)S(1)}, u32[]{:S(2)}, u32[]{:S(2)}) %collective-permute-start.28) | collective-permute-done | bytes 1048608 | tf_op jit(solution)/shard_map/ppermute | solution.py:323
  (288 shorter events, 115.1 us)
Async XLA Ops:
  7.2 152.1 %all-gather.5.cloned.1.call-start = ((), (), s32[]{:S(2)}) async-start(), calls=%async_computation.4 | async-start | bytes 5242880 | tf_op jit(solution)/shard_map/all_gather | solution.py:1001
  10.5 43.2 %collective-permute-start.2 = (bf16[256,3584]{1,0:T(8,128)(2,1)}, bf16[256,3584]{1,0:T(8,128)(2,1)S(1)}, u32[]{:S(2)}, u32[]{:S(2)}) collective-permute-start(bf16[256,3584]{1,0:T(8,128)(2,1)} %constant_dynamic-update-slice_fusion.own), channel_id=1, source_target_pairs={{0,8},{8,0},{16,24},{24,16},{1,9},{9,1},{17,25},{25,17},{2,10},{10... | collective-permute-start | bytes 5505032 | tf_op jit(solution)/shard_map/ppermute | solution.py:323
  13.5 41.8 %collective-permute-start.3 = (bf16[256,3584]{1,0:T(8,128)(2,1)}, bf16[256,3584]{1,0:T(8,128)(2,1)}, u32[]{:S(2)}, u32[]{:S(2)}) collective-permute-start(bf16[256,3584]{1,0:T(8,128)(2,1)} %constant_dynamic-update-slice_fusion.own), channel_id=1, source_target_pairs={{0,16},{8,24},{16,0},{24,8},{1,17},{9,25},{17,1},{25,9},{2,18},{10... | collective-permute-start | bytes 5505032 | tf_op jit(solution)/shard_map/ppermute | solution.py:323
  15.0 46.8 %collective-permute-start = (bf16[1024,512]{1,0:T(8,128)(2,1)S(1)}, bf16[1024,512]{1,0:T(8,128)(2,1)}, u32[]{:S(2)}, u32[]{:S(2)}) collective-permute-start(bf16[1024,512]{1,0:T(8,128)(2,1)S(1)} %copy-done.2), channel_id=1, source_target_pairs={{0,1},{1,0},{2,3},{3,2},{4,5},{5,4},{6,7},{7,6},{8,9},{9,8},{10,11... | collective-permute-start | bytes 3145736 | tf_op jit(solution)/shard_map/ppermute | solution.py:323
  16.6 47.6 %collective-permute-start.1 = (bf16[1024,512]{1,0:T(8,128)(2,1)S(1)}, bf16[1024,512]{1,0:T(8,128)(2,1)}, u32[]{:S(2)}, u32[]{:S(2)}) collective-permute-start(bf16[1024,512]{1,0:T(8,128)(2,1)S(1)} %copy-done.2), channel_id=1, source_target_pairs={{0,2},{1,3},{2,0},{3,1},{4,6},{5,7},{6,4},{7,5},{8,10},{9,11},{10,... | collective-permute-start | bytes 3145736 | tf_op jit(solution)/shard_map/ppermute | solution.py:323
  64.2 108.0 %all-gather.3.cloned.1.call-start = ((), (), s32[]{:S(2)}) async-start(), calls=%async_computation.3 | async-start | bytes 1310720 | tf_op jit(solution)/shard_map/all_gather | solution.py:1001
  64.3 35.6 %collective-permute-start.7 = (bf16[1024,512]{1,0:T(8,128)(2,1)}, bf16[1024,512]{1,0:T(8,128)(2,1)S(1)}, u32[]{:S(2)}, u32[]{:S(2)}) collective-permute-start(bf16[1024,512]{1,0:T(8,128)(2,1)} %collective-permute-done.1.refs_2_.first_piece), channel_id=1, source_target_pairs={{0,1},{1,0},{2,3},{3,2},{4,5},{5,4},{6,7},{7,6},{8,9},{9,8},{10,11... | collective-permute-start | bytes 3145736 | tf_op jit(solution)/shard_map/ppermute | solution.py:323
  67.9 31.8 %collective-permute-start.5 = (bf16[128,3584]{1,0:T(8,128)(2,1)}, bf16[128,3584]{1,0:T(8,128)(2,1)}, u32[]{:S(2)}, u32[]{:S(2)}) collective-permute-start(bf16[128,3584]{1,0:T(8,128)(2,1)} %slice.199), channel_id=1, source_target_pairs={{0,8},{8,0},{16,24},{24,16},{1,9},{9,1},{17,25},{25,17},{2,10},{10... | collective-permute-start | bytes 2752520 | tf_op jit(solution)/shard_map/ppermute | solution.py:323
  68.5 31.4 %collective-permute-start.6 = (bf16[128,3584]{1,0:T(8,128)(2,1)}, bf16[128,3584]{1,0:T(8,128)(2,1)S(1)}, u32[]{:S(2)}, u32[]{:S(2)}) collective-permute-start(bf16[128,3584]{1,0:T(8,128)(2,1)} %slice.200), channel_id=1, source_target_pairs={{0,16},{8,24},{16,0},{24,8},{1,17},{9,25},{17,1},{25,9},{2,18},{10... | collective-permute-start | bytes 2752520 | tf_op jit(solution)/shard_map/ppermute | solution.py:323
  109.8 224.1 %reduce-scatter.4.cloned.1.call-start = ((), (), s32[]{:S(2)}) async-start(), calls=%async_computation.5 | async-start | bytes 5242880 | tf_op jit(solution)/shard_map/reduce_scatter | solution.py:1021
  109.9 47.7 %collective-permute-start.13 = (bf16[1024,512]{1,0:T(8,128)(2,1)}, bf16[1024,512]{1,0:T(8,128)(2,1)}, u32[]{:S(2)}, u32[]{:S(2)}) collective-permute-start(bf16[1024,512]{1,0:T(8,128)(2,1)} %refs_0_.3), channel_id=1, source_target_pairs={{0,1},{1,0},{2,3},{3,2},{4,5},{5,4},{6,7},{7,6},{8,9},{9,8},{10,11... | collective-permute-start | bytes 3145736 | tf_op jit(solution)/shard_map/ppermute | solution.py:323
  110.2 49.1 %collective-permute-start.14 = (bf16[1024,512]{1,0:T(8,128)(2,1)}, bf16[1024,512]{1,0:T(8,128)(2,1)}, u32[]{:S(2)}, u32[]{:S(2)}) collective-permute-start(bf16[1024,512]{1,0:T(8,128)(2,1)} %refs_0_.3), channel_id=1, source_target_pairs={{0,2},{1,3},{2,0},{3,1},{4,6},{5,7},{6,4},{7,5},{8,10},{9,11},{10,... | collective-permute-start | bytes 3145736 | tf_op jit(solution)/shard_map/ppermute | solution.py:323
  111.8 24.6 %collective-permute-start.12 = (bf16[1024,2048]{1,0:T(8,128)(2,1)}, bf16[1024,2048]{1,0:T(8,128)(2,1)S(1)}, u32[]{:S(2)}, u32[]{:S(2)}) collective-permute-start(bf16[1024,2048]{1,0:T(8,128)(2,1)} %get-tuple-element.101.own.up_own), channel_id=1, source_target_pairs={{0,4},{4,0},{1,5},{5,1},{2,6},{6,2},{3,7},{7,3},{8,12},{12,8},{9,1... | collective-permute-start | bytes 12582920 | tf_op jit(solution)/shard_map/ppermute | solution.py:323
  172.8 25.8 %collective-permute-start.19 = (bf16[1024,512]{1,0:T(8,128)(2,1)}, bf16[1024,512]{1,0:T(8,128)(2,1)}, u32[]{:S(2)}, u32[]{:S(2)}) collective-permute-start(bf16[1024,512]{1,0:T(8,128)(2,1)} %collective-permute-done.14.refs_2_), channel_id=1, source_target_pairs={{0,1},{1,0},{2,3},{3,2},{4,5},{5,4},{6,7},{7,6},{8,9},{9,8},{10,11... | collective-permute-start | bytes 3145736 | tf_op jit(solution)/shard_map/ppermute | solution.py:323
  230.9 31.2 %collective-permute-start.22 = (bf16[512,1024]{1,0:T(8,128)(2,1)}, bf16[512,1024]{1,0:T(8,128)(2,1)}, u32[]{:S(2)}, u32[]{:S(2)}) collective-permute-start(bf16[512,1024]{1,0:T(8,128)(2,1)} %fusion.18), channel_id=1, source_target_pairs={{0,4},{4,0},{1,5},{5,1},{2,6},{6,2},{3,7},{7,3},{8,12},{12,8},{9,1... | collective-permute-start | bytes 3145736 | tf_op jit(solution)/shard_map/ppermute | solution.py:323
  231.0 149.9 %reduce-scatter.6.cloned.1.call-start = ((), (), s32[]{:S(2)}) async-start(), calls=%async_computation.6 | async-start | bytes 1310720 | tf_op jit(solution)/shard_map/reduce_scatter | solution.py:1036
  284.0 43.8 %collective-permute-start.27 = (bf16[1024,512]{1,0:T(8,128)(2,1)}, bf16[1024,512]{1,0:T(8,128)(2,1)}, u32[]{:S(2)}, u32[]{:S(2)}) collective-permute-start(bf16[1024,512]{1,0:T(8,128)(2,1)} %get-tuple-element.132), channel_id=1, source_target_pairs={{0,1},{1,0},{2,3},{3,2},{4,5},{5,4},{6,7},{7,6},{8,9},{9,8},{10,11... | collective-permute-start | bytes 3145736 | tf_op jit(solution)/shard_map/ppermute | solution.py:323
  285.8 45.2 %collective-permute-start.34 = (bf16[2048,256]{1,0:T(8,128)(2,1)S(1)}, bf16[2048,256]{1,0:T(8,128)(2,1)}, u32[]{:S(2)}, u32[]{:S(2)}) collective-permute-start(bf16[2048,256]{1,0:T(8,128)(2,1)S(1)} %pad_maximum_fusion.5), channel_id=1, source_target_pairs={{0,8},{8,0},{16,24},{24,16},{1,9},{9,1},{17,25},{25,17},{2,10},{10... | collective-permute-start | bytes 3145736 | tf_op jit(solution)/shard_map/ppermute | solution.py:323
  286.5 44.5 %collective-permute-start.35 = (bf16[2048,256]{1,0:T(8,128)(2,1)S(1)}, bf16[2048,256]{1,0:T(8,128)(2,1)S(1)}, u32[]{:S(2)}, u32[]{:S(2)}) collective-permute-start(bf16[2048,256]{1,0:T(8,128)(2,1)S(1)} %pad_maximum_fusion.4), channel_id=1, source_target_pairs={{0,16},{8,24},{16,0},{24,8},{1,17},{9,25},{17,1},{25,9},{2,18},{10... | collective-permute-start | bytes 3145736 | tf_op jit(solution)/shard_map/ppermute | solution.py:323
  343.9 102.5 %reduce-scatter.8.cloned.1.call-start = ((), (), s32[]{:S(2)}) async-start(), calls=%async_computation.7 | async-start | bytes 5242880 | tf_op jit(solution)/shard_map/reduce_scatter | solution.py:1036
  372.7 39.7 %collective-permute-start.26 = (bf16[1024,512]{1,0:T(8,128)(2,1)}, bf16[1024,512]{1,0:T(8,128)(2,1)S(1)}, u32[]{:S(2)}, u32[]{:S(2)}) collective-permute-start(bf16[1024,512]{1,0:T(8,128)(2,1)} %get-tuple-element.135), channel_id=1, source_target_pairs={{0,1},{1,0},{2,3},{3,2},{4,5},{5,4},{6,7},{7,6},{8,9},{9,8},{10,11... | collective-permute-start | bytes 3145736 | tf_op jit(solution)/shard_map/ppermute | solution.py:323
  392.0 48.0 %collective-permute-start.28 = (bf16[1024,512]{1,0:T(8,128)(2,1)S(1)}, bf16[1024,512]{1,0:T(8,128)(2,1)S(1)}, u32[]{:S(2)}, u32[]{:S(2)}) collective-permute-start(bf16[1024,512]{1,0:T(8,128)(2,1)S(1)} %copy-done.16), channel_id=1, source_target_pairs={{0,2},{1,3},{2,0},{3,1},{4,6},{5,7},{6,4},{7,5},{8,10},{9,11},{10,... | collective-permute-start | bytes 3145736 | tf_op jit(solution)/shard_map/ppermute | solution.py:323
  410.1 34.9 %collective-permute-start.40 = (bf16[256,1536]{1,0:T(8,128)(2,1)S(1)}, bf16[256,1536]{1,0:T(8,128)(2,1)S(1)}, u32[]{:S(2)}, u32[]{:S(2)}) collective-permute-start(bf16[256,1536]{1,0:T(8,128)(2,1)S(1)} %pad_maximum_fusion.7), channel_id=1, source_target_pairs={{0,8},{8,0},{16,24},{24,16},{1,9},{9,1},{17,25},{25,17},{2,10},{10... | collective-permute-start | bytes 2359304 | tf_op jit(solution)/shard_map/ppermute | solution.py:323
  410.8 34.2 %collective-permute-start.41 = (bf16[256,1536]{1,0:T(8,128)(2,1)S(1)}, bf16[256,1536]{1,0:T(8,128)(2,1)S(1)}, u32[]{:S(2)}, u32[]{:S(2)}) collective-permute-start(bf16[256,1536]{1,0:T(8,128)(2,1)S(1)} %pad_maximum_fusion.6), channel_id=1, source_target_pairs={{0,16},{8,24},{16,0},{24,8},{1,17},{9,25},{17,1},{25,9},{2,18},{10... | collective-permute-start | bytes 2359304 | tf_op jit(solution)/shard_map/ppermute | solution.py:323
  (74 other events, 785.6 us)
Sparse Core Ops, SparseCore 0:
  64.3 61.0 all-gather.4
  127.2 26.4 all-gather.2
  231.1 92.9 reduce-scatter.3
  344.0 28.2 reduce-scatter.5
  375.1 69.3 reduce-scatter.7

commit v3 on v2

--- a/solution.py
+++ b/solution.py
@@ -315,7 +315,8 @@
 wide = jnp.float32
 tile = 256
 megabyte = 1024 * 1024
-pace = 16
+pace = {"attend_back": 1, "mix": 1}
+room = {"project": 56, "mix": 56}
 
 
 def trade(x, axis, bit):
@@ -352,18 +353,22 @@
     return jnp.concatenate(corner, axis=0)
 
 
-def scatter_plane(total, axis, dim):
+def scatter_plane(total, axis, dim, *gate):
     place = lax.axis_index(axis)
     own, near, far, corner = (block_of(total, place ^ k, dim, 4) for k in range(4))
     half = own.shape[0] // 2
     upper = trade(corner[:half].astype(low), axis, 1)
     lower = trade(corner[half:].astype(low), axis, 2)
+    upper, lower = after(upper, *gate), after(lower, *gate)
     add = lambda a, b: (a.astype(wide) + b.astype(wide)).astype(low)
     far = jnp.concatenate([add(far[:half], upper), far[half:].astype(low)], axis=0)
     near = jnp.concatenate([near[:half].astype(low), add(near[half:], lower)], axis=0)
-    far_in = trade(far, axis, 2)
-    near_in = trade(near, axis, 1)
-    return (own.astype(wide) + near_in.astype(wide) + far_in.astype(wide)).astype(low), (far, near)
+    return (own, trade(near, axis, 1), trade(far, axis, 2)), (far, near)
+
+
+def close_plane(parts, *gate):
+    own, near, far = (part.astype(wide) for part in after(parts, *gate))
+    return (own + near + far).astype(low)
 
 
 def half_of(x, index, dim):
@@ -406,7 +411,9 @@
     return pl.BlockSpec((rows, width), lambda step, scalars: (0, jnp.maximum(step - first, 0)))
 
 
-def call(kernel, name, steps, in_specs, out_specs, out_shape, operands, flops, moved, scratch=(), exps=0):
+def call(
+    kernel, name, steps, in_specs, out_specs, out_shape, operands, flops, moved, scratch=(), exps=0
+):
     return pl.pallas_call(
         kernel,
         grid_spec=pltpu.PrefetchScalarGridSpec(
@@ -417,9 +424,11 @@
             scratch_shapes=list(scratch),
         ),
         out_shape=out_shape,
-        compiler_params=pltpu.CompilerParams(vmem_limit_bytes=56 * megabyte),
+        compiler_params=pltpu.CompilerParams(vmem_limit_bytes=room.get(name, 28) * megabyte),
         cost_estimate=pl.CostEstimate(
-            flops=flops * pace, bytes_accessed=moved * pace, transcendentals=exps * pace
+            flops=int(flops * pace.get(name, 16)),
+            bytes_accessed=int(moved * pace.get(name, 16)),
+            transcendentals=int(exps * pace.get(name, 16)),
         ),
         name=name,
     )(*operands)
@@ -437,23 +446,27 @@
     pieces, terms = refs[:4], refs[4:8]
     attn_out, ffn_out, stats_out, terms_out = refs[8:]
     width = 8 * tile
-    parts = [piece[...].astype(wide) for piece in pieces]
-    total = sum(jnp.sum(part, axis=1, keepdims=True) for part in parts)
-    mean = total * (1.0 / width)
-    spread = sum(jnp.sum((part - mean) * (part - mean), axis=1, keepdims=True) for part in parts)
-    inverse = lax.rsqrt(spread * (1.0 / width) + norm_epsilon)
-    for k in range(4):
-        block = scalars[2] ^ k
-        for half in range(2):
-            side = scalars[0] if half == 0 else 1 - scalars[0]
-            source = place_of(side, tile)
-            columns = place_of(4 * half + block, tile)
-            normed = (pieces[k][:, source].astype(wide) - mean) * inverse
-            term = terms[k][:, source].astype(wide)
-            attn_out[:, columns] = (normed * term[0:1] + term[1:2]).astype(low)
-            ffn_out[:, columns] = (normed * term[2:3] + term[3:4]).astype(low)
-    lane = lax.broadcasted_iota(jnp.int32, stats_out.shape, 1)
-    stats_out[...] = jnp.where(lane < 64, mean, inverse)
+    lane = lax.broadcasted_iota(jnp.int32, (strip, 128), 1)
+    for start in range(0, stats_out.shape[0], strip):
+        here = slice(start, start + strip)
+        parts = [piece[here, :].astype(wide) for piece in pieces]
+        total = sum(jnp.sum(part, axis=1, keepdims=True) for part in parts)
+        mean = total * (1.0 / width)
+        spread = sum(
+            jnp.sum((part - mean) * (part - mean), axis=1, keepdims=True) for part in parts
+        )
+        inverse = lax.rsqrt(spread * (1.0 / width) + norm_epsilon)
+        for k in range(4):
+            block = scalars[2] ^ k
+            for half in range(2):
+                side = scalars[0] if half == 0 else 1 - scalars[0]
+                source = place_of(side, tile)
+                columns = place_of(4 * half + block, tile)
+                normed = (pieces[k][here, source].astype(wide) - mean) * inverse
+                term = terms[k][:, source].astype(wide)
+                attn_out[here, columns] = (normed * term[0:1] + term[1:2]).astype(low)
+                ffn_out[here, columns] = (normed * term[2:3] + term[3:4]).astype(low)
+        stats_out[here, :] = jnp.where(lane < 64, mean, inverse)
 
     @pl.when(pl.program_id(0) == 0)
     def _():
@@ -464,9 +477,9 @@
                 terms_out[:, columns] = terms[k][0:8, place_of(side, tile)].astype(wide)
 
 
-def norm(scalars, pieces, terms):
-    rows, width = pieces[0].shape
-    term = fixed(terms[0].shape)
+def norm(scalars, pieces, rows):
+    width = pieces[0].shape[1]
+    term = pl.BlockSpec((16, width), lambda step, scalars: (rows // 16, 0))
     return call(
         norm_kernel,
         "norm",
@@ -479,7 +492,7 @@
             shaped(rows, 128, kind=wide),
             shaped(8, 4 * width, kind=wide),
         ],
-        (scalars, *pieces, *terms),
+        (scalars, *pieces, *pieces),
         rows * width * 40,
         rows * width * 24,
     )
@@ -519,63 +532,65 @@
     )
 
 
+strip = 32
+
+
+def strips(first, rows):
+    return [(at, first + at, first + at + strip) for at in range(0, rows, strip)]
+
+
 def double(rows_in, own, other):
     half = rows_in.shape[1] // 2
     return contract(rows_in[:, :half], own, (1, 0)) + contract(rows_in[:, half:], other, (1, 0))
 
 
 def heads_kernel(scalars, rows_in, own, other, shift_row, cosine, sine, mine, theirs):
-    step = pl.program_id(0)
-    joined = double(rows_in, own[...], other[...]) + shift_row[0:1, :]
-    part = lax.rem(step, 3)
-
-    def write(vectors):
-        @pl.when(step < 3)
-        def _():
-            theirs[0] = vectors.astype(low)
-
-        @pl.when(step >= 3)
-        def _():
-            mine[0] = vectors.astype(low)
-
-    @pl.when(part < 2)
-    def _():
-        write(turn(joined, cosine[...], sine[...], 1.0))
-
-    @pl.when(part == 2)
-    def _():
-        write(joined)
+    def run(out):
+        for first in range(0, rows_in.shape[0], tile):
+            product = double(rows_in.at[first : first + tile, :], own[...], other[...])
+            for at, start, stop in strips(first, tile):
+                joined = product[at : at + strip] + shift_row[0:1, :]
+                for part in range(3):
+                    vectors = joined[:, part * HEAD_DIM : (part + 1) * HEAD_DIM]
+                    if part < 2:
+                        vectors = turn(vectors, cosine[start:stop, :], sine[start:stop, :], 1.0)
+                    out[part, start:stop, :] = vectors.astype(low)
+
+    pl.when(pl.program_id(0) == 0)(partial(run, theirs))
+    pl.when(pl.program_id(0) == 1)(partial(run, mine))
 
 
 def heads(scalars, attn_in, weights, shift_row, cosine, sine):
     rows, width = attn_in.shape
+    columns = 3 * HEAD_DIM
 
     def column(step, scalars):
-        return jnp.where(step < 3, 1 - scalars[0], scalars[0]) * 3 + lax.rem(step, 3)
-
-    weight = pl.BlockSpec((width // 2, HEAD_DIM), lambda step, scalars: (0, column(step, scalars)))
-    shift = pl.BlockSpec((1, HEAD_DIM), lambda step, scalars: (0, column(step, scalars)))
-    last = lambda step, scalars: (jnp.maximum(step - 3, 0), 0, 0)
-    early = lambda step, scalars: (jnp.minimum(step, 2), 0, 0)
+        return 0, jnp.where(step == 0, 1 - scalars[0], scalars[0])
+
+    weight = pl.BlockSpec((width // 2, columns), column)
     return call(
         heads_kernel,
         "heads",
-        6,
-        [fixed(attn_in.shape), weight, weight, shift, fixed((rows, 128)), fixed((rows, 128))],
-        [pl.BlockSpec((1, rows, HEAD_DIM), last), pl.BlockSpec((1, rows, HEAD_DIM), early)],
+        2,
+        [fixed(attn_in.shape), weight, weight, pl.BlockSpec((1, columns), column)]
+        + [fixed((rows, 128))] * 2,
+        [kept((3, rows, HEAD_DIM))] * 2,
         [shaped(3, rows, HEAD_DIM)] * 2,
         (scalars, attn_in, *weights, shift_row, cosine, sine),
-        12 * rows * width * HEAD_DIM,
-        2 * (rows * width + 6 * width * HEAD_DIM + 6 * rows * HEAD_DIM),
+        4 * rows * width * columns,
+        2 * (rows * width + 2 * width * columns + 2 * rows * columns),
     )
 
 
 def expand_kernel(scalars, rows_in, own, other, shift_row, hidden, slope):
-    pre = double(rows_in, own[...], other[...]) + shift_row[0:1, :]
-    phi = 0.5 + 0.5 * lax.erf(pre * math.sqrt(0.5))
-    density = jnp.exp(pre * pre * -0.5) * (1.0 / math.sqrt(2.0 * math.pi))
-    hidden[...] = (pre * phi).astype(low)
-    slope[...] = (phi + pre * density).astype(low)
+    for first in range(0, rows_in.shape[0], tile):
+        product = double(rows_in.at[first : first + tile, :], own[...], other[...])
+        for at, start, stop in strips(first, tile):
+            pre = product[at : at + strip] + shift_row[0:1, :]
+            phi = 0.5 + 0.5 * lax.erf(pre * math.sqrt(0.5))
+            density = jnp.exp(pre * pre * -0.5) * (1.0 / math.sqrt(2.0 * math.pi))
+            hidden[start:stop, :] = (pre * phi).astype(low)
+            slope[start:stop, :] = (phi + pre * density).astype(low)
 
 
 def expand(scalars, ffn_in, weights, shift_row):
@@ -595,88 +610,88 @@
     )
 
 
-def project_kernel(scalars, mine, theirs, hidden, dense_own, dense_other, down_own, down_other, out):
-    for half, dense, down in ((0, dense_own, down_own), (1, dense_other, down_other)):
-        total = contract(hidden[...], down[...], (1, 0))
-        total += contract(mine[...], dense[place_of(scalars[0], HEAD_DIM), :], (1, 0))
-        total += contract(theirs[...], dense[place_of(1 - scalars[0], HEAD_DIM), :], (1, 0))
+def project_kernel(scalars, mine, theirs, hidden, own, other, out):
+    heads_rows = 2 * HEAD_DIM
+    for half, weight in enumerate((own, other)):
+        total = contract(hidden[...], weight[heads_rows:, :], (1, 0))
+        total += contract(mine[...], weight[place_of(scalars[0], HEAD_DIM), :], (1, 0))
+        total += contract(theirs[...], weight[place_of(1 - scalars[0], HEAD_DIM), :], (1, 0))
         out[:, half * tile : (half + 1) * tile] = total.astype(out.dtype)
 
 
-def project(scalars, mine, theirs, hidden, dense, down):
+def project(scalars, mine, theirs, hidden, outward):
     rows = hidden.shape[0]
-    depth = dense[0].shape[0] + down[0].shape[0]
-    weight = lambda x: by_column(x.shape[0], tile)
+    depth = outward.shape[0]
     return call(
         project_kernel,
         "project",
         4,
         [fixed(mine.shape), fixed(mine.shape), fixed(hidden.shape)]
-        + [weight(x) for x in (*dense, *down)],
+        + [
+            pl.BlockSpec((depth, tile), lambda step, scalars: (0, 2 * step + scalars[0])),
+            pl.BlockSpec((depth, tile), lambda step, scalars: (0, 2 * step + 1 - scalars[0])),
+        ],
         [by_column(rows, 2 * tile)],
         [shaped(rows, 8 * tile)],
-        (scalars, mine, theirs, hidden, *dense, *down),
+        (scalars, mine, theirs, hidden, outward, outward),
         16 * rows * tile * depth,
         2 * (rows * 8 * tile + depth * 8 * tile + rows * depth),
     )[0]
 
 
 def hidden_back_kernel(scalars, *refs):
-    pieces, (slope, dense_own, dense_other, down_own, down_other) = refs[:4], refs[4:9]
-    cotangent, pre_grad, mine, theirs, bias_grad = refs[9:]
+    pieces, (slope, weight) = refs[:4], refs[4:6]
+    cotangent, pre_grad, mine, theirs, bias_grad, natural, both = refs[6:]
     step = pl.program_id(0)
-    half = cotangent.shape[1] // 2
+    width = pieces[0].shape[1]
 
     @pl.when(step == 0)
     def _():
         for k in range(4):
             block = scalars[2] ^ k
+            natural[:, place_of(block, width)] = pieces[k][...]
             own, other = own_first(pieces[k], scalars[0])
             cotangent[:, place_of(block, tile)] = own
             cotangent[:, place_of(4 + block, tile)] = other
 
-    def back(own, other):
-        return contract(cotangent[:, :half], own[...], (1, 1)) + contract(
-            cotangent[:, half:], other[...], (1, 1)
-        )
+    rows = natural.shape[0]
 
     @pl.when(step == 0)
     def _():
-        theirs[...] = back(dense_own, dense_other).astype(low)
-
-    @pl.when(step == 1)
+        both[...] = contract(natural[...], weight[...], (1, 1)).astype(low)
+        theirs[...] = both[:, place_of(1 - scalars[0], HEAD_DIM)]
+        mine[...] = both[:, place_of(scalars[0], HEAD_DIM)]
+
+    @pl.when(step >= 1)
     def _():
-        mine[...] = back(dense_own, dense_other).astype(low)
-
-    @pl.when(step >= 2)
-    def _():
-        grad = (back(down_own, down_other) * slope[...].astype(wide)).astype(low)
-        pre_grad[...] = grad
-        bias_grad[...] = fold_rows(grad.astype(wide))
-
-
-def hidden_back(scalars, pieces, slope, dense, down):
+        total = jnp.zeros((8, weight.shape[0]), wide)
+        for first in range(0, rows, tile):
+            grad = contract(natural[first : first + tile, :], weight[...], (1, 1))
+            for at, start, stop in strips(first, tile):
+                scaled = grad[at : at + strip] * slope[start:stop, :].astype(wide)
+                scaled = scaled.astype(low)
+                pre_grad[start:stop, :] = scaled
+                total += fold_rows(scaled.astype(wide))
+        bias_grad[...] = total
+
+
+def hidden_back(scalars, pieces, slope, outward):
     rows, width = pieces[0].shape
-    hidden = down[0].shape[0]
-    heads_weight = pl.BlockSpec(
-        (HEAD_DIM, 2 * width),
-        lambda step, scalars: (jnp.where(step == 0, 1 - scalars[0], scalars[0]), 0),
-    )
-    weight = pl.BlockSpec(
-        (tile, 2 * width), lambda step, scalars: (jnp.maximum(step - 2, 0), 0)
-    )
+    depth = outward.shape[0]
+    hidden = depth - 2 * HEAD_DIM
+
+    weight = pl.BlockSpec((2 * tile, 4 * width), lambda step, scalars: (step, 0))
     return call(
         hidden_back_kernel,
         "hidden_back",
-        2 + hidden // tile,
-        [fixed((rows, width))] * 4
-        + [by_column(rows, tile, 2), heads_weight, heads_weight, weight, weight],
+        depth // (2 * tile),
+        [fixed((rows, width))] * 4 + [by_column(rows, 2 * tile, 1), weight],
         [
             kept((rows, 4 * width)),
-            by_column(rows, tile, 2),
+            by_column(rows, 2 * tile, 1),
             kept((rows, HEAD_DIM)),
             kept((rows, HEAD_DIM)),
-            by_column(8, tile, 2),
+            by_column(8, 2 * tile, 1),
         ],
         [
             shaped(rows, 4 * width),
@@ -685,9 +700,10 @@
             shaped(rows, HEAD_DIM),
             shaped(8, hidden, kind=wide),
         ],
-        (scalars, *pieces, slope, *dense, *down),
-        8 * rows * width * (2 * HEAD_DIM + hidden),
-        rows * width * 16 + 8 * width * hidden + rows * hidden * 4,
+        (scalars, *pieces, slope, outward),
+        8 * rows * width * depth,
+        rows * width * 16 + 8 * width * depth + rows * hidden * 4,
+        scratch=[pltpu.VMEM((rows, 4 * width), low), pltpu.VMEM((rows, 2 * HEAD_DIM), low)],
     )
 
 
@@ -695,45 +711,50 @@
     scalars, mine, theirs, pre_grad, qkv_own, qkv_other, up_own, up_other, terms_own, terms_other,
     stats, first_piece, second_piece, first_out, second_out, sums_own, sums_other, row_sums
 ):
-    mean = stats[:, 0:1]
-    inverse = stats[:, 64:65]
     step = pl.program_id(0)
-
-    def run(piece, out):
-        plain = None
+    rows = pre_grad.shape[0]
+    lane = lax.broadcasted_iota(jnp.int32, (strip, 128), 1)
+
+    def run(piece, out, fresh):
         for half, qkv, up, terms, sums in (
             (0, qkv_own, up_own, terms_own, sums_own),
             (1, qkv_other, up_other, terms_other, sums_other),
         ):
-            attn = contract(mine[...], qkv[:, place_of(scalars[0], 3 * HEAD_DIM)], (1, 1))
-            attn += contract(theirs[...], qkv[:, place_of(1 - scalars[0], 3 * HEAD_DIM)], (1, 1))
-            ffn = contract(pre_grad[...], up[...], (1, 1))
             side = scalars[0] if half == 0 else 1 - scalars[0]
-            normed = (piece[:, place_of(side, tile)].astype(wide) - mean) * inverse
-            mixed = attn * terms[0:1, :] + ffn * terms[2:3, :]
-            sums[0:8, :] = fold_rows(attn * normed)
-            sums[8:16, :] = fold_rows(attn)
-            sums[16:24, :] = fold_rows(ffn * normed)
-            sums[24:32, :] = fold_rows(ffn)
-            out[:, half * tile : (half + 1) * tile] = mixed.astype(out.dtype)
-            weighed = mixed * normed
-            here = mixed[:, :128] + mixed[:, 128:], weighed[:, :128] + weighed[:, 128:]
-            plain = here if plain is None else (plain[0] + here[0], plain[1] + here[1])
-        lane = lax.broadcasted_iota(jnp.int32, row_sums.shape, 1)
-        together = jnp.where(
-            lane < 64,
-            jnp.sum(plain[0], axis=1, keepdims=True),
-            jnp.sum(plain[1], axis=1, keepdims=True),
-        )
-        return together
-
-    @pl.when(step == 0)
-    def _():
-        row_sums[...] = run(first_piece, first_out)
-
-    @pl.when(step == 1)
-    def _():
-        row_sums[...] += run(second_piece, second_out)
+            totals = [jnp.zeros((8, tile), wide)] * 4
+            attn_gain, ffn_gain = terms[0:1, :], terms[2:3, :]
+            for first in range(0, rows, tile):
+                here = slice(first, first + tile)
+                attn_part = contract(
+                    mine[here, :], qkv[:, place_of(scalars[0], 3 * HEAD_DIM)], (1, 1)
+                ) + contract(
+                    theirs[here, :], qkv[:, place_of(1 - scalars[0], 3 * HEAD_DIM)], (1, 1)
+                )
+                ffn_part = contract(pre_grad[here, :], up[...], (1, 1))
+                for at, start, stop in strips(first, tile):
+                    attn, ffn = attn_part[at : at + strip], ffn_part[at : at + strip]
+                    mean, inverse = stats[start:stop, 0:1], stats[start:stop, 64:65]
+                    held = piece[start:stop, place_of(side, tile)].astype(wide)
+                    normed = (held - mean) * inverse
+                    mixed = attn * attn_gain + ffn * ffn_gain
+                    weighed = mixed * normed
+                    parts = (attn * normed, attn, ffn * normed, ffn)
+                    totals = [total + fold_rows(part) for total, part in zip(totals, parts)]
+                    out[start:stop, half * tile : (half + 1) * tile] = mixed.astype(out.dtype)
+                    across = jnp.where(
+                        lane < 64,
+                        jnp.sum(mixed[:, :128] + mixed[:, 128:], axis=1, keepdims=True),
+                        jnp.sum(weighed[:, :128] + weighed[:, 128:], axis=1, keepdims=True),
+                    )
+                    if fresh and half == 0:
+                        row_sums[start:stop, :] = across
+                    else:
+                        row_sums[start:stop, :] += across
+            for place, total in enumerate(totals):
+                sums[8 * place : 8 * place + 8, :] = total
+
+    pl.when(step == 0)(partial(run, first_piece, first_out, True))
+    pl.when(step == 1)(partial(run, second_piece, second_out, False))
 
 
 def mix(scalars, mine, theirs, pre_grad, qkv, up, terms, stats, pieces, order, kinds):
@@ -966,6 +987,8 @@
     width = 4 * held_width
     half = width // 2
 
+    norm_rows = jnp.stack([attn_norm_gain, attn_norm_bias, ffn_norm_gain, ffn_norm_bias] * 4)
+    held = jnp.concatenate([residual, norm_rows], axis=0)
     inward = jnp.concatenate([qkv_weight, up_weight], axis=1)
     split = qkv_weight.shape[1]
     other_depth = trade(path_depth, "ctx", 1)
@@ -974,31 +997,27 @@
     scalars = jnp.stack([core, trunk_end, line, plane]).astype(jnp.int32)
     qkv_shift = qkv_bias.astype(wide)[None, :]
     up_shift = up_bias.astype(wide)[None, :]
-    inward_near, inward_far, inward, cosine, sine, info = meet(
-        trade(inward, "fsdp", 1), trade(inward, "fsdp", 2), inward, cosine, sine, info
-    )
+    near, far, cosine, sine, info = meet(
+        trade(held, "tp", 1), trade(held, "tp", 2), cosine, sine, info
+    )
+    inward_near, inward_far, inward = meet(
+        trade(inward, "fsdp", 1), trade(inward, "fsdp", 2), inward, near
+    )[:3]
     middle = inward.shape[0] // 2
     upper_corner = trade(inward_far[:middle], "fsdp", 1)
     lower_corner = trade(inward_near[middle:], "fsdp", 2)
-    near, far = meet(
-        trade(residual, "tp", 1), trade(residual, "tp", 2), inward_near, inward_far
-    )[:2]
     corner = trade(far, "tp", 1)
-    norm_rows = jnp.stack([attn_norm_gain, attn_norm_bias, ffn_norm_gain, ffn_norm_bias] * 4)
-    first_rows = after(norm_rows, far)
-    terms = [trade(first_rows, "tp", bit) for bit in (1, 2, 3)]
-    upper_corner, lower_corner, corner, *terms = meet(upper_corner, lower_corner, corner, *terms)
+    upper_corner, lower_corner, corner = meet(upper_corner, lower_corner, corner)
     qkv_own, up_own = assemble(
         scalars, (inward, inward_near, inward_far), (upper_corner, lower_corner), split
     )
-    terms = (norm_rows, *terms)
-    pieces = (residual, near, far, corner)
+    pieces = (held, near, far, corner)
 
     def both_cores(own, *gate):
         return own, trade(after(own, *gate), "ctx", 1)
 
-    def offloaded(weight, dim):
-        return lax.all_gather(after(weight, near), "fsdp", axis=dim, tiled=True)
+    outward = jnp.concatenate([dense_weight, down_weight], axis=0)
+    outward = lax.all_gather(after(outward, upper_corner), ("fsdp", "ctx"), axis=1, tiled=True)
 
     qkv = both_cores(qkv_own)
     up = both_cores(up_own)
@@ -1006,23 +1025,21 @@
     grad_near = trade(first_grad, "tp", 1)
     grad_far = trade(first_grad, "tp", 2)
 
-    attn_in, ffn_in, stats, terms = norm(scalars, pieces, terms)
+    attn_in, ffn_in, stats, terms = norm(scalars, pieces, rows)
     mine, theirs = heads(scalars, attn_in, qkv, qkv_shift, cosine, sine)
     theirs = trade(theirs, "ctx", 1)
     hidden, slope = expand(after(scalars, mine), ffn_in, up, up_shift)
     grad_corner = trade(after(grad_far, slope), "tp", 1)
-    down = both_cores(offloaded(down_weight, 1), slope)
     packed, attended, twin_attended, log_total = attend(
         after(scalars, slope, grad_near, grad_far), mine, theirs, info
     )
-    dense = both_cores(offloaded(dense_weight, 1), attended)
     other_attended = trade(twin_attended, "ctx", 1)
-    chip_out = project(scalars, attended, other_attended, hidden, dense, down)
+    chip_out = project(scalars, attended, other_attended, hidden, outward)
     shared_out = lax.psum_scatter(chip_out, "tp", scatter_dimension=1, tiled=True)
 
     grad_pieces = (out_grad, grad_near, grad_far, grad_corner)
     cotangent, pre_grad, head_grad, other_grad, up_bias_rows = hidden_back(
-        after(scalars, chip_out), grad_pieces, slope, dense, down
+        after(scalars, chip_out), grad_pieces, slope, outward
     )
     other_grad = trade(other_grad, "ctx", 1)
 
@@ -1038,36 +1055,32 @@
     both_attended = join_cores(attended, other_attended, core, 1)
     down_other = outer(after(hidden, pre_grad), cotangent[:, half:]).astype(low)
     down_arrived = trade(down_other, "ctx", 1)
-    dense_other = outer(after(both_attended, down_other), cotangent[:, half:]).astype(low)
+    up_other = outer(after(ffn_in, down_other)[:, half:], pre_grad).astype(low)
+    up_arrived = trade(up_other, "ctx", 1)
+    down_total = add_low(outer(after(hidden, up_other), cotangent[:, :half]), down_arrived)
+    joined_grad, twin_grad, qkv_bias_rows = attend_back(
+        after(scalars, down_total), packed, head_grad, other_grad, log_total, cosine, sine, info
+    )
+    other_joined = trade(twin_grad, "ctx", 1)
+    down_parts, down_hop = scatter_plane(down_total, "fsdp", 1, joined_grad)
+    dense_other = outer(after(both_attended, joined_grad, *down_hop), cotangent[:, half:]).astype(low)
     dense_arrived = trade(dense_other, "ctx", 1)
-    joined_grad, twin_grad, qkv_bias_rows = attend_back(
-        after(scalars, dense_other), packed, head_grad, other_grad, log_total, cosine, sine, info
-    )
-    other_joined = trade(twin_grad, "ctx", 1)
-    down_total = add_low(
-        outer(after(hidden, joined_grad), cotangent[:, :half]), down_arrived
-    )
+    up_total = add_low(outer(after(ffn_in, dense_other)[:, :half], pre_grad), up_arrived)
+    up_grad = to_owner(up_total, 0)
     dense_total = add_low(
-        outer(after(both_attended, down_total), cotangent[:, :half]), dense_arrived
+        outer(after(both_attended, up_total, other_joined), cotangent[:, :half]), dense_arrived
     )
     dense_grad = to_owner(dense_total, 1)
     mix_in = (joined_grad, other_joined, pre_grad, qkv, up, terms, stats, pieces)
     *leave, sums_a, sums_b, row_a = mix(
         after(scalars, dense_total), *mix_in, (3, 1), (low, low)
     )
-    mixed_side, mixed_near = trade(leave[0], "tp", 1), trade(leave[1], "tp", 1)
-    down_grad, down_hop = scatter_plane(down_total, "fsdp", 1)
+    mixed_side = trade(leave[0], "tp", 1)
     *stay_mixed, sums_c, sums_d, row_b = mix(
-        after(scalars, leave[0], *down_hop), *mix_in, (2, 0), (wide, wide)
+        after(scalars, leave[0], shared_out), *mix_in, (2, 0), (wide, wide)
     )
     passed = (stay_mixed[0] + mixed_side.astype(wide)).astype(low)
-    far_mixed = trade(passed, "tp", 2)
     both_joined = join_cores(joined_grad, other_joined, core, 1)
-    up_other = outer(
-        after(ffn_in, stay_mixed[0], passed, down_grad, shared_out)[:, half:], pre_grad
-    ).astype(low)
-    up_arrived = trade(up_other, "ctx", 1)
-
     shared_out = shared_out.astype(wide)
     shared_out = join_cores(shared_out[:, :tile], shared_out[:, tile:], core, 1)
     output = (
@@ -1080,15 +1093,15 @@
     gather_sums = lambda own, other: jnp.stack([fold(own), fold(other)], axis=2).reshape(4, 2, 2 * tile)
     leaving, norm_sums = gather_sums(sums_a, sums_b), gather_sums(sums_c, sums_d)
     hop_side = trade(jnp.concatenate([leaving.reshape(-1), row_total.reshape(-1)]), "tp", 1)
-    qkv_other = outer(after(attn_in, up_other, hop_side)[:, half:], both_joined).astype(low)
-    qkv_arrived = trade(qkv_other, "ctx", 1)
     norm_sums = norm_sums + hop_side[: 8 * held_width].reshape(norm_sums.shape)
     row_total = row_total + hop_side[8 * held_width :].reshape(row_total.shape)
     hop_far = trade(jnp.concatenate([norm_sums[:, 0].reshape(-1), row_total.reshape(-1)]), "tp", 2)
-    up_total = add_low(
-        outer(after(ffn_in, qkv_other, hop_far)[:, :half], pre_grad), up_arrived
-    )
-    up_grad = to_owner(up_total, 0)
+    qkv_other = outer(
+        after(attn_in, stay_mixed[0], passed, hop_side, down_parts)[:, half:], both_joined
+    ).astype(low)
+    qkv_arrived = trade(qkv_other, "ctx", 1)
+    far_mixed = trade(after(passed, hop_far), "tp", 2)
+    mixed_near = trade(after(leave[1], hop_far), "tp", 1)
     norm_total = norm_sums[:, 1] + hop_far[: 4 * held_width].reshape(4, held_width)
     row_total = row_total + hop_far[4 * held_width :].reshape(row_total.shape)
     row_means = row_total / width
@@ -1103,10 +1116,14 @@
         ]
     )
     columns = columns + trade(columns, "fsdp", 1)
+    down_grad = close_plane(down_parts, qkv_other)
     qkv_total = add_low(
-        outer(after(attn_in, up_total, dense_grad)[:, :half], both_joined), qkv_arrived
+        outer(after(attn_in, qkv_other, down_grad, hop_far)[:, :half], both_joined), qkv_arrived
     )
     columns = columns + trade(columns, "fsdp", 2)
+    qkv_parts, qkv_hop = scatter_plane(qkv_total, "fsdp", 0)
+    qkv_grad = close_plane(qkv_parts)
+    dense_grad = after(dense_grad, *qkv_hop)
     other_columns = trade(columns, "ctx", 1)
     cut = columns.shape[0] - qkv_bias.shape[0] // 2
     qkv_bias_grad = join_cores(columns[cut:], other_columns[cut:], core, 0)
@@ -1115,7 +1132,6 @@
     out_bias_grad = together[width : width + held_width]
     up_bias_grad = together[width + held_width :]
 
-    qkv_grad, qkv_hop = scatter_plane(qkv_total, "fsdp", 0)
 
     far_mixed = after(far_mixed, mixed_near, other_columns, *qkv_hop)
     shared_mixed = stay_mixed[1] + mixed_near.astype(wide) + far_mixed.astype(wide)

time: 464 us -> 417 us (0.90)
  waiting for transfers between devices: 149 us -> 108 us
  Pallas kernels: 152 us -> 135 us
  other arithmetic: 30.7 us -> 40.2 us
  local copies, waits for them, and re-layouts: 22.4 us -> 27.7 us
    ppermute x42 -> x37, waiting for transfers between devices: 149 us -> 101 us  [trade(): return lax.ppermute(x, axis, [(i, i ^ bit) for i in range(peers)])]
    pallas_call x10, Pallas kernels: 152 us -> 135 us  [call(): pl.pallas_call(kernel, grid_spec=pltpu.PrefetchScalarGridSpec(num_scalar_...]
    all_gather x2 -> x1, waiting for transfers between devices: 0.01 us -> 6.7 us  [on_device_split(): lax.all_gather(after(outward, upper_corner), ('fsdp', 'ctx'), axis=1, til...]
    unnamed x108 -> x130, local copies, waits for them, and re-layouts: 13.1 us -> 15.8 us
    ppermute x42 -> x37, starting transfers between devices: 34.5 us -> 33.2 us  [trade(): return lax.ppermute(x, axis, [(i, i ^ bit) for i in range(peers)])]
  transfers between devices with their start and end apart: 47 -> 41, of which waited for: 20 -> 16; matrix products, arithmetic and copies ran while one was open for 17% -> 23% of each run, Pallas kernels for 29% -> 27%
where the time goes in v3:
time: 417 us; the launch traced here: 413 us
  Pallas kernels  135 us (32%)
  waiting for transfers between devices  108 us (26%)
  matrix products  53.2 us (13%)
  other arithmetic  40.2 us (10%)
  starting transfers between devices  33.6 us (8%)
  local copies, waits for them, and re-layouts  27.7 us (7%)
  between operations  15 us (4%)
    pallas_call x10, Pallas kernels, call(): pl.pallas_call(kernel, grid_spec=pltpu.PrefetchScalarGridSpec(num_scalar_...  135 us
    ppermute x37, waiting for transfers between devices, trade(): return lax.ppermute(x, axis, [(i, i ^ bit) for i in range(peers)])  101 us
    dot_general x8, matrix products, contract(): lax.dot_general(a, b, ((dims[:1], dims[1:]), ((), ())), preferred_element...  53.2 us
    ppermute x37, starting transfers between devices, trade(): return lax.ppermute(x, axis, [(i, i ^ bit) for i in range(peers)])  33.2 us
    unnamed x130, local copies, waits for them, and re-layouts  15.8 us
  transfers between devices with their start and end apart: 41, of which 16 were waited for; matrix products, arithmetic and copies ran while one was open for 23% of the time, Pallas kernels for 27%

profile of v3, /device:TPU:0, one launch (start us, length us, event | category | flops | bytes accessed | tf_op | source)
XLA Modules:
  0.0 413.1 jit_solution(17758075749742107589)
XLA Ops:
  20.8 5.5 %multiply_sine_fusion = (f32[2048,128]{1,0:T(8,128)}, f32[2048,128]{1,0:T(8,128)}) fusion(f32[128]{0:T(128)S(1)} %compare_select_fusion, f32[2048]{0:T(1024)S(1)} %add_convert_fusion.11), kind=kLoop, calls=%fused_computation.37 | loop fusion | flops 262144 | bytes 2105856 | tf_op jit(solution)/shard_map/sin | solution.py:961
  26.3 36.6 %collective-permute-done.refs_1_.refs_5_.second_piece = bf16[1040,512]{1,0:T(8,128)(2,1)S(1)} collective-permute-done((bf16[1040,512]{1,0:T(8,128)(2,1)S(1)}, bf16[1040,512]{1,0:T(8,128)(2,1)S(1)}, u32[]{:S(2)}, u32[]{:S(2)}) %collective-permute-start) | collective-permute-done | bytes 1064992 | tf_op jit(solution)/shard_map/ppermute | solution.py:324
  71.3 16.6 %collective-permute-done.7.refs_3_.refs_7_.first_piece = bf16[1040,512]{1,0:T(8,128)(2,1)} collective-permute-done((bf16[1040,512]{1,0:T(8,128)(2,1)S(1)}, bf16[1040,512]{1,0:T(8,128)(2,1)}, u32[]{:S(2)}, u32[]{:S(2)}) %collective-permute-start.7) | collective-permute-done | bytes 1064992 | tf_op jit(solution)/shard_map/ppermute | solution.py:324
  90.9 6.0 %assemble.1 = (bf16[1024,1536]{1,0:T(8,128)(2,1)}, bf16[1024,2048]{1,0:T(8,128)(2,1)S(1)}) custom-call(s32[4]{0:T(128)S(1)} %pad_add_fusion.scalars, bf16[256,3584]{1,0:T(8,128)(2,1)} %constant_dynamic-update-slice_fusion.own, bf16[256,3584]{1,0:T(8,128)(2,1)} %collective-permute-done.3.near, bf16[256,3584]{1,0:T(8,128)(2,1)} %collective-permute-done.4.far, ...), custom_call_target="tpu_custom_call" | custom-call | flops 14680064 | bytes 234881024 | tf_op jit(solution)/shard_map/assemble/pallas_call | solution.py:417
  102.3 7.4 %norm.1 = (bf16[1024,2048]{1,0:T(8,128)(2,1)S(1)}, bf16[1024,2048]{1,0:T(8,128)(2,1)S(1)}, f32[1024,128]{1,0:T(8,128)S(1)}, f32[8,2048]{1,0:T(8,128)S(1)}) custom-call(s32[4]{0:T(128)S(1)} %pad_add_fusion.scalars, bf16[1040,512]{1,0:T(8,128)(2,1)S(1)} %concatenate.55.refs_0_.refs_4_.second_piece, ...), custom_call_target="tpu_custom_call" | custom-call | flops 335544320 | bytes 201326592 | tf_op jit(solution)/shard_map/norm/pallas_call | solution.py:417
  111.2 12.7 %heads.1 = (bf16[3,1024,256]{2,1,0:T(8,128)(2,1)S(1)}, bf16[3,1024,256]{2,1,0:T(8,128)(2,1)S(1)}) custom-call(s32[4]{0:T(128)S(1)} %pad_add_fusion.scalars, bf16[1024,2048]{1,0:T(8,128)(2,1)S(1)} %get-tuple-element.152.rows_in, bf16[1024,1536]{1,0:T(8,128)(2,1)} %get-tuple-element.95.own.qkv_own, bf16[1024,1536]{1,0:T(8,128)(2,1)} %collective-permute-done.8.other.qkv_other, ...), custom_call_target="tpu_custom_call" | custom-call | flops 103079215104 | bytes 218103808 | tf_op jit(solution)/shard_map/heads/pallas_call | solution.py:417
  124.5 16.4 %expand.1 = (bf16[1024,2048]{1,0:T(8,128)(2,1)S(1)}, bf16[1024,2048]{1,0:T(8,128)(2,1)S(1)}) custom-call(s32[4]{0:T(128)S(1)} %pad_add_fusion.scalars, bf16[1024,2048]{1,0:T(8,128)(2,1)S(1)} %get-tuple-element.128.rows_in, bf16[1024,2048]{1,0:T(8,128)(2,1)S(1)} %copy-done.18, bf16[1024,2048]{1,0:T(8,128)(2,1)} %collective-permute-done.9.other.up_other, ...), custom_call_target="tpu_custom_call" | custom-call | flops 137438953472 | bytes 335544320 | tf_op jit(solution)/shard_map/expand/pallas_call | solution.py:417
  141.0 6.4 %collective-permute-done.11.refs_2_ = bf16[1024,512]{1,0:T(8,128)(2,1)} collective-permute-done((bf16[1024,512]{1,0:T(8,128)(2,1)}, bf16[1024,512]{1,0:T(8,128)(2,1)}, u32[]{:S(2)}, u32[]{:S(2)}) %collective-permute-start.11) | collective-permute-done | bytes 1048608 | tf_op jit(solution)/shard_map/ppermute | solution.py:324
  147.4 8.3 %attend.1 = (bf16[3,2048,256]{2,1,0:T(8,128)(2,1)S(1)}, bf16[1024,256]{1,0:T(8,128)(2,1)S(1)}, bf16[1024,256]{1,0:T(8,128)(2,1)S(1)}, f32[8,2048]{1,0:T(8,128)S(1)}) custom-call(s32[4]{0:T(128)S(1)} %pad_add_fusion.scalars, bf16[3,1024,256]{2,1,0:T(8,128)(2,1)S(1)} %get-tuple-element.98.mine, bf16[3,1024,256]{2,1,0:T(8,128)(2,1)S(1)} %collective-permute-done.12.theirs, ...), custom_call_target="tpu_custom_call" | custom-call | flops 38654705664 | bytes 134217728 | tf_op jit(solution)/shard_map/attend/pallas_call | solution.py:417
  160.1 6.7 %all-gather.2.cloned.1.call-done.own.other.refs_5_ = bf16[2560,2048]{1,0:T(8,128)(2,1)} async-done(((bf16[2560,256]{1,0:T(8,128)(2,1)}), bf16[2560,2048]{1,0:T(8,128)(2,1)}) %all-gather.2.cloned.1.call-update) | async-done | bytes 10485776 | tf_op jit(solution)/shard_map/all_gather | solution.py:1020
  166.8 16.8 %project.1 = bf16[1024,2048]{1,0:T(8,128)(2,1)} custom-call(s32[4]{0:T(128)} %copy-done.14, bf16[1024,256]{1,0:T(8,128)(2,1)} %copy-done.12, bf16[1024,256]{1,0:T(8,128)(2,1)} %copy-done.45, bf16[1024,2048]{1,0:T(8,128)(2,1)} %copy-done.28, bf16[2560,2048]{1,0:T(8,128)(2,1)} %all-gather.2.cloned.1.call-done.own.other.refs_5_, ...), custom_call_target="tpu_custom_call" | custom-call | flops 171798691840 | bytes 318767104 | tf_op jit(solution)/shard_map/project/pallas_call | solution.py:417
  186.2 17.9 %hidden_back.1 = (bf16[1024,2048]{1,0:T(8,128)(2,1)S(1)}, bf16[1024,2048]{1,0:T(8,128)(2,1)S(1)}, bf16[1024,256]{1,0:T(8,128)(2,1)S(1)}, bf16[1024,256]{1,0:T(8,128)(2,1)S(1)}, f32[8,2048]{1,0:T(8,128)S(1)}) custom-call(s32[4]{0:T(128)S(1)} %copy-done.15, bf16[1024,512]{1,0:T(8,128)(2,1)S(1)} %copy-done.3, ...), custom_call_target="tpu_custom_call" | custom-call | flops 171798691840 | bytes 436207616 | tf_op jit(solution)/shard_map/hidden_back/pallas_call | solution.py:417
  204.2 6.2 %convolution_convert_fusion.2 = bf16[2048,1024]{1,0:T(8,128)(2,1)} fusion(bf16[1024,2048]{1,0:T(8,128)(2,1)S(1)} %copy-done.29, bf16[1024,2048]{1,0:T(8,128)(2,1)S(1)} %get-tuple-element.116), kind=kOutput, calls=%fused_computation.5 | convolution fusion | flops 4297064448 | bytes 10485760 | tf_op jit(solution)/shard_map/dot_general | solution.py:385
  210.5 9.4 %convolution_convert_fusion.1 = bf16[1024,2048]{1,0:T(8,128)(2,1)} fusion(bf16[1024,2048]{1,0:T(8,128)(2,1)} %copy-done.24, bf16[1024,2048]{1,0:T(8,128)(2,1)} %copy-done.19), kind=kOutput, calls=%fused_computation.4 | convolution fusion | flops 4297064448 | bytes 10485760 | tf_op jit(solution)/shard_map/dot_general | solution.py:385
  222.9 8.0 %add_convert_fusion.1 = bf16[2048,1024]{1,0:T(8,128)(2,1)S(1)} fusion(bf16[2048,1024]{1,0:T(8,128)(2,1)} %collective-permute-done.15, bf16[1024,2048]{1,0:T(8,128)(2,1)} %copy-done.28, bf16[1024,2048]{1,0:T(8,128)(2,1)S(1)} %copy-done.23), kind=kOutput, calls=%fused_computation.1 | convolution fusion | flops 4301258752 | bytes 14680064 | tf_op jit(solution)/shard_map/dot_general | solution.py:385
  234.0 14.0 %attend_back.1 = (bf16[1024,768]{1,0:T(8,128)(2,1)S(1)}, bf16[1024,768]{1,0:T(8,128)(2,1)}, f32[8,768]{1,0:T(8,128)S(1)}) custom-call(s32[4]{0:T(128)S(1)} %copy-done.15, bf16[3,2048,256]{2,1,0:T(8,128)(2,1)S(1)} %copy-done.27, bf16[1024,256]{1,0:T(8,128)(2,1)S(1)} %get-tuple-element.121.own_grads, bf16[1024,256]{1,0:T(8,128)(2,1)S(1)} %collective-permute-done.16.twin_grads, ...), custom_call_target="tpu_custom_call" | custom-call | flops 6039797760 | bytes 8388608 | tf_op jit(solution)/shard_map/attend_back/pallas_call | solution.py:417
  253.9 7.9 %add_convert_fusion = bf16[1024,2048]{1,0:T(8,128)(2,1)} fusion(bf16[1024,2048]{1,0:T(8,128)(2,1)} %collective-permute-done.19, bf16[1024,2048]{1,0:T(8,128)(2,1)S(1)} %copy-done.25, bf16[1024,2048]{1,0:T(8,128)(2,1)S(1)} %copy-done.20), kind=kOutput, calls=%fused_computation | convolution fusion | flops 4301258752 | bytes 14680064 | tf_op jit(solution)/shard_map/dot_general | solution.py:385
  261.9 5.0 %add_convert_fusion.5 = bf16[512,1024]{1,0:T(8,128)(2,1)} fusion(bf16[512,1024]{1,0:T(8,128)(2,1)} %collective-permute-done.21, bf16[1024,512]{1,0:T(8,128)(2,1)} %copy-done.44, bf16[1024,2048]{1,0:T(8,128)(2,1)} %copy-done.22), kind=kOutput, calls=%fused_computation.25 | convolution fusion | flops 1075314688 | bytes 5242880 | tf_op jit(solution)/shard_map/dot_general | solution.py:385
  272.9 17.3 %mix.2 = (bf16[1024,512]{1,0:T(8,128)(2,1)}, bf16[1024,512]{1,0:T(8,128)(2,1)}, f32[32,512]{1,0:T(8,128)}, f32[32,512]{1,0:T(8,128)}, f32[1024,128]{1,0:T(8,128)}) custom-call(s32[4]{0:T(128)} %copy-done.14, bf16[1024,768]{1,0:T(8,128)(2,1)} %copy-done.6, bf16[1024,768]{1,0:T(8,128)(2,1)} %copy-done.41, bf16[1024,2048]{1,0:T(8,128)(2,1)} %copy-done.24, ...), custom_call_target="tpu_custom_call" | custom-call | flops 7516192768 | bytes 18874368 | tf_op jit(solution)/shard_map/mix/pallas_call | solution.py:417
  296.7 18.4 %mix.3 = (f32[1024,512]{1,0:T(8,128)}, f32[1024,512]{1,0:T(8,128)}, f32[32,512]{1,0:T(8,128)}, f32[32,512]{1,0:T(8,128)}, f32[1024,128]{1,0:T(8,128)}) custom-call(s32[4]{0:T(128)} %copy-done.14, bf16[1024,768]{1,0:T(8,128)(2,1)} %copy-done.6, bf16[1024,768]{1,0:T(8,128)(2,1)} %copy-done.41, bf16[1024,2048]{1,0:T(8,128)(2,1)} %copy-done.24, ...), custom_call_target="tpu_custom_call" | custom-call | flops 7516192768 | bytes 18874368 | tf_op jit(solution)/shard_map/mix/pallas_call | solution.py:417
  322.1 7.8 %convolution_convert_fusion = bf16[1024,1536]{1,0:T(8,128)(2,1)} fusion(bf16[1024,2048]{1,0:T(8,128)(2,1)} %copy-done.16, bf16[1024,768]{1,0:T(8,128)(2,1)} %get-tuple-element.182, bf16[1024,768]{1,0:T(8,128)(2,1)} %get-tuple-element.181), kind=kOutput, calls=%fused_computation.3 | convolution fusion | flops 3229089792 | bytes 8388608 | tf_op jit(solution)/shard_map/dot_general | solution.py:385
  347.5 6.6 %add_convert_fusion.2 = bf16[1024,1536]{1,0:T(8,128)(2,1)S(1)} fusion(bf16[1024,1536]{1,0:T(8,128)(2,1)} %collective-permute-done.32, bf16[1024,2048]{1,0:T(8,128)(2,1)} %copy-done.16, bf16[1024,768]{1,0:T(8,128)(2,1)} %get-tuple-element.182, bf16[1024,768]{1,0:T(8,128)(2,1)S(1)} %copy-done.40), kind=kOutput, calls=%fused_computation.2 | convolution fusion | flops 3232235520 | bytes 11534336 | tf_op jit(solution)/shard_map/dot_general | solution.py:385
  360.0 9.6 %collective-permute-done.33 = bf16[128,1536]{1,0:T(8,128)(2,1)S(1)} collective-permute-done((bf16[128,1536]{1,0:T(8,128)(2,1)S(1)}, bf16[128,1536]{1,0:T(8,128)(2,1)S(1)}, u32[]{:S(2)}, u32[]{:S(2)}) %collective-permute-start.33) | collective-permute-done | bytes 393248 | tf_op jit(solution)/shard_map/ppermute | solution.py:324
  377.1 15.0 %collective-permute-done.24 = bf16[1024,512]{1,0:T(8,128)(2,1)S(1)} collective-permute-done((bf16[1024,512]{1,0:T(8,128)(2,1)}, bf16[1024,512]{1,0:T(8,128)(2,1)S(1)}, u32[]{:S(2)}, u32[]{:S(2)}) %collective-permute-start.24) | collective-permute-done | bytes 1048608 | tf_op jit(solution)/shard_map/ppermute | solution.py:324
  (300 shorter events, 115.5 us)
Async XLA Ops:
  7.2 159.5 %all-gather.2.cloned.1.call-start = ((), (), s32[]{:S(2)}) async-start(), calls=%async_computation.3 | async-start | bytes 11796480 | tf_op jit(solution)/shard_map/all_gather | solution.py:1020
  10.5 55.2 %collective-permute-start.3 = (bf16[256,3584]{1,0:T(8,128)(2,1)}, bf16[256,3584]{1,0:T(8,128)(2,1)}, u32[]{:S(2)}, u32[]{:S(2)}) collective-permute-start(bf16[256,3584]{1,0:T(8,128)(2,1)} %constant_dynamic-update-slice_fusion.own), channel_id=1, source_target_pairs={{0,8},{8,0},{16,24},{24,16},{1,9},{9,1},{17,25},{25,17},{2,10},{10... | collective-permute-start | bytes 5505032 | tf_op jit(solution)/shard_map/ppermute | solution.py:324
  13.5 52.2 %collective-permute-start.4 = (bf16[256,3584]{1,0:T(8,128)(2,1)}, bf16[256,3584]{1,0:T(8,128)(2,1)}, u32[]{:S(2)}, u32[]{:S(2)}) collective-permute-start(bf16[256,3584]{1,0:T(8,128)(2,1)} %constant_dynamic-update-slice_fusion.own), channel_id=1, source_target_pairs={{0,16},{8,24},{16,0},{24,8},{1,17},{9,25},{17,1},{25,9},{2,18},{10... | collective-permute-start | bytes 5505032 | tf_op jit(solution)/shard_map/ppermute | solution.py:324
  15.4 47.5 %collective-permute-start = (bf16[1040,512]{1,0:T(8,128)(2,1)S(1)}, bf16[1040,512]{1,0:T(8,128)(2,1)S(1)}, u32[]{:S(2)}, u32[]{:S(2)}) collective-permute-start(bf16[1040,512]{1,0:T(8,128)(2,1)S(1)} %concatenate.55.refs_0_.refs_4_.second_piece), channel_id=1, source_target_pairs={{0,1},{1,0},{2,3},{3,2},{4,5},{5,4},{6,7},{7,6},{8,9},{9,8},{10,11... | collective-permute-start | bytes 3194888 | tf_op jit(solution)/shard_map/ppermute | solution.py:324
  17.1 48.3 %collective-permute-start.1 = (bf16[1040,512]{1,0:T(8,128)(2,1)S(1)}, bf16[1040,512]{1,0:T(8,128)(2,1)S(1)}, u32[]{:S(2)}, u32[]{:S(2)}) collective-permute-start(bf16[1040,512]{1,0:T(8,128)(2,1)S(1)} %concatenate.55.refs_0_.refs_4_.second_piece), channel_id=1, source_target_pairs={{0,2},{1,3},{2,0},{3,1},{4,6},{5,7},{6,4},{7,5},{8,10},{9,11},{10,... | collective-permute-start | bytes 3194888 | tf_op jit(solution)/shard_map/ppermute | solution.py:324
  65.4 22.5 %collective-permute-start.7 = (bf16[1040,512]{1,0:T(8,128)(2,1)S(1)}, bf16[1040,512]{1,0:T(8,128)(2,1)}, u32[]{:S(2)}, u32[]{:S(2)}) collective-permute-start(bf16[1040,512]{1,0:T(8,128)(2,1)S(1)} %collective-permute-done.1.refs_2_.refs_6_.first_piece), channel_id=1, source_target_pairs={{0,1},{1,0},{2,3},{3,2},{4,5},{5,4},{6,7},{7,6},{8,9},{9,8},{10,11... | collective-permute-start | bytes 3194888 | tf_op jit(solution)/shard_map/ppermute | solution.py:324
  67.9 20.6 %collective-permute-start.5 = (bf16[128,3584]{1,0:T(8,128)(2,1)}, bf16[128,3584]{1,0:T(8,128)(2,1)}, u32[]{:S(2)}, u32[]{:S(2)}) collective-permute-start(bf16[128,3584]{1,0:T(8,128)(2,1)} %slice.199), channel_id=1, source_target_pairs={{0,8},{8,0},{16,24},{24,16},{1,9},{9,1},{17,25},{25,17},{2,10},{10... | collective-permute-start | bytes 2752520 | tf_op jit(solution)/shard_map/ppermute | solution.py:324
  70.6 20.3 %collective-permute-start.6 = (bf16[128,3584]{1,0:T(8,128)(2,1)}, bf16[128,3584]{1,0:T(8,128)(2,1)}, u32[]{:S(2)}, u32[]{:S(2)}) collective-permute-start(bf16[128,3584]{1,0:T(8,128)(2,1)} %slice.200), channel_id=1, source_target_pairs={{0,16},{8,24},{16,0},{24,8},{1,17},{9,25},{17,1},{25,9},{2,18},{10... | collective-permute-start | bytes 2752520 | tf_op jit(solution)/shard_map/ppermute | solution.py:324
  100.1 47.3 %collective-permute-start.11 = (bf16[1024,512]{1,0:T(8,128)(2,1)}, bf16[1024,512]{1,0:T(8,128)(2,1)}, u32[]{:S(2)}, u32[]{:S(2)}) collective-permute-start(bf16[1024,512]{1,0:T(8,128)(2,1)} %refs_0_.1), channel_id=1, source_target_pairs={{0,2},{1,3},{2,0},{3,1},{4,6},{5,7},{6,4},{7,5},{8,10},{9,11},{10,... | collective-permute-start | bytes 3145736 | tf_op jit(solution)/shard_map/ppermute | solution.py:324
  101.0 46.4 %collective-permute-start.10 = (bf16[1024,512]{1,0:T(8,128)(2,1)}, bf16[1024,512]{1,0:T(8,128)(2,1)}, u32[]{:S(2)}, u32[]{:S(2)}) collective-permute-start(bf16[1024,512]{1,0:T(8,128)(2,1)} %refs_0_.1), channel_id=1, source_target_pairs={{0,1},{1,0},{2,3},{3,2},{4,5},{5,4},{6,7},{7,6},{8,9},{9,8},{10,11... | collective-permute-start | bytes 3145736 | tf_op jit(solution)/shard_map/ppermute | solution.py:324
  102.0 22.5 %collective-permute-start.9 = (bf16[1024,2048]{1,0:T(8,128)(2,1)}, bf16[1024,2048]{1,0:T(8,128)(2,1)}, u32[]{:S(2)}, u32[]{:S(2)}) collective-permute-start(bf16[1024,2048]{1,0:T(8,128)(2,1)} %copy-done.17), channel_id=1, source_target_pairs={{0,4},{4,0},{1,5},{5,1},{2,6},{6,2},{3,7},{7,3},{8,12},{12,8},{9,1... | collective-permute-start | bytes 12582920 | tf_op jit(solution)/shard_map/ppermute | solution.py:324
  102.0 194.7 %reduce-scatter.4.cloned.1.call-start = ((), (), s32[]{:S(2)}) async-start(), calls=%async_computation.4 | async-start | bytes 5242880 | tf_op jit(solution)/shard_map/reduce_scatter | solution.py:1038
  123.9 23.5 %collective-permute-start.12 = (bf16[3,1024,256]{2,1,0:T(8,128)(2,1)S(1)}, bf16[3,1024,256]{2,1,0:T(8,128)(2,1)S(1)}, u32[]{:S(2)}, u32[]{:S(2)}) collective-permute-start(bf16[3,1024,256]{2,1,0:T(8,128)(2,1)S(1)} %get-tuple-element.105), channel_id=1, source_target_pairs={{0,4},{4,0},{1,5},{5,1},{2,6},{6,2},{3,7},{7,3},{8,12},{12,8},{9,1... | collective-permute-start | bytes 4718600 | tf_op jit(solution)/shard_map/ppermute | solution.py:324
  158.2 25.9 %collective-permute-start.14 = (bf16[1024,512]{1,0:T(8,128)(2,1)}, bf16[1024,512]{1,0:T(8,128)(2,1)}, u32[]{:S(2)}, u32[]{:S(2)}) collective-permute-start(bf16[1024,512]{1,0:T(8,128)(2,1)} %collective-permute-done.11.refs_2_), channel_id=1, source_target_pairs={{0,1},{1,0},{2,3},{3,2},{4,5},{5,4},{6,7},{7,6},{8,9},{9,8},{10,11... | collective-permute-start | bytes 3145736 | tf_op jit(solution)/shard_map/ppermute | solution.py:324
  210.4 183.9 %reduce-scatter.6.cloned.1.call-start = ((), (), s32[]{:S(2)}) async-start(), calls=%async_computation.5 | async-start | bytes 1310720 | tf_op jit(solution)/shard_map/reduce_scatter | solution.py:1053
  219.9 33.3 %collective-permute-start.19 = (bf16[1024,2048]{1,0:T(8,128)(2,1)}, bf16[1024,2048]{1,0:T(8,128)(2,1)}, u32[]{:S(2)}, u32[]{:S(2)}) collective-permute-start(bf16[1024,2048]{1,0:T(8,128)(2,1)} %convolution_convert_fusion.1), channel_id=1, source_target_pairs={{0,4},{4,0},{1,5},{5,1},{2,6},{6,2},{3,7},{7,3},{8,12},{12,8},{9,1... | collective-permute-start | bytes 12582920 | tf_op jit(solution)/shard_map/ppermute | solution.py:324
  266.9 136.1 %reduce-scatter.8.cloned.1.call-start = ((), (), s32[]{:S(2)}) async-start(), calls=%async_computation.6 | async-start | bytes 5242880 | tf_op jit(solution)/shard_map/reduce_scatter | solution.py:1053
  270.8 51.2 %collective-permute-start.30 = (bf16[2048,256]{1,0:T(8,128)(2,1)}, bf16[2048,256]{1,0:T(8,128)(2,1)}, u32[]{:S(2)}, u32[]{:S(2)}) collective-permute-start(bf16[2048,256]{1,0:T(8,128)(2,1)} %pad_maximum_fusion.6), channel_id=1, source_target_pairs={{0,8},{8,0},{16,24},{24,16},{1,9},{9,1},{17,25},{25,17},{2,10},{10... | collective-permute-start | bytes 3145736 | tf_op jit(solution)/shard_map/ppermute | solution.py:324
  272.3 49.7 %collective-permute-start.31 = (bf16[2048,256]{1,0:T(8,128)(2,1)}, bf16[2048,256]{1,0:T(8,128)(2,1)}, u32[]{:S(2)}, u32[]{:S(2)}) collective-permute-start(bf16[2048,256]{1,0:T(8,128)(2,1)} %pad_maximum_fusion.5), channel_id=1, source_target_pairs={{0,16},{8,24},{16,0},{24,8},{1,17},{9,25},{17,1},{25,9},{2,18},{10... | collective-permute-start | bytes 3145736 | tf_op jit(solution)/shard_map/ppermute | solution.py:324
  292.0 25.9 %collective-permute-start.25 = (bf16[1024,512]{1,0:T(8,128)(2,1)}, bf16[1024,512]{1,0:T(8,128)(2,1)}, u32[]{:S(2)}, u32[]{:S(2)}) collective-permute-start(bf16[1024,512]{1,0:T(8,128)(2,1)} %get-tuple-element.133), channel_id=1, source_target_pairs={{0,1},{1,0},{2,3},{3,2},{4,5},{5,4},{6,7},{7,6},{8,9},{9,8},{10,11... | collective-permute-start | bytes 3145736 | tf_op jit(solution)/shard_map/ppermute | solution.py:324
  344.1 48.0 %collective-permute-start.24 = (bf16[1024,512]{1,0:T(8,128)(2,1)}, bf16[1024,512]{1,0:T(8,128)(2,1)S(1)}, u32[]{:S(2)}, u32[]{:S(2)}) collective-permute-start(bf16[1024,512]{1,0:T(8,128)(2,1)} %get-tuple-element.143), channel_id=1, source_target_pairs={{0,1},{1,0},{2,3},{3,2},{4,5},{5,4},{6,7},{7,6},{8,9},{9,8},{10,11... | collective-permute-start | bytes 3145736 | tf_op jit(solution)/shard_map/ppermute | solution.py:324
  345.0 48.9 %collective-permute-start.26 = (bf16[1024,512]{1,0:T(8,128)(2,1)}, bf16[1024,512]{1,0:T(8,128)(2,1)S(1)}, u32[]{:S(2)}, u32[]{:S(2)}) collective-permute-start(bf16[1024,512]{1,0:T(8,128)(2,1)} %add_convert_fusion.4), channel_id=1, source_target_pairs={{0,2},{1,3},{2,0},{3,1},{4,6},{5,7},{6,4},{7,5},{8,10},{9,11},{10,... | collective-permute-start | bytes 3145736 | tf_op jit(solution)/shard_map/ppermute | solution.py:324
  373.6 26.6 %collective-permute-start.35 = (bf16[256,1536]{1,0:T(8,128)(2,1)}, bf16[256,1536]{1,0:T(8,128)(2,1)}, u32[]{:S(2)}, u32[]{:S(2)}) collective-permute-start(bf16[256,1536]{1,0:T(8,128)(2,1)} %pad_maximum_fusion.8), channel_id=1, source_target_pairs={{0,8},{8,0},{16,24},{24,16},{1,9},{9,1},{17,25},{25,17},{2,10},{10... | collective-permute-start | bytes 2359304 | tf_op jit(solution)/shard_map/ppermute | solution.py:324
  374.6 25.6 %collective-permute-start.36 = (bf16[256,1536]{1,0:T(8,128)(2,1)}, bf16[256,1536]{1,0:T(8,128)(2,1)}, u32[]{:S(2)}, u32[]{:S(2)}) collective-permute-start(bf16[256,1536]{1,0:T(8,128)(2,1)} %pad_maximum_fusion.7), channel_id=1, source_target_pairs={{0,16},{8,24},{16,0},{24,8},{1,17},{9,25},{17,1},{25,9},{2,18},{10... | collective-permute-start | bytes 2359304 | tf_op jit(solution)/shard_map/ppermute | solution.py:324
  (79 other events, 990.8 us)
Sparse Core Ops, SparseCore 0:
  102.1 64.5 all-gather.1
  210.5 76.5 reduce-scatter.3
  290.3 28.2 reduce-scatter.5
  321.4 59.2 reduce-scatter.7

commit v4 on v3

--- a/solution.py
+++ b/solution.py
@@ -315,7 +315,7 @@
 wide = jnp.float32
 tile = 256
 megabyte = 1024 * 1024
-pace = {"attend_back": 1, "mix": 1}
+pace = {"assemble": 4000, "attend_back": 1, "mix": 1}
 room = {"project": 56, "mix": 56}
 
 
@@ -709,7 +709,8 @@
 
 def mix_kernel(
     scalars, mine, theirs, pre_grad, qkv_own, qkv_other, up_own, up_other, terms_own, terms_other,
-    stats, first_piece, second_piece, first_out, second_out, sums_own, sums_other, row_sums
+    stats, first_piece, second_piece, first_out, second_out, sums_own, sums_other, row_sums,
+    *both
 ):
     step = pl.program_id(0)
     rows = pre_grad.shape[0]
@@ -753,11 +754,18 @@
             for place, total in enumerate(totals):
                 sums[8 * place : 8 * place + 8, :] = total
 
+    for joined in both:
+
+        @pl.when(step == 0)
+        def _():
+            joined[:, place_of(scalars[0], 3 * HEAD_DIM)] = mine[...]
+            joined[:, place_of(1 - scalars[0], 3 * HEAD_DIM)] = theirs[...]
+
     pl.when(step == 0)(partial(run, first_piece, first_out, True))
     pl.when(step == 1)(partial(run, second_piece, second_out, False))
 
 
-def mix(scalars, mine, theirs, pre_grad, qkv, up, terms, stats, pieces, order, kinds):
+def mix(scalars, mine, theirs, pre_grad, qkv, up, terms, stats, pieces, order, kinds, join=False):
     rows = pre_grad.shape[0]
     width = pieces[0].shape[1]
     depth = qkv[0].shape[1] + up[0].shape[1]
@@ -776,10 +784,13 @@
         + [weight(x) for x in (*qkv, *up)]
         + [term(0), term(4), fixed((rows, 128))]
         + [fixed((rows, width))] * 2,
-        [kept((rows, width))] * 2 + [sums, sums, kept((rows, 128))],
+        [kept((rows, width))] * 2
+        + [sums, sums, kept((rows, 128))]
+        + [kept((rows, 6 * HEAD_DIM))] * join,
         [shaped(rows, width, kind=kind) for kind in kinds]
         + [shaped(32, 2 * tile, kind=wide)] * 2
-        + [shaped(rows, 128, kind=wide)],
+        + [shaped(rows, 128, kind=wide)]
+        + [shaped(rows, 6 * HEAD_DIM)] * join,
         (scalars, mine, theirs, pre_grad, *qkv, *up, terms, terms, stats, pieces[order[0]], pieces[order[1]]),
         4 * rows * width * depth,
         2 * (4 * rows * width + 2 * depth * width + rows * depth),
@@ -1070,23 +1081,15 @@
     dense_total = add_low(
         outer(after(both_attended, up_total, other_joined), cotangent[:, :half]), dense_arrived
     )
-    dense_grad = to_owner(dense_total, 1)
     mix_in = (joined_grad, other_joined, pre_grad, qkv, up, terms, stats, pieces)
-    *leave, sums_a, sums_b, row_a = mix(
-        after(scalars, dense_total), *mix_in, (3, 1), (low, low)
+    *leave, sums_a, sums_b, row_a, both_joined = mix(
+        after(scalars, dense_total), *mix_in, (3, 1), (low, low), True
     )
     mixed_side = trade(leave[0], "tp", 1)
     *stay_mixed, sums_c, sums_d, row_b = mix(
         after(scalars, leave[0], shared_out), *mix_in, (2, 0), (wide, wide)
     )
     passed = (stay_mixed[0] + mixed_side.astype(wide)).astype(low)
-    both_joined = join_cores(joined_grad, other_joined, core, 1)
-    shared_out = shared_out.astype(wide)
-    shared_out = join_cores(shared_out[:, :tile], shared_out[:, tile:], core, 1)
-    output = (
-        residual.astype(wide) + shared_out + dense_bias.astype(wide) + down_bias.astype(wide)
-    ).astype(low)
-
     row_sums = row_a + row_b
     row_total = jnp.stack([row_sums[:, 0], row_sums[:, 64]])
     fold = lambda x: jnp.sum(x.reshape(4, 8, 2, tile), axis=1)
@@ -1106,7 +1109,17 @@
     row_total = row_total + hop_far[4 * held_width :].reshape(row_total.shape)
     row_means = row_total / width
     norm_total = join_cores(norm_total[:, :tile], norm_total[:, tile:], core, 1)
-    held_grad_sum = jnp.sum(out_grad.astype(wide), axis=0)
+    down_grad = close_plane(down_parts, qkv_other)
+    qkv_total = add_low(
+        outer(after(attn_in, qkv_other, down_grad, hop_far)[:, :half], both_joined), qkv_arrived
+    )
+    shared_out = after(shared_out, qkv_total).astype(wide)
+    shared_out = join_cores(shared_out[:, :tile], shared_out[:, tile:], core, 1)
+    output = (
+        residual.astype(wide) + shared_out + dense_bias.astype(wide) + down_bias.astype(wide)
+    ).astype(low)
+
+    held_grad_sum = jnp.sum(after(out_grad, qkv_total).astype(wide), axis=0)
     columns = jnp.concatenate(
         [
             norm_total.reshape(-1),
@@ -1115,15 +1128,13 @@
             jnp.sum(qkv_bias_rows, axis=0),
         ]
     )
+    columns = after(columns, qkv_total)
     columns = columns + trade(columns, "fsdp", 1)
-    down_grad = close_plane(down_parts, qkv_other)
-    qkv_total = add_low(
-        outer(after(attn_in, qkv_other, down_grad, hop_far)[:, :half], both_joined), qkv_arrived
-    )
     columns = columns + trade(columns, "fsdp", 2)
+    dense_grad = to_owner(after(dense_total, up_grad, qkv_total), 1)
     qkv_parts, qkv_hop = scatter_plane(qkv_total, "fsdp", 0)
     qkv_grad = close_plane(qkv_parts)
-    dense_grad = after(dense_grad, *qkv_hop)
+    dense_grad, up_grad = after(dense_grad, *qkv_hop), after(up_grad, *qkv_hop)
     other_columns = trade(columns, "ctx", 1)
     cut = columns.shape[0] - qkv_bias.shape[0] // 2
     qkv_bias_grad = join_cores(columns[cut:], other_columns[cut:], core, 0)

time: 417 us -> 400 us (0.959)
  other arithmetic: 40.2 us -> 35.4 us
    select_n x6 -> x5, other arithmetic: 6.29 us -> 1.58 us  [join_cores(): first = jnp.where(core == 0, mine, theirs)]
    ppermute x37, waiting for transfers between devices: 101 us -> 97 us  [trade(): return lax.ppermute(x, axis, [(i, i ^ bit) for i in range(peers)])]
  transfers between devices with their start and end apart: 41 -> 41, of which waited for: 16 -> 17; matrix products, arithmetic and copies ran while one was open for 23% -> 22% of each run, Pallas kernels for 27% -> 28%
where the time goes in v4:
time: 400 us; the launch traced here: 397 us
  Pallas kernels  136 us (34%)
  waiting for transfers between devices  104 us (26%)
  matrix products  50.3 us (13%)
  other arithmetic  35.4 us (9%)
  starting transfers between devices  32.2 us (8%)
  local copies, waits for them, and re-layouts  24 us (6%)
  between operations  15 us (4%)
    pallas_call x10, Pallas kernels, call(): pl.pallas_call(kernel, grid_spec=pltpu.PrefetchScalarGridSpec(num_scalar_...  136 us
    ppermute x37, waiting for transfers between devices, trade(): return lax.ppermute(x, axis, [(i, i ^ bit) for i in range(peers)])  97 us
    dot_general x8, matrix products, contract(): lax.dot_general(a, b, ((dims[:1], dims[1:]), ((), ())), preferred_element...  50.3 us
    ppermute x37, starting transfers between devices, trade(): return lax.ppermute(x, axis, [(i, i ^ bit) for i in range(peers)])  31.8 us
    unnamed x130, local copies, waits for them, and re-layouts  13.6 us
  transfers between devices with their start and end apart: 41, of which 17 were waited for; matrix products, arithmetic and copies ran while one was open for 22% of the time, Pallas kernels for 28%

profile of v4, /device:TPU:0, one launch (start us, length us, event | category | flops | bytes accessed | tf_op | source)
XLA Modules:
  0.0 396.7 jit_solution(6872117655407099432)
XLA Ops:
  20.8 5.5 %multiply_sine_fusion = (f32[2048,128]{1,0:T(8,128)}, f32[2048,128]{1,0:T(8,128)}) fusion(f32[128]{0:T(128)S(1)} %compare_select_fusion, f32[2048]{0:T(1024)S(1)} %add_convert_fusion.11), kind=kLoop, calls=%fused_computation.34 | loop fusion | flops 262144 | bytes 2105856 | tf_op jit(solution)/shard_map/sin | solution.py:972
  26.3 36.6 %collective-permute-done.refs_1_.refs_5_.second_piece = bf16[1040,512]{1,0:T(8,128)(2,1)S(1)} collective-permute-done((bf16[1040,512]{1,0:T(8,128)(2,1)S(1)}, bf16[1040,512]{1,0:T(8,128)(2,1)S(1)}, u32[]{:S(2)}, u32[]{:S(2)}) %collective-permute-start) | collective-permute-done | bytes 1064992 | tf_op jit(solution)/shard_map/ppermute | solution.py:324
  71.3 16.6 %collective-permute-done.7.refs_3_.refs_7_.first_piece = bf16[1040,512]{1,0:T(8,128)(2,1)} collective-permute-done((bf16[1040,512]{1,0:T(8,128)(2,1)S(1)}, bf16[1040,512]{1,0:T(8,128)(2,1)}, u32[]{:S(2)}, u32[]{:S(2)}) %collective-permute-start.7) | collective-permute-done | bytes 1064992 | tf_op jit(solution)/shard_map/ppermute | solution.py:324
  90.9 6.0 %assemble.1 = (bf16[1024,1536]{1,0:T(8,128)(2,1)}, bf16[1024,2048]{1,0:T(8,128)(2,1)S(1)}) custom-call(s32[4]{0:T(128)S(1)} %pad_add_fusion.scalars, bf16[256,3584]{1,0:T(8,128)(2,1)} %constant_dynamic-update-slice_fusion.own, bf16[256,3584]{1,0:T(8,128)(2,1)} %collective-permute-done.3.near, bf16[256,3584]{1,0:T(8,128)(2,1)} %collective-permute-done.4.far, ...), custom_call_target="tpu_custom_call" | custom-call | flops 3670016000 | bytes 58720256000 | tf_op jit(solution)/shard_map/assemble/pallas_call | solution.py:417
  102.3 7.4 %norm.1 = (bf16[1024,2048]{1,0:T(8,128)(2,1)S(1)}, bf16[1024,2048]{1,0:T(8,128)(2,1)S(1)}, f32[1024,128]{1,0:T(8,128)S(1)}, f32[8,2048]{1,0:T(8,128)S(1)}) custom-call(s32[4]{0:T(128)S(1)} %pad_add_fusion.scalars, bf16[1040,512]{1,0:T(8,128)(2,1)S(1)} %concatenate.52.refs_0_.refs_4_.second_piece, ...), custom_call_target="tpu_custom_call" | custom-call | flops 335544320 | bytes 201326592 | tf_op jit(solution)/shard_map/norm/pallas_call | solution.py:417
  111.2 12.7 %heads.1 = (bf16[3,1024,256]{2,1,0:T(8,128)(2,1)S(1)}, bf16[3,1024,256]{2,1,0:T(8,128)(2,1)S(1)}) custom-call(s32[4]{0:T(128)S(1)} %pad_add_fusion.scalars, bf16[1024,2048]{1,0:T(8,128)(2,1)S(1)} %get-tuple-element.153.rows_in, bf16[1024,1536]{1,0:T(8,128)(2,1)} %get-tuple-element.101.own.qkv_own, bf16[1024,1536]{1,0:T(8,128)(2,1)} %collective-permute-done.8.other.qkv_other, ...), custom_call_target="tpu_custom_call" | custom-call | flops 103079215104 | bytes 218103808 | tf_op jit(solution)/shard_map/heads/pallas_call | solution.py:417
  124.5 16.4 %expand.1 = (bf16[1024,2048]{1,0:T(8,128)(2,1)S(1)}, bf16[1024,2048]{1,0:T(8,128)(2,1)S(1)}) custom-call(s32[4]{0:T(128)S(1)} %pad_add_fusion.scalars, bf16[1024,2048]{1,0:T(8,128)(2,1)S(1)} %get-tuple-element.133.rows_in, bf16[1024,2048]{1,0:T(8,128)(2,1)S(1)} %copy-done.17, bf16[1024,2048]{1,0:T(8,128)(2,1)} %collective-permute-done.9.other.up_other, ...), custom_call_target="tpu_custom_call" | custom-call | flops 137438953472 | bytes 335544320 | tf_op jit(solution)/shard_map/expand/pallas_call | solution.py:417
  141.0 6.4 %collective-permute-done.11.refs_2_ = bf16[1024,512]{1,0:T(8,128)(2,1)} collective-permute-done((bf16[1024,512]{1,0:T(8,128)(2,1)}, bf16[1024,512]{1,0:T(8,128)(2,1)}, u32[]{:S(2)}, u32[]{:S(2)}) %collective-permute-start.11) | collective-permute-done | bytes 1048608 | tf_op jit(solution)/shard_map/ppermute | solution.py:324
  147.4 8.3 %attend.1 = (bf16[3,2048,256]{2,1,0:T(8,128)(2,1)S(1)}, bf16[1024,256]{1,0:T(8,128)(2,1)S(1)}, bf16[1024,256]{1,0:T(8,128)(2,1)S(1)}, f32[8,2048]{1,0:T(8,128)S(1)}) custom-call(s32[4]{0:T(128)S(1)} %pad_add_fusion.scalars, bf16[3,1024,256]{2,1,0:T(8,128)(2,1)S(1)} %get-tuple-element.104.mine, bf16[3,1024,256]{2,1,0:T(8,128)(2,1)S(1)} %collective-permute-done.12.theirs, ...), custom_call_target="tpu_custom_call" | custom-call | flops 38654705664 | bytes 134217728 | tf_op jit(solution)/shard_map/attend/pallas_call | solution.py:417
  160.1 6.7 %all-gather.2.cloned.1.call-done.own.other.refs_5_ = bf16[2560,2048]{1,0:T(8,128)(2,1)} async-done(((bf16[2560,256]{1,0:T(8,128)(2,1)}), bf16[2560,2048]{1,0:T(8,128)(2,1)}) %all-gather.2.cloned.1.call-update) | async-done | bytes 10485776 | tf_op jit(solution)/shard_map/all_gather | solution.py:1031
  166.8 16.8 %project.1 = bf16[1024,2048]{1,0:T(8,128)(2,1)} custom-call(s32[4]{0:T(128)} %copy-done.12, bf16[1024,256]{1,0:T(8,128)(2,1)} %copy-done.10, bf16[1024,256]{1,0:T(8,128)(2,1)} %copy-done.42, bf16[1024,2048]{1,0:T(8,128)(2,1)} %copy-done.28, bf16[2560,2048]{1,0:T(8,128)(2,1)} %all-gather.2.cloned.1.call-done.own.other.refs_5_, ...), custom_call_target="tpu_custom_call" | custom-call | flops 171798691840 | bytes 318767104 | tf_op jit(solution)/shard_map/project/pallas_call | solution.py:417
  186.2 17.9 %hidden_back.1 = (bf16[1024,2048]{1,0:T(8,128)(2,1)S(1)}, bf16[1024,2048]{1,0:T(8,128)(2,1)S(1)}, bf16[1024,256]{1,0:T(8,128)(2,1)S(1)}, bf16[1024,256]{1,0:T(8,128)(2,1)S(1)}, f32[8,2048]{1,0:T(8,128)S(1)}) custom-call(s32[4]{0:T(128)S(1)} %copy-done.13, bf16[1024,512]{1,0:T(8,128)(2,1)S(1)} %copy-done.3, ...), custom_call_target="tpu_custom_call" | custom-call | flops 171798691840 | bytes 436207616 | tf_op jit(solution)/shard_map/hidden_back/pallas_call | solution.py:417
  204.2 6.2 %convolution_convert_fusion.2 = bf16[2048,1024]{1,0:T(8,128)(2,1)} fusion(bf16[1024,2048]{1,0:T(8,128)(2,1)S(1)} %copy-done.29, bf16[1024,2048]{1,0:T(8,128)(2,1)S(1)} %get-tuple-element.121), kind=kOutput, calls=%fused_computation.5 | convolution fusion | flops 4297064448 | bytes 10485760 | tf_op jit(solution)/shard_map/dot_general | solution.py:385
  210.5 9.4 %convolution_convert_fusion.1 = bf16[1024,2048]{1,0:T(8,128)(2,1)} fusion(bf16[1024,2048]{1,0:T(8,128)(2,1)} %copy-done.23, bf16[1024,2048]{1,0:T(8,128)(2,1)} %copy-done.18), kind=kOutput, calls=%fused_computation.4 | convolution fusion | flops 4297064448 | bytes 10485760 | tf_op jit(solution)/shard_map/dot_general | solution.py:385
  222.9 8.0 %add_convert_fusion.1 = bf16[2048,1024]{1,0:T(8,128)(2,1)S(1)} fusion(bf16[2048,1024]{1,0:T(8,128)(2,1)} %collective-permute-done.15, bf16[1024,2048]{1,0:T(8,128)(2,1)} %copy-done.28, bf16[1024,2048]{1,0:T(8,128)(2,1)S(1)} %copy-done.22), kind=kOutput, calls=%fused_computation.1 | convolution fusion | flops 4301258752 | bytes 14680064 | tf_op jit(solution)/shard_map/dot_general | solution.py:385
  233.3 14.2 %attend_back.1 = (bf16[1024,768]{1,0:T(8,128)(2,1)S(1)}, bf16[1024,768]{1,0:T(8,128)(2,1)}, f32[8,768]{1,0:T(8,128)S(1)}) custom-call(s32[4]{0:T(128)S(1)} %copy-done.13, bf16[3,2048,256]{2,1,0:T(8,128)(2,1)S(1)} %copy-done.27, bf16[1024,256]{1,0:T(8,128)(2,1)S(1)} %get-tuple-element.126.own_grads, bf16[1024,256]{1,0:T(8,128)(2,1)S(1)} %collective-permute-done.16.twin_grads, ...), custom_call_target="tpu_custom_call" | custom-call | flops 6039797760 | bytes 8388608 | tf_op jit(solution)/shard_map/attend_back/pallas_call | solution.py:417
  255.1 8.0 %add_convert_fusion = bf16[1024,2048]{1,0:T(8,128)(2,1)} fusion(bf16[1024,2048]{1,0:T(8,128)(2,1)} %collective-permute-done.19, bf16[1024,2048]{1,0:T(8,128)(2,1)S(1)} %copy-done.24, bf16[1024,2048]{1,0:T(8,128)(2,1)S(1)} %copy-done.19), kind=kOutput, calls=%fused_computation | convolution fusion | flops 4301258752 | bytes 14680064 | tf_op jit(solution)/shard_map/dot_general | solution.py:385
  263.1 4.5 %add_convert_fusion.5 = bf16[512,1024]{1,0:T(8,128)(2,1)} fusion(bf16[512,1024]{1,0:T(8,128)(2,1)} %collective-permute-done.21, bf16[1024,512]{1,0:T(8,128)(2,1)} %copy-done.41, bf16[1024,2048]{1,0:T(8,128)(2,1)} %copy-done.21), kind=kOutput, calls=%fused_computation.24 | convolution fusion | flops 1075314688 | bytes 5242880 | tf_op jit(solution)/shard_map/dot_general | solution.py:385
  267.6 18.3 %mix.2 = (bf16[1024,512]{1,0:T(8,128)(2,1)}, bf16[1024,512]{1,0:T(8,128)(2,1)}, f32[32,512]{1,0:T(8,128)}, f32[32,512]{1,0:T(8,128)}, f32[1024,128]{1,0:T(8,128)}, /*index=5*/bf16[1024,1536]{1,0:T(8,128)(2,1)}) custom-call(s32[4]{0:T(128)} %copy-done.12, bf16[1024,768]{1,0:T(8,128)(2,1)} %copy-done.25, bf16[1024,768]{1,0:T(8,128)(2,1)} %collective-permute-done.20.theirs, ...), custom_call_target="tpu_custom_call" | custom-call | flops 7516192768 | bytes 18874368 | tf_op jit(solution)/shard_map/mix/pallas_call | solution.py:417
  288.8 17.8 %mix.3 = (f32[1024,512]{1,0:T(8,128)}, f32[1024,512]{1,0:T(8,128)}, f32[32,512]{1,0:T(8,128)}, f32[32,512]{1,0:T(8,128)}, f32[1024,128]{1,0:T(8,128)}) custom-call(s32[4]{0:T(128)} %copy-done.12, bf16[1024,768]{1,0:T(8,128)(2,1)} %copy-done.25, bf16[1024,768]{1,0:T(8,128)(2,1)} %collective-permute-done.20.theirs, bf16[1024,2048]{1,0:T(8,128)(2,1)} %copy-done.23, ...), custom_call_target="tpu_custom_call" | custom-call | flops 7516192768 | bytes 18874368 | tf_op jit(solution)/shard_map/mix/pallas_call | solution.py:417
  316.2 5.0 %convolution_convert_fusion = bf16[1024,1536]{1,0:T(8,128)(2,1)} fusion(bf16[1024,1536]{1,0:T(8,128)(2,1)S(1)} %copy-done.61, bf16[1024,2048]{1,0:T(8,128)(2,1)S(1)} %copy-done.15), kind=kOutput, calls=%fused_computation.3 | convolution fusion | flops 3222798336 | bytes 8388608 | tf_op jit(solution)/shard_map/dot_general | solution.py:385
  331.8 6.9 %add_convert_fusion.2 = bf16[1024,1536]{1,0:T(8,128)(2,1)S(1)} fusion(bf16[1024,1536]{1,0:T(8,128)(2,1)} %collective-permute-done.27, bf16[1024,1536]{1,0:T(8,128)(2,1)} %get-tuple-element.147, bf16[1024,2048]{1,0:T(8,128)(2,1)} %copy-done.14), kind=kOutput, calls=%fused_computation.2 | convolution fusion | flops 3225944064 | bytes 11534336 | tf_op jit(solution)/shard_map/dot_general | solution.py:385
  360.8 14.4 %collective-permute-done.28 = bf16[1024,512]{1,0:T(8,128)(2,1)} collective-permute-done((bf16[1024,512]{1,0:T(8,128)(2,1)}, bf16[1024,512]{1,0:T(8,128)(2,1)}, u32[]{:S(2)}, u32[]{:S(2)}) %collective-permute-start.28) | collective-permute-done | bytes 1048608 | tf_op jit(solution)/shard_map/ppermute | solution.py:324
  375.2 4.0 collective-permute-done.29
  (299 shorter events, 107.5 us)
Async XLA Ops:
  7.2 159.6 %all-gather.2.cloned.1.call-start = ((), (), s32[]{:S(2)}) async-start(), calls=%async_computation.3 | async-start | bytes 11796480 | tf_op jit(solution)/shard_map/all_gather | solution.py:1031
  10.5 55.2 %collective-permute-start.3 = (bf16[256,3584]{1,0:T(8,128)(2,1)}, bf16[256,3584]{1,0:T(8,128)(2,1)}, u32[]{:S(2)}, u32[]{:S(2)}) collective-permute-start(bf16[256,3584]{1,0:T(8,128)(2,1)} %constant_dynamic-update-slice_fusion.own), channel_id=1, source_target_pairs={{0,8},{8,0},{16,24},{24,16},{1,9},{9,1},{17,25},{25,17},{2,10},{10... | collective-permute-start | bytes 5505032 | tf_op jit(solution)/shard_map/ppermute | solution.py:324
  13.5 52.2 %collective-permute-start.4 = (bf16[256,3584]{1,0:T(8,128)(2,1)}, bf16[256,3584]{1,0:T(8,128)(2,1)}, u32[]{:S(2)}, u32[]{:S(2)}) collective-permute-start(bf16[256,3584]{1,0:T(8,128)(2,1)} %constant_dynamic-update-slice_fusion.own), channel_id=1, source_target_pairs={{0,16},{8,24},{16,0},{24,8},{1,17},{9,25},{17,1},{25,9},{2,18},{10... | collective-permute-start | bytes 5505032 | tf_op jit(solution)/shard_map/ppermute | solution.py:324
  15.4 47.5 %collective-permute-start = (bf16[1040,512]{1,0:T(8,128)(2,1)S(1)}, bf16[1040,512]{1,0:T(8,128)(2,1)S(1)}, u32[]{:S(2)}, u32[]{:S(2)}) collective-permute-start(bf16[1040,512]{1,0:T(8,128)(2,1)S(1)} %concatenate.52.refs_0_.refs_4_.second_piece), channel_id=1, source_target_pairs={{0,1},{1,0},{2,3},{3,2},{4,5},{5,4},{6,7},{7,6},{8,9},{9,8},{10,11... | collective-permute-start | bytes 3194888 | tf_op jit(solution)/shard_map/ppermute | solution.py:324
  17.1 48.3 %collective-permute-start.1 = (bf16[1040,512]{1,0:T(8,128)(2,1)S(1)}, bf16[1040,512]{1,0:T(8,128)(2,1)S(1)}, u32[]{:S(2)}, u32[]{:S(2)}) collective-permute-start(bf16[1040,512]{1,0:T(8,128)(2,1)S(1)} %concatenate.52.refs_0_.refs_4_.second_piece), channel_id=1, source_target_pairs={{0,2},{1,3},{2,0},{3,1},{4,6},{5,7},{6,4},{7,5},{8,10},{9,11},{10,... | collective-permute-start | bytes 3194888 | tf_op jit(solution)/shard_map/ppermute | solution.py:324
  65.4 22.5 %collective-permute-start.7 = (bf16[1040,512]{1,0:T(8,128)(2,1)S(1)}, bf16[1040,512]{1,0:T(8,128)(2,1)}, u32[]{:S(2)}, u32[]{:S(2)}) collective-permute-start(bf16[1040,512]{1,0:T(8,128)(2,1)S(1)} %collective-permute-done.1.refs_2_.refs_6_.first_piece), channel_id=1, source_target_pairs={{0,1},{1,0},{2,3},{3,2},{4,5},{5,4},{6,7},{7,6},{8,9},{9,8},{10,11... | collective-permute-start | bytes 3194888 | tf_op jit(solution)/shard_map/ppermute | solution.py:324
  67.9 20.6 %collective-permute-start.5 = (bf16[128,3584]{1,0:T(8,128)(2,1)}, bf16[128,3584]{1,0:T(8,128)(2,1)}, u32[]{:S(2)}, u32[]{:S(2)}) collective-permute-start(bf16[128,3584]{1,0:T(8,128)(2,1)} %slice.199), channel_id=1, source_target_pairs={{0,8},{8,0},{16,24},{24,16},{1,9},{9,1},{17,25},{25,17},{2,10},{10... | collective-permute-start | bytes 2752520 | tf_op jit(solution)/shard_map/ppermute | solution.py:324
  70.6 20.3 %collective-permute-start.6 = (bf16[128,3584]{1,0:T(8,128)(2,1)}, bf16[128,3584]{1,0:T(8,128)(2,1)}, u32[]{:S(2)}, u32[]{:S(2)}) collective-permute-start(bf16[128,3584]{1,0:T(8,128)(2,1)} %slice.200), channel_id=1, source_target_pairs={{0,16},{8,24},{16,0},{24,8},{1,17},{9,25},{17,1},{25,9},{2,18},{10... | collective-permute-start | bytes 2752520 | tf_op jit(solution)/shard_map/ppermute | solution.py:324
  100.1 47.3 %collective-permute-start.11 = (bf16[1024,512]{1,0:T(8,128)(2,1)}, bf16[1024,512]{1,0:T(8,128)(2,1)}, u32[]{:S(2)}, u32[]{:S(2)}) collective-permute-start(bf16[1024,512]{1,0:T(8,128)(2,1)} %refs_0_.1), channel_id=1, source_target_pairs={{0,2},{1,3},{2,0},{3,1},{4,6},{5,7},{6,4},{7,5},{8,10},{9,11},{10,... | collective-permute-start | bytes 3145736 | tf_op jit(solution)/shard_map/ppermute | solution.py:324
  100.9 46.4 %collective-permute-start.10 = (bf16[1024,512]{1,0:T(8,128)(2,1)}, bf16[1024,512]{1,0:T(8,128)(2,1)}, u32[]{:S(2)}, u32[]{:S(2)}) collective-permute-start(bf16[1024,512]{1,0:T(8,128)(2,1)} %refs_0_.1), channel_id=1, source_target_pairs={{0,1},{1,0},{2,3},{3,2},{4,5},{5,4},{6,7},{7,6},{8,9},{9,8},{10,11... | collective-permute-start | bytes 3145736 | tf_op jit(solution)/shard_map/ppermute | solution.py:324
  102.0 22.5 %collective-permute-start.9 = (bf16[1024,2048]{1,0:T(8,128)(2,1)}, bf16[1024,2048]{1,0:T(8,128)(2,1)}, u32[]{:S(2)}, u32[]{:S(2)}) collective-permute-start(bf16[1024,2048]{1,0:T(8,128)(2,1)} %copy-done.16), channel_id=1, source_target_pairs={{0,4},{4,0},{1,5},{5,1},{2,6},{6,2},{3,7},{7,3},{8,12},{12,8},{9,1... | collective-permute-start | bytes 12582920 | tf_op jit(solution)/shard_map/ppermute | solution.py:324
  102.0 186.8 %reduce-scatter.4.cloned.1.call-start = ((), (), s32[]{:S(2)}) async-start(), calls=%async_computation.4 | async-start | bytes 5242880 | tf_op jit(solution)/shard_map/reduce_scatter | solution.py:1049
  123.9 23.5 %collective-permute-start.12 = (bf16[3,1024,256]{2,1,0:T(8,128)(2,1)S(1)}, bf16[3,1024,256]{2,1,0:T(8,128)(2,1)S(1)}, u32[]{:S(2)}, u32[]{:S(2)}) collective-permute-start(bf16[3,1024,256]{2,1,0:T(8,128)(2,1)S(1)} %get-tuple-element.111), channel_id=1, source_target_pairs={{0,4},{4,0},{1,5},{5,1},{2,6},{6,2},{3,7},{7,3},{8,12},{12,8},{9,1... | collective-permute-start | bytes 4718600 | tf_op jit(solution)/shard_map/ppermute | solution.py:324
  158.2 25.9 %collective-permute-start.14 = (bf16[1024,512]{1,0:T(8,128)(2,1)}, bf16[1024,512]{1,0:T(8,128)(2,1)}, u32[]{:S(2)}, u32[]{:S(2)}) collective-permute-start(bf16[1024,512]{1,0:T(8,128)(2,1)} %collective-permute-done.11.refs_2_), channel_id=1, source_target_pairs={{0,1},{1,0},{2,3},{3,2},{4,5},{5,4},{6,7},{7,6},{8,9},{9,8},{10,11... | collective-permute-start | bytes 3145736 | tf_op jit(solution)/shard_map/ppermute | solution.py:324
  210.4 145.9 %reduce-scatter.6.cloned.1.call-start = ((), (), s32[]{:S(2)}) async-start(), calls=%async_computation.5 | async-start | bytes 5242880 | tf_op jit(solution)/shard_map/reduce_scatter | solution.py:1064
  219.9 35.2 %collective-permute-start.19 = (bf16[1024,2048]{1,0:T(8,128)(2,1)}, bf16[1024,2048]{1,0:T(8,128)(2,1)}, u32[]{:S(2)}, u32[]{:S(2)}) collective-permute-start(bf16[1024,2048]{1,0:T(8,128)(2,1)} %convolution_convert_fusion.1), channel_id=1, source_target_pairs={{0,4},{4,0},{1,5},{5,1},{2,6},{6,2},{3,7},{7,3},{8,12},{12,8},{9,1... | collective-permute-start | bytes 12582920 | tf_op jit(solution)/shard_map/ppermute | solution.py:324
  253.0 63.1 %collective-permute-start.24 = (bf16[2048,256]{1,0:T(8,128)(2,1)}, bf16[2048,256]{1,0:T(8,128)(2,1)}, u32[]{:S(2)}, u32[]{:S(2)}) collective-permute-start(bf16[2048,256]{1,0:T(8,128)(2,1)} %pad_maximum_fusion.3), channel_id=1, source_target_pairs={{0,8},{8,0},{16,24},{24,16},{1,9},{9,1},{17,25},{25,17},{2,10},{10... | collective-permute-start | bytes 3145736 | tf_op jit(solution)/shard_map/ppermute | solution.py:324
  253.7 62.4 %collective-permute-start.25 = (bf16[2048,256]{1,0:T(8,128)(2,1)}, bf16[2048,256]{1,0:T(8,128)(2,1)}, u32[]{:S(2)}, u32[]{:S(2)}) collective-permute-start(bf16[2048,256]{1,0:T(8,128)(2,1)} %pad_maximum_fusion.2), channel_id=1, source_target_pairs={{0,16},{8,24},{16,0},{24,8},{1,17},{9,25},{17,1},{25,9},{2,18},{10... | collective-permute-start | bytes 3145736 | tf_op jit(solution)/shard_map/ppermute | solution.py:324
  263.0 124.5 %reduce-scatter.8.cloned.1.call-start = ((), (), s32[]{:S(2)}) async-start(), calls=%async_computation.6 | async-start | bytes 1310720 | tf_op jit(solution)/shard_map/reduce_scatter | solution.py:1064
  287.7 25.6 %collective-permute-start.22 = (bf16[1024,512]{1,0:T(8,128)(2,1)}, bf16[1024,512]{1,0:T(8,128)(2,1)}, u32[]{:S(2)}, u32[]{:S(2)}) collective-permute-start(bf16[1024,512]{1,0:T(8,128)(2,1)} %get-tuple-element.139), channel_id=1, source_target_pairs={{0,1},{1,0},{2,3},{3,2},{4,5},{5,4},{6,7},{7,6},{8,9},{9,8},{10,11... | collective-permute-start | bytes 3145736 | tf_op jit(solution)/shard_map/ppermute | solution.py:324
  328.8 46.4 %collective-permute-start.28 = (bf16[1024,512]{1,0:T(8,128)(2,1)}, bf16[1024,512]{1,0:T(8,128)(2,1)}, u32[]{:S(2)}, u32[]{:S(2)}) collective-permute-start(bf16[1024,512]{1,0:T(8,128)(2,1)} %get-tuple-element.157), channel_id=1, source_target_pairs={{0,1},{1,0},{2,3},{3,2},{4,5},{5,4},{6,7},{7,6},{8,9},{9,8},{10,11... | collective-permute-start | bytes 3145736 | tf_op jit(solution)/shard_map/ppermute | solution.py:324
  330.4 48.7 %collective-permute-start.29 = (bf16[1024,512]{1,0:T(8,128)(2,1)}, bf16[1024,512]{1,0:T(8,128)(2,1)}, u32[]{:S(2)}, u32[]{:S(2)}) collective-permute-start(bf16[1024,512]{1,0:T(8,128)(2,1)} %add_convert_fusion.4), channel_id=1, source_target_pairs={{0,2},{1,3},{2,0},{3,1},{4,6},{5,7},{6,4},{7,5},{8,10},{9,11},{10,... | collective-permute-start | bytes 3145736 | tf_op jit(solution)/shard_map/ppermute | solution.py:324
  357.6 27.0 %collective-permute-start.35 = (bf16[256,1536]{1,0:T(8,128)(2,1)S(1)}, bf16[256,1536]{1,0:T(8,128)(2,1)S(1)}, u32[]{:S(2)}, u32[]{:S(2)}) collective-permute-start(bf16[256,1536]{1,0:T(8,128)(2,1)S(1)} %pad_maximum_fusion.5), channel_id=1, source_target_pairs={{0,8},{8,0},{16,24},{24,16},{1,9},{9,1},{17,25},{25,17},{2,10},{10... | collective-permute-start | bytes 2359304 | tf_op jit(solution)/shard_map/ppermute | solution.py:324
  359.4 25.2 %collective-permute-start.36 = (bf16[256,1536]{1,0:T(8,128)(2,1)S(1)}, bf16[256,1536]{1,0:T(8,128)(2,1)S(1)}, u32[]{:S(2)}, u32[]{:S(2)}) collective-permute-start(bf16[256,1536]{1,0:T(8,128)(2,1)S(1)} %pad_maximum_fusion.4), channel_id=1, source_target_pairs={{0,16},{8,24},{16,0},{24,8},{1,17},{9,25},{17,1},{25,9},{2,18},{10... | collective-permute-start | bytes 2359304 | tf_op jit(solution)/shard_map/ppermute | solution.py:324
  (79 other events, 933.3 us)
Sparse Core Ops, SparseCore 0:
  102.1 64.6 all-gather.1
  210.5 76.5 reduce-scatter.3
  290.4 53.3 reduce-scatter.5
  356.4 30.9 reduce-scatter.7

commit v5 on v4

--- a/solution.py
+++ b/solution.py
@@ -1144,7 +1144,8 @@
     up_bias_grad = together[width + held_width :]
 
 
-    far_mixed = after(far_mixed, mixed_near, other_columns, *qkv_hop)
+    up_grad = up_grad.astype(wide)
+    far_mixed = after(far_mixed, mixed_near, other_columns, output, up_grad, *qkv_hop)
     shared_mixed = stay_mixed[1] + mixed_near.astype(wide) + far_mixed.astype(wide)
     shared_mixed = join_cores(shared_mixed[:, :tile], shared_mixed[:, tile:], core, 1)
     mean = stats[:, 0:1]
@@ -1163,7 +1164,7 @@
         qkv_bias_grad,
         dense_grad.astype(wide),
         out_bias_grad,
-        up_grad.astype(wide),
+        up_grad,
         up_bias_grad,
         down_grad.astype(wide),
         out_bias_grad,

time: 400 us -> 402 us (level)
    ppermute x37, waiting for transfers between devices: 97 us -> 102 us  [trade(): return lax.ppermute(x, axis, [(i, i ^ bit) for i in range(peers)])]
    unnamed x130 -> x124, local copies, waits for them, and re-layouts: 13.6 us -> 14 us
  transfers between devices with their start and end apart: 41 -> 41, of which waited for: 17 -> 16; matrix products, arithmetic and copies ran while one was open for 22% -> 21% of each run, Pallas kernels for 28% -> 28%
where the time goes in v5:
time: 402 us; the launch traced here: 398 us
  Pallas kernels  136 us (34%)
  waiting for transfers between devices  108 us (27%)
  matrix products  50.4 us (13%)
  other arithmetic  35.2 us (9%)
  starting transfers between devices  30.6 us (8%)
  local copies, waits for them, and re-layouts  22.8 us (6%)
  between operations  15.1 us (4%)
    pallas_call x10, Pallas kernels, call(): pl.pallas_call(kernel, grid_spec=pltpu.PrefetchScalarGridSpec(num_scalar_...  136 us
    ppermute x37, waiting for transfers between devices, trade(): return lax.ppermute(x, axis, [(i, i ^ bit) for i in range(peers)])  102 us
    dot_general x8, matrix products, contract(): lax.dot_general(a, b, ((dims[:1], dims[1:]), ((), ())), preferred_element...  50.4 us
    ppermute x37, starting transfers between devices, trade(): return lax.ppermute(x, axis, [(i, i ^ bit) for i in range(peers)])  30.2 us
    unnamed x124, local copies, waits for them, and re-layouts  14 us
  transfers between devices with their start and end apart: 41, of which 16 were waited for; matrix products, arithmetic and copies ran while one was open for 21% of the time, Pallas kernels for 28%

profile of v5, /device:TPU:0, one launch (start us, length us, event | category | flops | bytes accessed | tf_op | source)
XLA Modules:
  0.0 398.3 jit_solution(10863095039245939417)
XLA Ops:
  20.8 5.5 %multiply_sine_fusion = (f32[2048,128]{1,0:T(8,128)}, f32[2048,128]{1,0:T(8,128)}) fusion(f32[128]{0:T(128)S(1)} %compare_select_fusion, f32[2048]{0:T(1024)S(1)} %add_convert_fusion.11), kind=kLoop, calls=%fused_computation.34 | loop fusion | flops 262144 | bytes 2105856 | tf_op jit(solution)/shard_map/sin | solution.py:972
  26.3 36.6 %collective-permute-done.refs_1_.refs_5_.second_piece = bf16[1040,512]{1,0:T(8,128)(2,1)S(1)} collective-permute-done((bf16[1040,512]{1,0:T(8,128)(2,1)S(1)}, bf16[1040,512]{1,0:T(8,128)(2,1)S(1)}, u32[]{:S(2)}, u32[]{:S(2)}) %collective-permute-start) | collective-permute-done | bytes 1064992 | tf_op jit(solution)/shard_map/ppermute | solution.py:324
  71.2 16.7 %collective-permute-done.7.refs_3_.refs_7_.first_piece = bf16[1040,512]{1,0:T(8,128)(2,1)} collective-permute-done((bf16[1040,512]{1,0:T(8,128)(2,1)S(1)}, bf16[1040,512]{1,0:T(8,128)(2,1)}, u32[]{:S(2)}, u32[]{:S(2)}) %collective-permute-start.7) | collective-permute-done | bytes 1064992 | tf_op jit(solution)/shard_map/ppermute | solution.py:324
  90.9 6.0 %assemble.1 = (bf16[1024,1536]{1,0:T(8,128)(2,1)}, bf16[1024,2048]{1,0:T(8,128)(2,1)S(1)}) custom-call(s32[4]{0:T(128)S(1)} %pad_add_fusion.scalars, bf16[256,3584]{1,0:T(8,128)(2,1)} %constant_dynamic-update-slice_fusion.own, bf16[256,3584]{1,0:T(8,128)(2,1)} %collective-permute-done.3.near, bf16[256,3584]{1,0:T(8,128)(2,1)} %collective-permute-done.4.far, ...), custom_call_target="tpu_custom_call" | custom-call | flops 3670016000 | bytes 58720256000 | tf_op jit(solution)/shard_map/assemble/pallas_call | solution.py:417
  102.3 7.4 %norm.1 = (bf16[1024,2048]{1,0:T(8,128)(2,1)S(1)}, bf16[1024,2048]{1,0:T(8,128)(2,1)S(1)}, f32[1024,128]{1,0:T(8,128)S(1)}, f32[8,2048]{1,0:T(8,128)S(1)}) custom-call(s32[4]{0:T(128)S(1)} %pad_add_fusion.scalars, bf16[1040,512]{1,0:T(8,128)(2,1)S(1)} %concatenate.52.refs_0_.refs_4_.second_piece, ...), custom_call_target="tpu_custom_call" | custom-call | flops 335544320 | bytes 201326592 | tf_op jit(solution)/shard_map/norm/pallas_call | solution.py:417
  111.2 12.7 %heads.1 = (bf16[3,1024,256]{2,1,0:T(8,128)(2,1)S(1)}, bf16[3,1024,256]{2,1,0:T(8,128)(2,1)S(1)}) custom-call(s32[4]{0:T(128)S(1)} %pad_add_fusion.scalars, bf16[1024,2048]{1,0:T(8,128)(2,1)S(1)} %get-tuple-element.153.rows_in, bf16[1024,1536]{1,0:T(8,128)(2,1)} %get-tuple-element.101.own.qkv_own, bf16[1024,1536]{1,0:T(8,128)(2,1)} %collective-permute-done.8.other.qkv_other, ...), custom_call_target="tpu_custom_call" | custom-call | flops 103079215104 | bytes 218103808 | tf_op jit(solution)/shard_map/heads/pallas_call | solution.py:417
  124.5 16.4 %expand.1 = (bf16[1024,2048]{1,0:T(8,128)(2,1)S(1)}, bf16[1024,2048]{1,0:T(8,128)(2,1)S(1)}) custom-call(s32[4]{0:T(128)S(1)} %pad_add_fusion.scalars, bf16[1024,2048]{1,0:T(8,128)(2,1)S(1)} %get-tuple-element.133.rows_in, bf16[1024,2048]{1,0:T(8,128)(2,1)S(1)} %copy-done.17, bf16[1024,2048]{1,0:T(8,128)(2,1)} %collective-permute-done.9.other.up_other, ...), custom_call_target="tpu_custom_call" | custom-call | flops 137438953472 | bytes 335544320 | tf_op jit(solution)/shard_map/expand/pallas_call | solution.py:417
  140.9 4.6 %collective-permute-done.10.refs_1_ = bf16[1024,512]{1,0:T(8,128)(2,1)} collective-permute-done((bf16[1024,512]{1,0:T(8,128)(2,1)}, bf16[1024,512]{1,0:T(8,128)(2,1)}, u32[]{:S(2)}, u32[]{:S(2)}) %collective-permute-start.10) | collective-permute-done | bytes 1048608 | tf_op jit(solution)/shard_map/ppermute | solution.py:324
  147.8 8.3 %attend.1 = (bf16[3,2048,256]{2,1,0:T(8,128)(2,1)S(1)}, bf16[1024,256]{1,0:T(8,128)(2,1)S(1)}, bf16[1024,256]{1,0:T(8,128)(2,1)S(1)}, f32[8,2048]{1,0:T(8,128)S(1)}) custom-call(s32[4]{0:T(128)S(1)} %pad_add_fusion.scalars, bf16[3,1024,256]{2,1,0:T(8,128)(2,1)S(1)} %get-tuple-element.104.mine, bf16[3,1024,256]{2,1,0:T(8,128)(2,1)S(1)} %collective-permute-done.12.theirs, ...), custom_call_target="tpu_custom_call" | custom-call | flops 38654705664 | bytes 134217728 | tf_op jit(solution)/shard_map/attend/pallas_call | solution.py:417
  160.5 6.3 %all-gather.2.cloned.1.call-done.own.other.refs_5_ = bf16[2560,2048]{1,0:T(8,128)(2,1)} async-done(((bf16[2560,256]{1,0:T(8,128)(2,1)}), bf16[2560,2048]{1,0:T(8,128)(2,1)}) %all-gather.2.cloned.1.call-update) | async-done | bytes 10485776 | tf_op jit(solution)/shard_map/all_gather | solution.py:1031
  166.8 16.8 %project.1 = bf16[1024,2048]{1,0:T(8,128)(2,1)} custom-call(s32[4]{0:T(128)} %copy-done.12, bf16[1024,256]{1,0:T(8,128)(2,1)} %copy-done.10, bf16[1024,256]{1,0:T(8,128)(2,1)} %copy-done.41, bf16[1024,2048]{1,0:T(8,128)(2,1)} %copy-done.28, bf16[2560,2048]{1,0:T(8,128)(2,1)} %all-gather.2.cloned.1.call-done.own.other.refs_5_, ...), custom_call_target="tpu_custom_call" | custom-call | flops 171798691840 | bytes 318767104 | tf_op jit(solution)/shard_map/project/pallas_call | solution.py:417
  186.7 17.9 %hidden_back.1 = (bf16[1024,2048]{1,0:T(8,128)(2,1)S(1)}, bf16[1024,2048]{1,0:T(8,128)(2,1)S(1)}, bf16[1024,256]{1,0:T(8,128)(2,1)S(1)}, bf16[1024,256]{1,0:T(8,128)(2,1)S(1)}, f32[8,2048]{1,0:T(8,128)S(1)}) custom-call(s32[4]{0:T(128)S(1)} %copy-done.13, bf16[1024,512]{1,0:T(8,128)(2,1)S(1)} %copy-done.3, ...), custom_call_target="tpu_custom_call" | custom-call | flops 171798691840 | bytes 436207616 | tf_op jit(solution)/shard_map/hidden_back/pallas_call | solution.py:417
  204.6 6.2 %convolution_convert_fusion.2 = bf16[2048,1024]{1,0:T(8,128)(2,1)} fusion(bf16[1024,2048]{1,0:T(8,128)(2,1)S(1)} %copy-done.29, bf16[1024,2048]{1,0:T(8,128)(2,1)S(1)} %get-tuple-element.121), kind=kOutput, calls=%fused_computation.5 | convolution fusion | flops 4297064448 | bytes 10485760 | tf_op jit(solution)/shard_map/dot_general | solution.py:385
  210.9 9.4 %convolution_convert_fusion.1 = bf16[1024,2048]{1,0:T(8,128)(2,1)} fusion(bf16[1024,2048]{1,0:T(8,128)(2,1)} %copy-done.23, bf16[1024,2048]{1,0:T(8,128)(2,1)} %copy-done.18), kind=kOutput, calls=%fused_computation.4 | convolution fusion | flops 4297064448 | bytes 10485760 | tf_op jit(solution)/shard_map/dot_general | solution.py:385
  223.3 8.1 %add_convert_fusion.1 = bf16[2048,1024]{1,0:T(8,128)(2,1)S(1)} fusion(bf16[2048,1024]{1,0:T(8,128)(2,1)} %collective-permute-done.15, bf16[1024,2048]{1,0:T(8,128)(2,1)} %copy-done.28, bf16[1024,2048]{1,0:T(8,128)(2,1)S(1)} %copy-done.22), kind=kOutput, calls=%fused_computation.1 | convolution fusion | flops 4301258752 | bytes 14680064 | tf_op jit(solution)/shard_map/dot_general | solution.py:385
  233.7 14.2 %attend_back.1 = (bf16[1024,768]{1,0:T(8,128)(2,1)S(1)}, bf16[1024,768]{1,0:T(8,128)(2,1)}, f32[8,768]{1,0:T(8,128)S(1)}) custom-call(s32[4]{0:T(128)S(1)} %copy-done.13, bf16[3,2048,256]{2,1,0:T(8,128)(2,1)S(1)} %copy-done.27, bf16[1024,256]{1,0:T(8,128)(2,1)S(1)} %get-tuple-element.126.own_grads, bf16[1024,256]{1,0:T(8,128)(2,1)S(1)} %collective-permute-done.16.twin_grads, ...), custom_call_target="tpu_custom_call" | custom-call | flops 6039797760 | bytes 8388608 | tf_op jit(solution)/shard_map/attend_back/pallas_call | solution.py:417
  255.5 8.0 %add_convert_fusion = bf16[1024,2048]{1,0:T(8,128)(2,1)} fusion(bf16[1024,2048]{1,0:T(8,128)(2,1)} %collective-permute-done.19, bf16[1024,2048]{1,0:T(8,128)(2,1)S(1)} %copy-done.24, bf16[1024,2048]{1,0:T(8,128)(2,1)S(1)} %copy-done.19), kind=kOutput, calls=%fused_computation | convolution fusion | flops 4301258752 | bytes 14680064 | tf_op jit(solution)/shard_map/dot_general | solution.py:385
  263.6 4.4 %add_convert_fusion.5 = bf16[512,1024]{1,0:T(8,128)(2,1)} fusion(bf16[512,1024]{1,0:T(8,128)(2,1)} %collective-permute-done.21, bf16[1024,512]{1,0:T(8,128)(2,1)} %copy-done.40, bf16[1024,2048]{1,0:T(8,128)(2,1)} %copy-done.21), kind=kOutput, calls=%fused_computation.24 | convolution fusion | flops 1075314688 | bytes 5242880 | tf_op jit(solution)/shard_map/dot_general | solution.py:385
  268.0 18.3 %mix.2 = (bf16[1024,512]{1,0:T(8,128)(2,1)}, bf16[1024,512]{1,0:T(8,128)(2,1)}, f32[32,512]{1,0:T(8,128)}, f32[32,512]{1,0:T(8,128)}, f32[1024,128]{1,0:T(8,128)}, /*index=5*/bf16[1024,1536]{1,0:T(8,128)(2,1)}) custom-call(s32[4]{0:T(128)} %copy-done.12, bf16[1024,768]{1,0:T(8,128)(2,1)} %copy-done.25, bf16[1024,768]{1,0:T(8,128)(2,1)} %collective-permute-done.20.theirs, ...), custom_call_target="tpu_custom_call" | custom-call | flops 7516192768 | bytes 18874368 | tf_op jit(solution)/shard_map/mix/pallas_call | solution.py:417
  288.7 17.9 %mix.3 = (f32[1024,512]{1,0:T(8,128)}, f32[1024,512]{1,0:T(8,128)}, f32[32,512]{1,0:T(8,128)}, f32[32,512]{1,0:T(8,128)}, f32[1024,128]{1,0:T(8,128)}) custom-call(s32[4]{0:T(128)} %copy-done.12, bf16[1024,768]{1,0:T(8,128)(2,1)} %copy-done.25, bf16[1024,768]{1,0:T(8,128)(2,1)} %collective-permute-done.20.theirs, bf16[1024,2048]{1,0:T(8,128)(2,1)} %copy-done.23, ...), custom_call_target="tpu_custom_call" | custom-call | flops 7516192768 | bytes 18874368 | tf_op jit(solution)/shard_map/mix/pallas_call | solution.py:417
  314.8 5.0 %convolution_convert_fusion = bf16[1024,1536]{1,0:T(8,128)(2,1)} fusion(bf16[1024,1536]{1,0:T(8,128)(2,1)S(1)} %copy-done.58, bf16[1024,2048]{1,0:T(8,128)(2,1)S(1)} %copy-done.15), kind=kOutput, calls=%fused_computation.3 | convolution fusion | flops 3222798336 | bytes 8388608 | tf_op jit(solution)/shard_map/dot_general | solution.py:385
  328.8 7.1 %add_convert_fusion.2 = bf16[1024,1536]{1,0:T(8,128)(2,1)S(1)} fusion(bf16[1024,1536]{1,0:T(8,128)(2,1)} %collective-permute-done.27, bf16[1024,1536]{1,0:T(8,128)(2,1)} %get-tuple-element.147, bf16[1024,2048]{1,0:T(8,128)(2,1)} %copy-done.14), kind=kOutput, calls=%fused_computation.2 | convolution fusion | flops 3225944064 | bytes 11534336 | tf_op jit(solution)/shard_map/dot_general | solution.py:385
  343.0 8.0 %collective-permute-done.31 = f32[5376]{0:T(1024)S(1)} collective-permute-done((f32[5376]{0:T(1024)S(1)}, f32[5376]{0:T(1024)S(1)}, u32[]{:S(2)}, u32[]{:S(2)}) %collective-permute-start.31) | collective-permute-done | bytes 21536 | tf_op jit(solution)/shard_map/ppermute | solution.py:324
  357.0 21.1 %collective-permute-done.35 = bf16[256,1536]{1,0:T(8,128)(2,1)} collective-permute-done((bf16[256,1536]{1,0:T(8,128)(2,1)}, bf16[256,1536]{1,0:T(8,128)(2,1)}, u32[]{:S(2)}, u32[]{:S(2)}) %collective-permute-start.35) | collective-permute-done | bytes 786464 | tf_op jit(solution)/shard_map/ppermute | solution.py:324
  (294 shorter events, 100.5 us)
Async XLA Ops:
  7.2 159.5 %all-gather.2.cloned.1.call-start = ((), (), s32[]{:S(2)}) async-start(), calls=%async_computation.3 | async-start | bytes 11796480 | tf_op jit(solution)/shard_map/all_gather | solution.py:1031
  10.5 55.2 %collective-permute-start.3 = (bf16[256,3584]{1,0:T(8,128)(2,1)}, bf16[256,3584]{1,0:T(8,128)(2,1)}, u32[]{:S(2)}, u32[]{:S(2)}) collective-permute-start(bf16[256,3584]{1,0:T(8,128)(2,1)} %constant_dynamic-update-slice_fusion.own), channel_id=1, source_target_pairs={{0,8},{8,0},{16,24},{24,16},{1,9},{9,1},{17,25},{25,17},{2,10},{10... | collective-permute-start | bytes 5505032 | tf_op jit(solution)/shard_map/ppermute | solution.py:324
  13.5 52.2 %collective-permute-start.4 = (bf16[256,3584]{1,0:T(8,128)(2,1)}, bf16[256,3584]{1,0:T(8,128)(2,1)}, u32[]{:S(2)}, u32[]{:S(2)}) collective-permute-start(bf16[256,3584]{1,0:T(8,128)(2,1)} %constant_dynamic-update-slice_fusion.own), channel_id=1, source_target_pairs={{0,16},{8,24},{16,0},{24,8},{1,17},{9,25},{17,1},{25,9},{2,18},{10... | collective-permute-start | bytes 5505032 | tf_op jit(solution)/shard_map/ppermute | solution.py:324
  15.4 47.5 %collective-permute-start = (bf16[1040,512]{1,0:T(8,128)(2,1)S(1)}, bf16[1040,512]{1,0:T(8,128)(2,1)S(1)}, u32[]{:S(2)}, u32[]{:S(2)}) collective-permute-start(bf16[1040,512]{1,0:T(8,128)(2,1)S(1)} %concatenate.52.refs_0_.refs_4_.second_piece), channel_id=1, source_target_pairs={{0,1},{1,0},{2,3},{3,2},{4,5},{5,4},{6,7},{7,6},{8,9},{9,8},{10,11... | collective-permute-start | bytes 3194888 | tf_op jit(solution)/shard_map/ppermute | solution.py:324
  17.1 48.3 %collective-permute-start.1 = (bf16[1040,512]{1,0:T(8,128)(2,1)S(1)}, bf16[1040,512]{1,0:T(8,128)(2,1)S(1)}, u32[]{:S(2)}, u32[]{:S(2)}) collective-permute-start(bf16[1040,512]{1,0:T(8,128)(2,1)S(1)} %concatenate.52.refs_0_.refs_4_.second_piece), channel_id=1, source_target_pairs={{0,2},{1,3},{2,0},{3,1},{4,6},{5,7},{6,4},{7,5},{8,10},{9,11},{10,... | collective-permute-start | bytes 3194888 | tf_op jit(solution)/shard_map/ppermute | solution.py:324
  65.4 22.5 %collective-permute-start.7 = (bf16[1040,512]{1,0:T(8,128)(2,1)S(1)}, bf16[1040,512]{1,0:T(8,128)(2,1)}, u32[]{:S(2)}, u32[]{:S(2)}) collective-permute-start(bf16[1040,512]{1,0:T(8,128)(2,1)S(1)} %collective-permute-done.1.refs_2_.refs_6_.first_piece), channel_id=1, source_target_pairs={{0,1},{1,0},{2,3},{3,2},{4,5},{5,4},{6,7},{7,6},{8,9},{9,8},{10,11... | collective-permute-start | bytes 3194888 | tf_op jit(solution)/shard_map/ppermute | solution.py:324
  67.9 20.6 %collective-permute-start.5 = (bf16[128,3584]{1,0:T(8,128)(2,1)}, bf16[128,3584]{1,0:T(8,128)(2,1)}, u32[]{:S(2)}, u32[]{:S(2)}) collective-permute-start(bf16[128,3584]{1,0:T(8,128)(2,1)} %slice.199), channel_id=1, source_target_pairs={{0,8},{8,0},{16,24},{24,16},{1,9},{9,1},{17,25},{25,17},{2,10},{10... | collective-permute-start | bytes 2752520 | tf_op jit(solution)/shard_map/ppermute | solution.py:324
  70.6 20.3 %collective-permute-start.6 = (bf16[128,3584]{1,0:T(8,128)(2,1)}, bf16[128,3584]{1,0:T(8,128)(2,1)}, u32[]{:S(2)}, u32[]{:S(2)}) collective-permute-start(bf16[128,3584]{1,0:T(8,128)(2,1)} %slice.200), channel_id=1, source_target_pairs={{0,16},{8,24},{16,0},{24,8},{1,17},{9,25},{17,1},{25,9},{2,18},{10... | collective-permute-start | bytes 2752520 | tf_op jit(solution)/shard_map/ppermute | solution.py:324
  100.0 45.5 %collective-permute-start.10 = (bf16[1024,512]{1,0:T(8,128)(2,1)}, bf16[1024,512]{1,0:T(8,128)(2,1)}, u32[]{:S(2)}, u32[]{:S(2)}) collective-permute-start(bf16[1024,512]{1,0:T(8,128)(2,1)} %refs_0_.1), channel_id=1, source_target_pairs={{0,1},{1,0},{2,3},{3,2},{4,5},{5,4},{6,7},{7,6},{8,9},{9,8},{10,11... | collective-permute-start | bytes 3145736 | tf_op jit(solution)/shard_map/ppermute | solution.py:324
  100.7 47.1 %collective-permute-start.11 = (bf16[1024,512]{1,0:T(8,128)(2,1)}, bf16[1024,512]{1,0:T(8,128)(2,1)}, u32[]{:S(2)}, u32[]{:S(2)}) collective-permute-start(bf16[1024,512]{1,0:T(8,128)(2,1)} %refs_0_.1), channel_id=1, source_target_pairs={{0,2},{1,3},{2,0},{3,1},{4,6},{5,7},{6,4},{7,5},{8,10},{9,11},{10,... | collective-permute-start | bytes 3145736 | tf_op jit(solution)/shard_map/ppermute | solution.py:324
  101.9 22.5 %collective-permute-start.9 = (bf16[1024,2048]{1,0:T(8,128)(2,1)}, bf16[1024,2048]{1,0:T(8,128)(2,1)}, u32[]{:S(2)}, u32[]{:S(2)}) collective-permute-start(bf16[1024,2048]{1,0:T(8,128)(2,1)} %copy-done.16), channel_id=1, source_target_pairs={{0,4},{4,0},{1,5},{5,1},{2,6},{6,2},{3,7},{7,3},{8,12},{12,8},{9,1... | collective-permute-start | bytes 12582920 | tf_op jit(solution)/shard_map/ppermute | solution.py:324
  101.9 186.7 %reduce-scatter.4.cloned.1.call-start = ((), (), s32[]{:S(2)}) async-start(), calls=%async_computation.4 | async-start | bytes 5242880 | tf_op jit(solution)/shard_map/reduce_scatter | solution.py:1049
  123.9 23.9 %collective-permute-start.12 = (bf16[3,1024,256]{2,1,0:T(8,128)(2,1)S(1)}, bf16[3,1024,256]{2,1,0:T(8,128)(2,1)S(1)}, u32[]{:S(2)}, u32[]{:S(2)}) collective-permute-start(bf16[3,1024,256]{2,1,0:T(8,128)(2,1)S(1)} %get-tuple-element.111), channel_id=1, source_target_pairs={{0,4},{4,0},{1,5},{5,1},{2,6},{6,2},{3,7},{7,3},{8,12},{12,8},{9,1... | collective-permute-start | bytes 4718600 | tf_op jit(solution)/shard_map/ppermute | solution.py:324
  158.6 25.9 %collective-permute-start.14 = (bf16[1024,512]{1,0:T(8,128)(2,1)}, bf16[1024,512]{1,0:T(8,128)(2,1)}, u32[]{:S(2)}, u32[]{:S(2)}) collective-permute-start(bf16[1024,512]{1,0:T(8,128)(2,1)} %collective-permute-done.11.refs_2_), channel_id=1, source_target_pairs={{0,1},{1,0},{2,3},{3,2},{4,5},{5,4},{6,7},{7,6},{8,9},{9,8},{10,11... | collective-permute-start | bytes 3145736 | tf_op jit(solution)/shard_map/ppermute | solution.py:324
  210.8 144.9 %reduce-scatter.6.cloned.1.call-start = ((), (), s32[]{:S(2)}) async-start(), calls=%async_computation.5 | async-start | bytes 5242880 | tf_op jit(solution)/shard_map/reduce_scatter | solution.py:1064
  220.3 35.2 %collective-permute-start.19 = (bf16[1024,2048]{1,0:T(8,128)(2,1)}, bf16[1024,2048]{1,0:T(8,128)(2,1)}, u32[]{:S(2)}, u32[]{:S(2)}) collective-permute-start(bf16[1024,2048]{1,0:T(8,128)(2,1)} %convolution_convert_fusion.1), channel_id=1, source_target_pairs={{0,4},{4,0},{1,5},{5,1},{2,6},{6,2},{3,7},{7,3},{8,12},{12,8},{9,1... | collective-permute-start | bytes 12582920 | tf_op jit(solution)/shard_map/ppermute | solution.py:324
  253.4 61.3 %collective-permute-start.24 = (bf16[2048,256]{1,0:T(8,128)(2,1)}, bf16[2048,256]{1,0:T(8,128)(2,1)}, u32[]{:S(2)}, u32[]{:S(2)}) collective-permute-start(bf16[2048,256]{1,0:T(8,128)(2,1)} %pad_maximum_fusion.3), channel_id=1, source_target_pairs={{0,8},{8,0},{16,24},{24,16},{1,9},{9,1},{17,25},{25,17},{2,10},{10... | collective-permute-start | bytes 3145736 | tf_op jit(solution)/shard_map/ppermute | solution.py:324
  254.1 60.6 %collective-permute-start.25 = (bf16[2048,256]{1,0:T(8,128)(2,1)}, bf16[2048,256]{1,0:T(8,128)(2,1)}, u32[]{:S(2)}, u32[]{:S(2)}) collective-permute-start(bf16[2048,256]{1,0:T(8,128)(2,1)} %pad_maximum_fusion.2), channel_id=1, source_target_pairs={{0,16},{8,24},{16,0},{24,8},{1,17},{9,25},{17,1},{25,9},{2,18},{10... | collective-permute-start | bytes 3145736 | tf_op jit(solution)/shard_map/ppermute | solution.py:324
  263.5 125.7 %reduce-scatter.8.cloned.1.call-start = ((), (), s32[]{:S(2)}) async-start(), calls=%async_computation.6 | async-start | bytes 1310720 | tf_op jit(solution)/shard_map/reduce_scatter | solution.py:1064
  286.3 25.6 %collective-permute-start.22 = (bf16[1024,512]{1,0:T(8,128)(2,1)}, bf16[1024,512]{1,0:T(8,128)(2,1)}, u32[]{:S(2)}, u32[]{:S(2)}) collective-permute-start(bf16[1024,512]{1,0:T(8,128)(2,1)} %get-tuple-element.139), channel_id=1, source_target_pairs={{0,1},{1,0},{2,3},{3,2},{4,5},{5,4},{6,7},{7,6},{8,9},{9,8},{10,11... | collective-permute-start | bytes 3145736 | tf_op jit(solution)/shard_map/ppermute | solution.py:324
  325.5 59.0 %collective-permute-start.29 = (bf16[1024,512]{1,0:T(8,128)(2,1)}, bf16[1024,512]{1,0:T(8,128)(2,1)}, u32[]{:S(2)}, u32[]{:S(2)}) collective-permute-start(bf16[1024,512]{1,0:T(8,128)(2,1)} %add_convert_fusion.4), channel_id=1, source_target_pairs={{0,2},{1,3},{2,0},{3,1},{4,6},{5,7},{6,4},{7,5},{8,10},{9,11},{10,... | collective-permute-start | bytes 3145736 | tf_op jit(solution)/shard_map/ppermute | solution.py:324
  327.1 57.4 %collective-permute-start.28 = (bf16[1024,512]{1,0:T(8,128)(2,1)}, bf16[1024,512]{1,0:T(8,128)(2,1)}, u32[]{:S(2)}, u32[]{:S(2)}) collective-permute-start(bf16[1024,512]{1,0:T(8,128)(2,1)} %get-tuple-element.157), channel_id=1, source_target_pairs={{0,1},{1,0},{2,3},{3,2},{4,5},{5,4},{6,7},{7,6},{8,9},{9,8},{10,11... | collective-permute-start | bytes 3145736 | tf_op jit(solution)/shard_map/ppermute | solution.py:324
  352.2 25.9 %collective-permute-start.35 = (bf16[256,1536]{1,0:T(8,128)(2,1)}, bf16[256,1536]{1,0:T(8,128)(2,1)}, u32[]{:S(2)}, u32[]{:S(2)}) collective-permute-start(bf16[256,1536]{1,0:T(8,128)(2,1)} %pad_maximum_fusion.5), channel_id=1, source_target_pairs={{0,8},{8,0},{16,24},{24,16},{1,9},{9,1},{17,25},{25,17},{2,10},{10... | collective-permute-start | bytes 2359304 | tf_op jit(solution)/shard_map/ppermute | solution.py:324
  354.6 25.6 %collective-permute-start.36 = (bf16[256,1536]{1,0:T(8,128)(2,1)}, bf16[256,1536]{1,0:T(8,128)(2,1)}, u32[]{:S(2)}, u32[]{:S(2)}) collective-permute-start(bf16[256,1536]{1,0:T(8,128)(2,1)} %pad_maximum_fusion.4), channel_id=1, source_target_pairs={{0,16},{8,24},{16,0},{24,8},{1,17},{9,25},{17,1},{25,9},{2,18},{10... | collective-permute-start | bytes 2359304 | tf_op jit(solution)/shard_map/ppermute | solution.py:324
  (76 other events, 970.5 us)
Sparse Core Ops, SparseCore 0:
  102.1 64.6 all-gather.1
  210.9 76.1 reduce-scatter.3
  290.4 55.3 reduce-scatter.5
  355.9 32.2 reduce-scatter.7
